TPU v7x, 32 devices: a whole 2x2x4 slice. The times are simulated.
32 devices in a mesh: region: 8 (over y, x, core), patch: 4 (over z).
Axes of the slice: x: 2, y: 2, z: 4, core: 2. Of those that a mesh axis runs over, the one named last changes fastest.
Arguments:
- nodes: bfloat16 [8192, 512], P(('region', 'patch')), may hold values from -6 to 6
- edges: bfloat16 [65536, 512], P(('region', 'patch')), may hold values from -6 to 6
- senders: int32 [65536], P(('region', 'patch')), may hold values from 0 to 799, as said below
- receivers: int32 [65536], P(('region', 'patch')), may hold values from 0 to 767, as said below
- valid_counts: int32 [32], P(('region', 'patch')), may hold values from 512 to 2048, as said below
- hub_owner: int32 [2, 8], P(None, 'region'), may hold values from 0 to 3
- edge_in: bfloat16 [2, 3, 512, 512], replicated, may hold values from -0.15625 to 0.15625
- edge_bias: float32 [2, 512], replicated, may hold values from -3 to 3
- edge_out: bfloat16 [2, 512, 512], replicated, may hold values from -0.25 to 0.25
- edge_gain: float32 [2, 512], replicated, may hold values from 0.25 to 1.75
- edge_shift: float32 [2, 512], replicated, may hold values from -2 to 2
- node_in: bfloat16 [2, 2, 512, 512], replicated, may hold values from -0.1875 to 0.1875
- node_bias: float32 [2, 512], replicated, may hold values from -3 to 3
- node_out: bfloat16 [2, 512, 512], replicated, may hold values from -0.25 to 0.25
- node_gain: float32 [2, 512], replicated, may hold values from 0.25 to 1.75
- node_shift: float32 [2, 512], replicated, may hold values from -2 to 2
Outputs:
- nodes_out: bfloat16 [8192, 512], P(('region', 'patch'))
- edges_out: bfloat16 [65536, 512], P(('region', 'patch'))
Inputs may be any that keep to these rules, and one draw needn't show every extreme that they name: `senders`: codes below 256 name a row of the previous patch, below 512 of the own patch, below 768 of the next patch, the rest a hub row. `receivers`: codes below 256 name a row of the previous patch, below 512 of the own patch, the rest of the next patch. `valid_counts`: live slots are the first ones of a patch; some patch has all 2048 slots live.
All inputs are finite; a program needn't handle non-finite values.
Results may differ from a plain program's by a relative error of at most 0.012.
Values may be sent and summed in bfloat16 or wider, within the bound.
No kernel may reach another device: no remote copies, remote signals or barrier semaphores. Data moves between devices by JAX's collectives and lax.ppermute only.
A program may use at most 64 MiB of HBM per device.

v0:
```python
import jax
import jax.numpy as jnp
from jax import lax
from jax.sharding import PartitionSpec as P

HUB = 32
LAYERS = 2


epsilon = 1e-05


def extended(cells, sides, width):
    for axis, dim in sides:
        count = lax.axis_size(axis)
        head = lax.slice_in_dim(cells, 0, width, axis=dim)
        tail = lax.slice_in_dim(cells, cells.shape[dim] - width, cells.shape[dim], axis=dim)
        cells = jnp.concatenate(
            [
                lax.ppermute(tail, axis, [(i, (i + 1) % count) for i in range(count)]),
                cells,
                lax.ppermute(head, axis, [((i + 1) % count, i) for i in range(count)]),
            ],
            axis=dim,
        )
    return cells


def spread_2(value, axis, source):
    kept = jnp.where(lax.axis_index(axis) == source, value, 0).astype(value.dtype)
    return lax.psum(kept, axis)


def from_behind(block, axis, distance):
    devices = range(lax.axis_size(axis))
    route = [((i - distance) % len(devices), i) for i in devices]
    return lax.ppermute(block, axis, route)


def activate(value):
    return value / (1.0 + jnp.exp(-value))


def layer_norm(value, gain, shift):
    center = value - jnp.mean(value, axis=-1, keepdims=True)
    spread = jnp.mean(center * center, axis=-1, keepdims=True)
    return center * lax.rsqrt(spread + epsilon) * gain + shift


def update_edges(
    edge_block,
    send_codes,
    recv_codes,
    send_table,
    recv_table,
    first_weight,
    first_bias,
    second_weight,
    gain,
    shift,
):
    pre_edge = jnp.dot(edge_block, first_weight, preferred_element_type=jnp.float32)
    pre_edge = pre_edge + jnp.take(send_table, send_codes, axis=0).astype(jnp.float32)
    pre_edge = pre_edge + jnp.take(recv_table, recv_codes, axis=0).astype(jnp.float32)
    pre_edge = pre_edge + first_bias
    activated = activate(pre_edge).astype(jnp.bfloat16)
    mixed = jnp.dot(activated, second_weight, preferred_element_type=jnp.float32)
    return edge_block.astype(jnp.float32) + layer_norm(mixed, gain, shift)


def local(
    nodes,
    edges,
    senders,
    receivers,
    valid_counts,
    hub_owner,
    edge_in,
    edge_bias,
    edge_out,
    edge_gain,
    edge_shift,
    node_in,
    node_bias,
    node_out,
    node_gain,
    node_shift,
):
    node_rows = nodes.shape[0]
    features = nodes.shape[1]
    edge_rows = edges.shape[0]
    valid_rows = valid_counts[0]
    positions = lax.broadcasted_iota(jnp.int32, (edge_rows,), 0)
    is_valid = positions < valid_rows
    for layer_index in range(LAYERS):
        holder = hub_owner[layer_index, 0]
        both_weights = jnp.concatenate([edge_in[layer_index, 1], edge_in[layer_index, 2]], axis=1)
        near_nodes = extended(nodes, (("patch", 0),), node_rows)
        proj_table = jnp.dot(near_nodes, both_weights, preferred_element_type=jnp.float32).astype(
            jnp.bfloat16
        )
        hub_nodes = spread_2(nodes[:HUB], "patch", holder)
        hub_send = jnp.dot(
            hub_nodes, edge_in[layer_index, 1], preferred_element_type=jnp.float32
        ).astype(jnp.bfloat16)
        send_table = jnp.concatenate([proj_table[:, :features], hub_send], axis=0)
        recv_table = proj_table[:, features:]
        first_weight = edge_in[layer_index, 0]
        first_bias = edge_bias[layer_index]
        second_weight = edge_out[layer_index]
        gain = edge_gain[layer_index]
        shift = edge_shift[layer_index]
        updated = update_edges(
            edges,
            senders,
            receivers,
            send_table,
            recv_table,
            first_weight,
            first_bias,
            second_weight,
            gain,
            shift,
        )
        new_edges = jnp.where(is_valid[:, None], updated, 0.0).astype(jnp.bfloat16)
        edges = new_edges
        partial_value = jax.ops.segment_sum(
            edges.astype(jnp.float32), receivers, num_segments=3 * node_rows
        )
        from_next = from_behind(partial_value[:node_rows].astype(jnp.bfloat16), "patch", -1).astype(
            jnp.float32
        )
        from_prev = from_behind(
            partial_value[2 * node_rows :].astype(jnp.bfloat16), "patch", 1
        ).astype(jnp.float32)
        aggregate = (from_prev + partial_value[node_rows : 2 * node_rows] + from_next).astype(
            jnp.bfloat16
        )
        pre_node = jnp.dot(nodes, node_in[layer_index, 0], preferred_element_type=jnp.float32)
        pre_node = pre_node + jnp.dot(
            aggregate, node_in[layer_index, 1], preferred_element_type=jnp.float32
        )
        pre_node = pre_node + node_bias[layer_index]
        node_act = activate(pre_node).astype(jnp.bfloat16)
        node_mixed = jnp.dot(node_act, node_out[layer_index], preferred_element_type=jnp.float32)
        nodes = (
            nodes.astype(jnp.float32)
            + layer_norm(node_mixed, node_gain[layer_index], node_shift[layer_index])
        ).astype(jnp.bfloat16)
    return (nodes, edges)


def solution(mesh):
    placed = (
        P(("region", "patch"), None),
        P(("region", "patch"), None),
        P(("region", "patch")),
        P(("region", "patch")),
        P(("region", "patch")),
        P(None, "region"),
        P(),
        P(),
        P(),
        P(),
        P(),
        P(),
        P(),
        P(),
        P(),
        P(),
    )
    return jax.shard_map(
        local,
        mesh=mesh,
        in_specs=placed,
        out_specs=(P(("region", "patch"), None), P(("region", "patch"), None)),
        check_vma=False,
    )
```

profile of v0, /device:TPU:0, one launch (start us, length us, event | category | flops | bytes accessed | tf_op | source)
XLA Modules:
  0.0 188.3 jit_solution(6239812496928486717)
XLA Ops:
  0.6 3.1 %collective-permute-start = (bf16[256,512]{1,0:T(8,128)(2,1)}, bf16[256,512]{1,0:T(8,128)(2,1)}, u32[]{:S(2)}, u32[]{:S(2)}) collective-permute-start(bf16[256,512]{1,0:T(8,128)(2,1)} %param.20), channel_id=1, source_target_pairs={{0,1},{1,2},{2,3},{3,0},{4,5},{5,6},{6,7},{7,4},{8,9},{9,10},{10,1... | collective-permute-start | bytes 786440 | tf_op jit(solution)/shard_map/ppermute | solution.py:20
  8.0 2.9 %slice_bitcast_fusion.1 = (bf16[512,512]{1,0:T(8,128)(2,1)}, bf16[512,512]{1,0:T(8,128)(2,1)S(1)}, bf16[512,512]{1,0:T(8,128)(2,1)S(1)}, bf16[512,512]{1,0:T(8,128)(2,1)}) fusion(bf16[2,3,512,512]{3,2,1,0:T(8,128)(2,1)} %param.26), kind=kLoop, calls=%fused_computation.73 | loop fusion | bytes 4194304 | tf_op jit(solution)/shard_map/squeeze | solution.py:97
  12.9 2.4 %copy.20 = bf16[2048,512]{0,1:T(8,128)(2,1)} copy(bf16[2048,512]{1,0:T(8,128)(2,1)S(1)} %copy-done.5) | data formatting | bytes 4194304 | tf_op args[1]
  15.3 17.6 %psum.14 = bf16[32,512]{1,0:T(8,128)(2,1)S(1)} all-reduce(bf16[32,512]{1,0:T(8,128)(2,1)S(1)} %slice_select_fusion.1), channel_id=1, replica_groups=mesh['region'=8,'patch'=4] {'patch'}, use_global_device_ids=true, to_apply=%region_0.1 | all-reduce | flops 16384 | bytes 65536 | tf_op jit(solution)/shard_map/psum | solution.py:31
  36.4 9.2 %gather_fusion = bf16[2048,512]{1,0:T(8,128)(2,1)} fusion(bf16[800,512]{1,0:T(8,128)(2,1)S(1)} %pad_maximum_fusion, s32[2048]{0:T(1024)S(1)} %fusion.76), kind=kCustom, calls=%fused_computation.clone | custom fusion | bytes 4202496 | tf_op jit(solution)/shard_map/jit(_take)/gather | solution.py:63
  45.6 9.2 %gather_fusion.1 = bf16[2048,512]{1,0:T(8,128)(2,1)} fusion(bf16[768,512]{1,0:T(8,128)(2,1)S(1)} %get-tuple-element.15, s32[2048]{0:T(1024)S(1)} %fusion.77), kind=kCustom, calls=%fused_computation.1.clone | custom fusion | bytes 4202496 | tf_op jit(solution)/shard_map/jit(_take)/gather | solution.py:64
  54.7 6.5 %fusion.97 = (f32[2048]{0:T(1024)S(1)}, f32[2048,512]{0,1:T(8,128)}) fusion(bf16[2,512,512]{2,1,0:T(8,128)(2,1)} %param.28, bf16[2048,512]{1,0:T(8,128)(2,1)} %param.21, bf16[2048,512]{1,0:T(8,128)(2,1)} %gather_fusion.1, bf16[2048,512]{1,0:T(8,128)(2,1)S(1)} %copy-done.4, f32[512]{0:T(512)S(1)} %bitcast.99, pred[2048]{0:T(1024)(128)(4,1)S(1)} %get-tuple-element.42, ...), kind=kOutput, calls=%fused_computation.126 | convolution fusion | flops 2160064512 | bytes 11548672 | tf_op jit(solution)/shard_map/dot_general | solution.py:67
  61.3 2.8 %multiply_reduce_fusion.1 = f32[2048]{0:T(1024)S(1)} fusion(f32[2048,512]{0,1:T(8,128)} %get-tuple-element.35, f32[2048]{0:T(1024)S(1)} %broadcast_multiply_fusion.1), kind=kLoop, calls=%fused_computation.10 | loop fusion | flops 3143680 | bytes 4210688 | tf_op jit(solution)/shard_map/reduce_sum | solution.py:46
  64.7 2.8 %select_convert_fusion.1 = bf16[2048,512]{0,1:T(8,128)(2,1)S(1)} fusion(bf16[2048,512]{0,1:T(8,128)(2,1)} %copy.20, f32[2048,512]{0,1:T(8,128)S(1)} %copy-done.3, f32[512]{0:T(512)S(1)} %bitcast.94, f32[512]{0:T(512)S(1)} %bitcast.93, f32[2048]{0:T(1024)S(1)} %add_rsqrt_fusion.1, f32[2048]{0:T(1024)S(1)} %broadcast_multiply_fusion.1, ...), kind=kLoop, calls=%fused_computation.9 | loop fusion | flops 8388608 | bytes 8411136 | tf_op jit(solution)/shard_map/convert_element_type | solution.py:125
  67.5 3.1 %copy.21 = f32[2048,512]{1,0:T(8,128)} copy(bf16[2048,512]{0,1:T(8,128)(2,1)S(1)} %select_convert_fusion.1) | data formatting | bytes 6291456 | tf_op jit(solution)/shard_map/convert_element_type | solution.py:128
  70.6 14.5 %scatter_custom_fusion = f32[768,512]{1,0:T(8,128)} fusion(s32[2048]{0:T(1024)} %param.23, f32[2048,512]{1,0:T(8,128)} %copy.21, f32[]{:T(128)} %constant.24.clone.1), kind=kCustom, calls=%fused_computation.44 | custom fusion | flops 1048576 | bytes 1573376 | tf_op jit(solution)/shard_map/scatter-add | solution.py:127
  86.8 3.8 %collective-permute-start.3 = (bf16[256,512]{1,0:T(8,128)(2,1)S(1)}, bf16[256,512]{1,0:T(8,128)(2,1)}, u32[]{:S(2)}, u32[]{:S(2)}) collective-permute-start(bf16[256,512]{1,0:T(8,128)(2,1)S(1)} %get-tuple-element.19), channel_id=1, source_target_pairs={{1,0},{2,1},{3,2},{0,3},{5,4},{6,5},{7,6},{4,7},{9,8},{10,9},{11,1... | collective-permute-start | bytes 786440 | tf_op jit(solution)/shard_map/ppermute | solution.py:37
  91.6 3.8 %collective-permute-done.2 = bf16[256,512]{1,0:T(8,128)(2,1)} collective-permute-done((bf16[256,512]{1,0:T(8,128)(2,1)S(1)}, bf16[256,512]{1,0:T(8,128)(2,1)}, u32[]{:S(2)}, u32[]{:S(2)}) %collective-permute-start.2) | collective-permute-done | bytes 262176 | tf_op jit(solution)/shard_map/ppermute | solution.py:37
  99.8 2.9 %collective-permute-start.5 = (bf16[256,512]{1,0:T(8,128)(2,1)S(1)}, bf16[256,512]{1,0:T(8,128)(2,1)S(1)}, u32[]{:S(2)}, u32[]{:S(2)}) collective-permute-start(bf16[256,512]{1,0:T(8,128)(2,1)S(1)} %add_convert_fusion.1), channel_id=1, source_target_pairs={{1,0},{2,1},{3,2},{0,3},{5,4},{6,5},{7,6},{4,7},{9,8},{10,9},{11,1... | collective-permute-start | bytes 786440 | tf_op jit(solution)/shard_map/ppermute | solution.py:22
  102.7 17.4 %psum.15 = bf16[32,512]{1,0:T(8,128)(2,1)S(1)} all-reduce(bf16[32,512]{1,0:T(8,128)(2,1)S(1)} %slice_select_fusion), channel_id=1, replica_groups=mesh['region'=8,'patch'=4] {'patch'}, use_global_device_ids=true, to_apply=%region_6.9 | all-reduce | flops 16384 | bytes 65536 | tf_op jit(solution)/shard_map/psum | solution.py:31
  123.5 9.2 %gather_fusion.2 = bf16[2048,512]{1,0:T(8,128)(2,1)} fusion(bf16[800,512]{1,0:T(8,128)(2,1)S(1)} %pad_maximum_fusion.1, s32[2048]{0:T(1024)S(1)} %fusion.76), kind=kCustom, calls=%fused_computation.2.clone | custom fusion | bytes 4202496 | tf_op jit(solution)/shard_map/jit(_take)/gather | solution.py:63
  132.8 9.2 %gather_fusion.3 = bf16[2048,512]{1,0:T(8,128)(2,1)} fusion(bf16[768,512]{1,0:T(8,128)(2,1)S(1)} %get-tuple-element.13, s32[2048]{0:T(1024)S(1)} %fusion.77), kind=kCustom, calls=%fused_computation.3.clone | custom fusion | bytes 4202496 | tf_op jit(solution)/shard_map/jit(_take)/gather | solution.py:64
  141.9 7.9 %fusion.105 = (f32[2048]{0:T(1024)S(1)}, f32[2048,512]{0,1:T(8,128)}) fusion(bf16[2,512,512]{2,1,0:T(8,128)(2,1)} %param.28, bf16[2048,512]{0,1:T(8,128)(2,1)S(1)} %copy-done.1, bf16[2048,512]{1,0:T(8,128)(2,1)} %gather_fusion.3, bf16[2048,512]{1,0:T(8,128)(2,1)} %gather_fusion.2, f32[512]{0:T(512)S(1)} %bitcast.97, ...), kind=kOutput, calls=%fused_computation.128 | convolution fusion | flops 2160064512 | bytes 11548672 | tf_op jit(solution)/shard_map/dot_general | solution.py:67
  149.9 2.8 %multiply_reduce_fusion = f32[2048]{0:T(1024)S(1)} fusion(f32[2048,512]{0,1:T(8,128)} %get-tuple-element.39, f32[2048]{0:T(1024)S(1)} %broadcast_multiply_fusion), kind=kLoop, calls=%fused_computation.7 | loop fusion | flops 3143680 | bytes 4210688 | tf_op jit(solution)/shard_map/reduce_sum | solution.py:46
  152.7 3.3 %select_convert_fusion = bf16[2048,512]{0,1:T(8,128)(2,1)S(1)} fusion(f32[2048,512]{0,1:T(8,128)} %get-tuple-element.39, f32[512]{0:T(512)S(1)} %bitcast.90, f32[512]{0:T(512)S(1)} %bitcast.89, f32[2048]{0:T(1024)S(1)} %add_rsqrt_fusion, f32[2048]{0:T(1024)S(1)} %broadcast_multiply_fusion, pred[2048]{0:T(1024)(128)(4,1)S(1)} %iota_compare_fusion, ...), kind=kLoop, calls=%fused_computation.6 | loop fusion | flops 8388608 | bytes 8411136 | tf_op jit(solution)/shard_map/convert_element_type | solution.py:125
  156.0 3.0 %copy.22 = f32[2048,512]{1,0:T(8,128)} copy(bf16[2048,512]{0,1:T(8,128)(2,1)S(1)} %select_convert_fusion) | data formatting | bytes 6291456 | tf_op jit(solution)/shard_map/convert_element_type | solution.py:128
  159.0 14.5 %scatter_custom_fusion.1 = f32[768,512]{1,0:T(8,128)} fusion(s32[2048]{0:T(1024)} %param.23, f32[2048,512]{1,0:T(8,128)} %copy.22, f32[]{:T(128)} %constant.24.clone.1), kind=kCustom, calls=%fused_computation.42 | custom fusion | flops 1048576 | bytes 1573376 | tf_op jit(solution)/shard_map/scatter-add | solution.py:127
  175.7 3.8 %collective-permute-start.7 = (bf16[256,512]{1,0:T(8,128)(2,1)S(1)}, bf16[256,512]{1,0:T(8,128)(2,1)}, u32[]{:S(2)}, u32[]{:S(2)}) collective-permute-start(bf16[256,512]{1,0:T(8,128)(2,1)S(1)} %get-tuple-element.17), channel_id=1, source_target_pairs={{1,0},{2,1},{3,2},{0,3},{5,4},{6,5},{7,6},{4,7},{9,8},{10,9},{11,1... | collective-permute-start | bytes 786440 | tf_op jit(solution)/shard_map/ppermute | solution.py:37
  180.9 2.5 %copy.23 = bf16[2048,512]{1,0:T(8,128)(2,1)} copy(bf16[2048,512]{0,1:T(8,128)(2,1)S(1)} %select_convert_fusion) | data formatting | bytes 4194304
  (84 shorter events, 27.3 us)
Async XLA Ops:
  0.6 33.6 %collective-permute-start = (bf16[256,512]{1,0:T(8,128)(2,1)}, bf16[256,512]{1,0:T(8,128)(2,1)}, u32[]{:S(2)}, u32[]{:S(2)}) collective-permute-start(bf16[256,512]{1,0:T(8,128)(2,1)} %param.20), channel_id=1, source_target_pairs={{0,1},{1,2},{2,3},{3,0},{4,5},{5,6},{6,7},{7,4},{8,9},{9,10},{10,1... | collective-permute-start | bytes 786440 | tf_op jit(solution)/shard_map/ppermute | solution.py:20
  3.7 30.5 %collective-permute-start.1 = (bf16[256,512]{1,0:T(8,128)(2,1)}, bf16[256,512]{1,0:T(8,128)(2,1)}, u32[]{:S(2)}, u32[]{:S(2)}) collective-permute-start(bf16[256,512]{1,0:T(8,128)(2,1)} %param.20), channel_id=1, source_target_pairs={{1,0},{2,1},{3,2},{0,3},{5,4},{6,5},{7,6},{4,7},{9,8},{10,9},{11,1... | collective-permute-start | bytes 786440 | tf_op jit(solution)/shard_map/ppermute | solution.py:22
  8.0 2.9 %copy-start.15 = (s32[2,1]{0,1:T(1,128)S(1)}, s32[2,1]{0,1:T(1,128)}, u32[]{:S(2)}) copy-start(s32[2,1]{0,1:T(1,128)} %param.25) | copy-start | bytes 28
  8.0 4.2 %copy-start.6 = (bf16[256,512]{1,0:T(8,128)(2,1)S(1)}, bf16[256,512]{1,0:T(8,128)(2,1)}, u32[]{:S(2)}) copy-start(bf16[256,512]{1,0:T(8,128)(2,1)} %param.20) | copy-start | bytes 786436
  8.0 4.2 %copy-start.9 = (f32[2,512]{1,0:T(2,128)S(1)}, f32[2,512]{1,0:T(2,128)}, u32[]{:S(2)}) copy-start(f32[2,512]{1,0:T(2,128)} %param.27) | copy-start | bytes 12292
  8.0 4.2 %copy-start.10 = (f32[2,512]{1,0:T(2,128)S(1)}, f32[2,512]{1,0:T(2,128)}, u32[]{:S(2)}) copy-start(f32[2,512]{1,0:T(2,128)} %param.29) | copy-start | bytes 12292
  8.0 4.2 %copy-start.11 = (f32[2,512]{1,0:T(2,128)S(1)}, f32[2,512]{1,0:T(2,128)}, u32[]{:S(2)}) copy-start(f32[2,512]{1,0:T(2,128)} %param.30) | copy-start | bytes 12292
  8.0 4.9 %copy-start.5 = (bf16[2048,512]{1,0:T(8,128)(2,1)S(1)}, bf16[2048,512]{1,0:T(8,128)(2,1)}, u32[]{:S(2)}) copy-start(bf16[2048,512]{1,0:T(8,128)(2,1)} %param.21) | copy-start | bytes 6291460
  12.9 2.4 %copy-start.12 = (f32[2,512]{1,0:T(2,128)S(1)}, f32[2,512]{1,0:T(2,128)}, u32[]{:S(2)}) copy-start(f32[2,512]{1,0:T(2,128)} %param.32) | copy-start | bytes 12292
  12.9 2.4 %copy-start.13 = (f32[2,512]{1,0:T(2,128)S(1)}, f32[2,512]{1,0:T(2,128)}, u32[]{:S(2)}) copy-start(f32[2,512]{1,0:T(2,128)} %param.34) | copy-start | bytes 12292
  45.5 9.2 %copy-start.4 = (bf16[2048,512]{1,0:T(8,128)(2,1)S(1)}, bf16[2048,512]{1,0:T(8,128)(2,1)}, u32[]{:S(2)}) copy-start(bf16[2048,512]{1,0:T(8,128)(2,1)} %gather_fusion) | copy-start | bytes 6291460
  61.3 3.4 %copy-start.3 = (f32[2048,512]{0,1:T(8,128)S(1)}, f32[2048,512]{0,1:T(8,128)}, u32[]{:S(2)}) copy-start(f32[2048,512]{0,1:T(8,128)} %get-tuple-element.35) | copy-start | bytes 12582916
  67.5 3.1 %copy-start = (bf16[2048,512]{0,1:T(8,128)(2,1)}, bf16[2048,512]{0,1:T(8,128)(2,1)S(1)}, u32[]{:S(2)}) copy-start(bf16[2048,512]{0,1:T(8,128)(2,1)S(1)} %select_convert_fusion.1) | copy-start | bytes 6291460
  85.1 5.6 %copy-start.14 = (f32[2,512]{1,0:T(2,128)S(1)}, f32[2,512]{1,0:T(2,128)}, u32[]{:S(2)}) copy-start(f32[2,512]{1,0:T(2,128)} %param.35) | copy-start | bytes 12292
  85.1 6.2 %copy-start.7 = (bf16[2,2,512,512]{3,2,1,0:T(8,128)(2,1)S(1)}, bf16[2,2,512,512]{3,2,1,0:T(8,128)(2,1)}, u32[]{:S(2)}) copy-start(bf16[2,2,512,512]{3,2,1,0:T(8,128)(2,1)} %param.31) | copy-start | bytes 6291460
  86.8 8.6 %collective-permute-start.2 = (bf16[256,512]{1,0:T(8,128)(2,1)S(1)}, bf16[256,512]{1,0:T(8,128)(2,1)}, u32[]{:S(2)}, u32[]{:S(2)}) collective-permute-start(bf16[256,512]{1,0:T(8,128)(2,1)S(1)} %get-tuple-element.18), channel_id=1, source_target_pairs={{3,0},{0,1},{1,2},{2,3},{7,4},{4,5},{5,6},{6,7},{11,8},{8,9},{9,10... | collective-permute-start | bytes 786440 | tf_op jit(solution)/shard_map/ppermute | solution.py:37
  86.8 9.5 %collective-permute-start.3 = (bf16[256,512]{1,0:T(8,128)(2,1)S(1)}, bf16[256,512]{1,0:T(8,128)(2,1)}, u32[]{:S(2)}, u32[]{:S(2)}) collective-permute-start(bf16[256,512]{1,0:T(8,128)(2,1)S(1)} %get-tuple-element.19), channel_id=1, source_target_pairs={{1,0},{2,1},{3,2},{0,3},{5,4},{6,5},{7,6},{4,7},{9,8},{10,9},{11,1... | collective-permute-start | bytes 786440 | tf_op jit(solution)/shard_map/ppermute | solution.py:37
  98.4 23.0 %copy-start.8 = (bf16[512,512]{1,0:T(8,128)(2,1)S(1)}, bf16[512,512]{1,0:T(8,128)(2,1)}, u32[]{:S(2)}) copy-start(bf16[512,512]{1,0:T(8,128)(2,1)} %get-tuple-element.8) | copy-start | bytes 1572868
  98.8 22.5 %collective-permute-start.4 = (bf16[256,512]{1,0:T(8,128)(2,1)S(1)}, bf16[256,512]{1,0:T(8,128)(2,1)S(1)}, u32[]{:S(2)}, u32[]{:S(2)}) collective-permute-start(bf16[256,512]{1,0:T(8,128)(2,1)S(1)} %add_convert_fusion.1), channel_id=1, source_target_pairs={{0,1},{1,2},{2,3},{3,0},{4,5},{5,6},{6,7},{7,4},{8,9},{9,10},{10,1... | collective-permute-start | bytes 786440 | tf_op jit(solution)/shard_map/ppermute | solution.py:20
  99.8 21.5 %collective-permute-start.5 = (bf16[256,512]{1,0:T(8,128)(2,1)S(1)}, bf16[256,512]{1,0:T(8,128)(2,1)S(1)}, u32[]{:S(2)}, u32[]{:S(2)}) collective-permute-start(bf16[256,512]{1,0:T(8,128)(2,1)S(1)} %add_convert_fusion.1), channel_id=1, source_target_pairs={{1,0},{2,1},{3,2},{0,3},{5,4},{6,5},{7,6},{4,7},{9,8},{10,9},{11,1... | collective-permute-start | bytes 786440 | tf_op jit(solution)/shard_map/ppermute | solution.py:22
  132.8 9.2 %copy-start.1 = (bf16[2048,512]{0,1:T(8,128)(2,1)S(1)}, bf16[2048,512]{0,1:T(8,128)(2,1)}, u32[]{:S(2)}) copy-start(bf16[2048,512]{0,1:T(8,128)(2,1)} %copy-done) | copy-start | bytes 6291460
  149.9 2.9 %copy-start.2 = (bf16[2048,512]{0,1:T(8,128)(2,1)S(1)}, bf16[2048,512]{0,1:T(8,128)(2,1)}, u32[]{:S(2)}) copy-start(bf16[2048,512]{0,1:T(8,128)(2,1)} %copy-done) | copy-start | bytes 6291460
  175.7 8.5 %collective-permute-start.6 = (bf16[256,512]{1,0:T(8,128)(2,1)}, bf16[256,512]{1,0:T(8,128)(2,1)S(1)}, u32[]{:S(2)}, u32[]{:S(2)}) collective-permute-start(bf16[256,512]{1,0:T(8,128)(2,1)} %get-tuple-element.16), channel_id=1, source_target_pairs={{3,0},{0,1},{1,2},{2,3},{7,4},{4,5},{5,6},{6,7},{11,8},{8,9},{9,10... | collective-permute-start | bytes 786440 | tf_op jit(solution)/shard_map/ppermute | solution.py:37
  175.7 9.3 %collective-permute-start.7 = (bf16[256,512]{1,0:T(8,128)(2,1)S(1)}, bf16[256,512]{1,0:T(8,128)(2,1)}, u32[]{:S(2)}, u32[]{:S(2)}) collective-permute-start(bf16[256,512]{1,0:T(8,128)(2,1)S(1)} %get-tuple-element.17), channel_id=1, source_target_pairs={{1,0},{2,1},{3,2},{0,3},{5,4},{6,5},{7,6},{4,7},{9,8},{10,9},{11,1... | collective-permute-start | bytes 786440 | tf_op jit(solution)/shard_map/ppermute | solution.py:37
where the time goes:
time: 189 us; the launch traced here: 188 us
  local copies, waits for them, and re-layouts  52.9 us (28%)
  other arithmetic  47.6 us (25%)
  blocking collectives  35 us (19%)
  matrix products  26.7 us (14%)
  starting transfers between devices  16.8 us (9%)
  waiting for transfers between devices  6.37 us (3%)
  between operations  2.99 us (2%)
    psum x2, blocking collectives, spread_2(): return lax.psum(kept, axis)  35 us
    scatter-add x2, other arithmetic, local(): jax.ops.segment_sum(edges.astype(jnp.float32), receivers, num_segments=3...  28.9 us
    gather x2, local copies, waits for them, and re-layouts, update_edges(): jnp.take(send_table, send_codes, axis=0).astype(jnp.float32)  18.4 us
    gather x2, local copies, waits for them, and re-layouts, update_edges(): jnp.take(recv_table, recv_codes, axis=0).astype(jnp.float32)  18.3 us
    dot_general x2, matrix products, update_edges(): jnp.dot(activated, second_weight, preferred_element_type=jnp.float32)  14.5 us
    ppermute x4, starting transfers between devices, from_behind(): return lax.ppermute(block, axis, route)  7.69 us
    ppermute x4, waiting for transfers between devices, from_behind(): return lax.ppermute(block, axis, route)  6.34 us
    convert_element_type x2, other arithmetic, local(): new_edges = jnp.where(is_valid[:, None], updated, 0.0).astype(jnp.bfloat16)  6.11 us
  transfers between devices with their start and end apart: 8, of which 4 were waited for; matrix products, arithmetic and copies ran while one was open for 8% of the time, Pallas kernels for 0%

commit v1 on v0

v1 whole, which is shorter than its diff:
```python
import functools

import jax
import jax.numpy as jnp
from jax import lax
from jax.experimental import pallas as pl
from jax.experimental.pallas import tpu as pltpu
from jax.sharding import PartitionSpec as P

HUB = 32
LAYERS = 2
LANES = 128

epsilon = 1e-05

F32 = jnp.float32
BF16 = jnp.bfloat16


def from_behind(block, axis, distance):
    size = lax.axis_size(axis)
    return lax.ppermute(block, axis, [((i - distance) % size, i) for i in range(size)])


def dot(left, right):
    return jnp.dot(left, right, preferred_element_type=F32)


def silu(value):
    half = value * 0.5
    return half + half * jnp.tanh(half)


def layer_norm(value, gain, shift):
    center = value - jnp.mean(value, axis=-1, keepdims=True)
    spread = jnp.mean(center * center, axis=-1, keepdims=True)
    return center * lax.rsqrt(spread + epsilon) * gain + shift


def columns_of(codes_ref, first, count):
    rows = [
        jnp.broadcast_to(codes_ref[pl.ds(first + i, 1), :], (LANES, LANES)).T
        for i in range(count)
    ]
    return jnp.concatenate(rows, axis=0)


def one_hot(codes, start, width):
    lane = lax.broadcasted_iota(jnp.int32, codes.shape, 1)
    offset = codes - lane
    parts = [
        jnp.where(offset == start + t * LANES, 1.0, 0.0).astype(BF16)
        for t in range(width // LANES)
    ]
    return jnp.concatenate(parts, axis=1)


def one_hot_rows(codes_ref, first, count, width):
    parts = []
    for i in range(count):
        row = codes_ref[pl.ds(first + i, 1), :]
        sub = lax.broadcasted_iota(jnp.int32, (width, LANES), 0)
        parts.append(jnp.where(sub == row, 1.0, 0.0).astype(BF16))
    return jnp.concatenate(parts, axis=1)


def linear_kernel(layer, edges_ref, weight_ref, bias_ref, out_ref):
    out_ref[...] = dot(edges_ref[...], weight_ref[0, 0]) + bias_ref[layer : layer + 1, :]


def own_kernel(rows, fused, layer, *refs):
    if fused:
        (send_ref, recv_ref, edges_ref, first_ref, bias_ref, nodes_ref, ws_ref, wr_ref) = refs[:8]
    else:
        (send_ref, recv_ref, pre_ref, nodes_ref, ws_ref, wr_ref) = refs[:6]
    out_ref, table_ref = refs[-2:]
    step = pl.program_id(0)

    @pl.when(step == 0)
    def _():
        own = nodes_ref[...]
        table_ref[:rows, :] = dot(own, ws_ref[0, 0]).astype(BF16)
        table_ref[rows:, :] = dot(own, wr_ref[0, 0]).astype(BF16)

    count = out_ref.shape[0] // LANES
    picks = jnp.concatenate(
        [
            one_hot(columns_of(send_ref, step * count, count), rows, rows),
            one_hot(columns_of(recv_ref, step * count, count), rows, rows),
        ],
        axis=1,
    )
    total = dot(picks, table_ref[...])
    if fused:
        total = total + dot(edges_ref[...], first_ref[0, 0]) + bias_ref[layer : layer + 1, :]
    else:
        total = total + pre_ref[...]
    out_ref[...] = total


def edge_kernel(
    rows,
    layer,
    size,
    valid_ref,
    owner_ref,
    send_ref,
    recv_ref,
    edges_ref,
    pre_ref,
    own_ref,
    prev_ref,
    next_ref,
    far_ref,
    ws_ref,
    wr_ref,
    wo_ref,
    gain_ref,
    shift_ref,
    out_ref,
    to_prev_ref,
    kept_ref,
    to_next_ref,
    table_ref,
    total_ref,
):
    step = pl.program_id(0)

    @pl.when(step == 0)
    def _():
        weight_s = ws_ref[0, 0]
        weight_r = wr_ref[0, 0]
        before = prev_ref[...]
        after = next_ref[...]
        table_ref[0 * rows : 1 * rows, :] = dot(before, weight_s).astype(BF16)
        table_ref[1 * rows : 2 * rows, :] = dot(after, weight_s).astype(BF16)
        table_ref[2 * rows : 3 * rows, :] = dot(before, weight_r).astype(BF16)
        table_ref[3 * rows : 4 * rows, :] = dot(after, weight_r).astype(BF16)
        away = owner_ref[layer, 0] - lax.axis_index("patch")
        away = jnp.where(away < 0, away + size, away)
        hub = own_ref[:HUB, :]
        if size > 3:
            spot = jnp.clip(away - 2, 0, size - 4)
            hub = jnp.where(away > 1, far_ref[pl.ds(pl.multiple_of(spot * HUB, HUB), HUB), :], hub)
        hub = jnp.where(away == size - 1, prev_ref[:HUB, :], hub)
        hub = jnp.where(away == 1, next_ref[:HUB, :], hub)
        hub = jnp.where(away == 0, own_ref[:HUB, :], hub)
        table_ref[4 * rows : 4 * rows + HUB, :] = dot(hub, weight_s).astype(BF16)
        table_ref[4 * rows + HUB :, :] = jnp.zeros_like(table_ref[4 * rows + HUB :, :])
        total_ref[...] = jnp.zeros_like(total_ref)

    block = out_ref.shape[0]
    count = block // LANES
    send = columns_of(send_ref, step * count, count)
    recv = columns_of(recv_ref, step * count, count)
    picks = jnp.concatenate(
        [
            one_hot(send, 0, rows),
            one_hot(send, 2 * rows, rows),
            one_hot(recv, 0, rows),
            one_hot(recv, 2 * rows, rows),
            one_hot(send, 3 * rows, LANES),
        ],
        axis=1,
    )
    activated = silu(pre_ref[...] + dot(picks, table_ref[...])).astype(BF16)
    mixed = dot(activated, wo_ref[0])
    normed = layer_norm(mixed, gain_ref[layer : layer + 1, :], shift_ref[layer : layer + 1, :])
    spot = step * block + lax.broadcasted_iota(jnp.int32, (block, 1), 0)
    updated = jnp.where(spot < valid_ref[0], edges_ref[...].astype(F32) + normed, 0.0).astype(BF16)
    out_ref[...] = updated
    total_ref[...] += dot(one_hot_rows(recv_ref, step * count, count, 3 * rows), updated)

    @pl.when(step == pl.num_programs(0) - 1)
    def _():
        to_prev_ref[...] = total_ref[:rows, :].astype(BF16)
        kept_ref[...] = total_ref[rows : 2 * rows, :]
        to_next_ref[...] = total_ref[2 * rows :, :].astype(BF16)


def node_kernel(
    layer,
    nodes_ref,
    kept_ref,
    from_prev_ref,
    from_next_ref,
    wh_ref,
    wa_ref,
    bias_ref,
    wo_ref,
    gain_ref,
    shift_ref,
    out_ref,
):
    nodes = nodes_ref[...]
    summed = from_prev_ref[...].astype(F32) + kept_ref[...] + from_next_ref[...].astype(F32)
    pre_node = dot(nodes, wh_ref[0, 0]) + dot(summed.astype(BF16), wa_ref[0, 0])
    pre_node = pre_node + bias_ref[layer : layer + 1, :]
    mixed = dot(silu(pre_node).astype(BF16), wo_ref[0])
    normed = layer_norm(mixed, gain_ref[layer : layer + 1, :], shift_ref[layer : layer + 1, :])
    out_ref[...] = (nodes.astype(F32) + normed).astype(BF16)


def whole(shape):
    return pl.BlockSpec(shape, lambda *_: (0,) * len(shape))


def picked(shape, spot):
    block = (1,) * len(spot) + shape[len(spot) :]
    index = tuple(spot) + (0,) * (len(shape) - len(spot))
    return pl.BlockSpec(block, lambda *_: index)


def scalars():
    return pl.BlockSpec(memory_space=pltpu.SMEM)


def cost(flops, moved):
    return pl.CostEstimate(flops=flops, bytes_accessed=moved, transcendentals=0)


def local(
    nodes,
    edges,
    senders,
    receivers,
    valid_counts,
    hub_owner,
    edge_in,
    edge_bias,
    edge_out,
    edge_gain,
    edge_shift,
    node_in,
    node_bias,
    node_out,
    node_gain,
    node_shift,
):
    rows, width = nodes.shape
    slots = edges.shape[0]
    size = lax.axis_size("patch")
    block = min(512, slots)
    steps = slots // block
    send = senders.reshape(slots // LANES, LANES)
    recv = receivers.reshape(slots // LANES, LANES)
    by_block = pl.BlockSpec((block, width), lambda i: (i, 0))
    square = 2 * slots * width * width
    pre = None
    for layer in range(LAYERS):
        from_prev = from_behind(nodes, "patch", 1)
        from_next = from_behind(nodes, "patch", -1)
        top = nodes[:HUB]
        far = [from_behind(top, "patch", -d) for d in range(2, size - 1)]
        far = jnp.concatenate(far, axis=0) if len(far) > 1 else (far[0] if far else top)
        w0 = picked(edge_in.shape, (layer, 0))
        ws = picked(edge_in.shape, (layer, 1))
        wr = picked(edge_in.shape, (layer, 2))
        fused = pre is None
        if fused:
            head = (edges, edge_in, edge_bias)
            head_specs = [by_block, w0, whole(edge_bias.shape)]
        else:
            head = (pre,)
            head_specs = [by_block]
        pre = pl.pallas_call(
            functools.partial(own_kernel, rows, fused, layer),
            out_shape=jax.ShapeDtypeStruct((slots, width), F32),
            grid=(steps,),
            in_specs=[whole(send.shape), whole(recv.shape)]
            + head_specs
            + [whole(nodes.shape), ws, wr],
            out_specs=by_block,
            scratch_shapes=[pltpu.VMEM((2 * rows, width), BF16)],
            cost_estimate=cost(square * (2 if fused else 1), 6 * slots * width),
            name="own_part",
        )(send, recv, *head, nodes, edge_in, edge_in)
        edges, to_prev, kept, to_next = pl.pallas_call(
            functools.partial(edge_kernel, rows, layer, size),
            out_shape=(
                jax.ShapeDtypeStruct((slots, width), BF16),
                jax.ShapeDtypeStruct((rows, width), BF16),
                jax.ShapeDtypeStruct((rows, width), F32),
                jax.ShapeDtypeStruct((rows, width), BF16),
            ),
            grid=(steps,),
            in_specs=[
                scalars(),
                scalars(),
                whole(send.shape),
                whole(recv.shape),
                by_block,
                by_block,
                whole(nodes.shape),
                whole(nodes.shape),
                whole(nodes.shape),
                whole(far.shape),
                ws,
                wr,
                picked(edge_out.shape, (layer,)),
                whole(edge_gain.shape),
                whole(edge_shift.shape),
            ],
            out_specs=(by_block,) + (whole((rows, width)),) * 3,
            scratch_shapes=[
                pltpu.VMEM((4 * rows + LANES, width), BF16),
                pltpu.VMEM((3 * rows, width), F32),
            ],
            cost_estimate=cost(6 * square, 8 * slots * width),
            name="edge_part",
        )(
            valid_counts,
            hub_owner,
            send,
            recv,
            edges,
            pre,
            nodes,
            from_prev,
            from_next,
            far,
            edge_in,
            edge_in,
            edge_out,
            edge_gain,
            edge_shift,
        )
        sum_next = from_behind(to_prev, "patch", -1)
        sum_prev = from_behind(to_next, "patch", 1)
        if layer + 1 < LAYERS:
            pre = pl.pallas_call(
                functools.partial(linear_kernel, layer + 1),
                out_shape=jax.ShapeDtypeStruct((slots, width), F32),
                grid=(steps,),
                in_specs=[
                    by_block,
                    picked(edge_in.shape, (layer + 1, 0)),
                    whole(edge_bias.shape),
                ],
                out_specs=by_block,
                cost_estimate=cost(square, 6 * slots * width),
                name="linear_part",
            )(edges, edge_in, edge_bias)
        nodes = pl.pallas_call(
            functools.partial(node_kernel, layer),
            out_shape=jax.ShapeDtypeStruct((rows, width), BF16),
            grid=(1,),
            in_specs=[whole((rows, width))] * 4
            + [
                picked(node_in.shape, (layer, 0)),
                picked(node_in.shape, (layer, 1)),
                whole(node_bias.shape),
                picked(node_out.shape, (layer,)),
                whole(node_gain.shape),
                whole(node_shift.shape),
            ],
            out_specs=whole((rows, width)),
            cost_estimate=cost(6 * rows * width * width, 2 * width * width * 3),
            name="node_part",
        )(
            nodes,
            kept,
            sum_prev,
            sum_next,
            node_in,
            node_in,
            node_bias,
            node_out,
            node_gain,
            node_shift,
        )
    return (nodes, edges)


def solution(mesh):
    placed = (
        P(("region", "patch"), None),
        P(("region", "patch"), None),
        P(("region", "patch")),
        P(("region", "patch")),
        P(("region", "patch")),
        P(None, "region"),
    ) + (P(),) * 10
    return jax.shard_map(
        local,
        mesh=mesh,
        in_specs=placed,
        out_specs=(P(("region", "patch"), None), P(("region", "patch"), None)),
        check_vma=False,
    )
```

time: 189 us -> 101 us (0.53)
  Pallas kernels: 0 us -> 50.6 us
  other arithmetic: 47.6 us -> 0 us
  local copies, waits for them, and re-layouts: 52.9 us -> 6.44 us
  blocking collectives: 35 us -> 0 us
  matrix products: 26.7 us -> 0 us
  waiting for transfers between devices: 6.37 us -> 23.8 us
    pallas_call x0 -> x7, Pallas kernels: none -> 50.6 us  [the longest x2 25.4 us: local(): pl.pallas_call(functools.partial(edge_kernel, rows, layer, size), out_sha...]
    gather x4 -> x0, local copies, waits for them, and re-layouts: 36.7 us -> none  [the longest x2 18.4 us: update_edges(): jnp.take(send_table, send_codes, axis=0).astype(jnp.float32)]
    psum x2 -> x0, blocking collectives: 35 us -> none  [spread_2(): return lax.psum(kept, axis)]
    scatter-add x2 -> x0, other arithmetic: 28.9 us -> none  [local(): jax.ops.segment_sum(edges.astype(jnp.float32), receivers, num_segments=3...]
    dot_general x10 -> x0, matrix products: 26.7 us -> none  [the longest x2 14.5 us: update_edges(): jnp.dot(activated, second_weight, preferred_element_type=jnp.float32)]
    ppermute x8 -> x10, waiting for transfers between devices: 6.37 us -> 23.8 us  [from_behind(): lax.ppermute(block, axis, [((i - distance) % size, i) for i in range(size)])]
    convert_element_type x4 -> x0, other arithmetic: 7.19 us -> none  [the longest x2 6.11 us: local(): new_edges = jnp.where(is_valid[:, None], updated, 0.0).astype(jnp.bfloat16)]
    convert_element_type x2 -> x0, local copies, waits for them, and re-layouts: 6.06 us -> none  [local(): edges.astype(jnp.float32)]
  transfers between devices with their start and end apart: 8 -> 10, of which waited for: 4 -> 5; matrix products, arithmetic and copies ran while one was open for 8% -> 2% of each run, Pallas kernels for 0% -> 18%
where the time goes in v1:
time: 101 us; the launch traced here: 100 us
  Pallas kernels  50.6 us (50%)
  waiting for transfers between devices  23.8 us (24%)
  starting transfers between devices  18.3 us (18%)
  local copies, waits for them, and re-layouts  6.44 us (6%)
  between operations  1.35 us (1%)
    pallas_call x2, Pallas kernels, local(): pl.pallas_call(functools.partial(edge_kernel, rows, layer, size), out_sha...  25.4 us
    ppermute x10, waiting for transfers between devices, from_behind(): lax.ppermute(block, axis, [((i - distance) % size, i) for i in range(size)])  23.8 us
    ppermute x10, starting transfers between devices, from_behind(): lax.ppermute(block, axis, [((i - distance) % size, i) for i in range(size)])  18.3 us
    pallas_call x2, Pallas kernels, local(): pl.pallas_call(functools.partial(own_kernel, rows, fused, layer), out_sha...  13.2 us
    pallas_call x2, Pallas kernels, local(): pl.pallas_call(functools.partial(node_kernel, layer), out_shape=jax.Shape...  6.77 us
    pallas_call x1, Pallas kernels, local(): pl.pallas_call(functools.partial(linear_kernel, layer + 1), out_shape=jax...  5.2 us
    unnamed x23, local copies, waits for them, and re-layouts  4.88 us
  transfers between devices with their start and end apart: 10, of which 5 were waited for; matrix products, arithmetic and copies ran while one was open for 2% of the time, Pallas kernels for 18%

profile of v1, /device:TPU:0, one launch (start us, length us, event | category | flops | bytes accessed | tf_op | source)
XLA Modules:
  0.0 100.4 jit_solution(783038971421888242)
XLA Ops:
  0.6 3.1 %collective-permute-start = (bf16[256,512]{1,0:T(8,128)(2,1)}, bf16[256,512]{1,0:T(8,128)(2,1)S(1)}, u32[]{:S(2)}, u32[]{:S(2)}) collective-permute-start(bf16[256,512]{1,0:T(8,128)(2,1)} %nodes_ref.1), channel_id=1, source_target_pairs={{3,0},{0,1},{1,2},{2,3},{7,4},{4,5},{5,6},{6,7},{11,8},{8,9},{9,10... | collective-permute-start | bytes 786440 | tf_op jit(solution)/shard_map/ppermute | solution.py:22
  3.7 2.1 %collective-permute-start.1 = (bf16[256,512]{1,0:T(8,128)(2,1)}, bf16[256,512]{1,0:T(8,128)(2,1)S(1)}, u32[]{:S(2)}, u32[]{:S(2)}) collective-permute-start(bf16[256,512]{1,0:T(8,128)(2,1)} %nodes_ref.1), channel_id=1, source_target_pairs={{1,0},{2,1},{3,2},{0,3},{5,4},{6,5},{7,6},{4,7},{9,8},{10,9},{11,1... | collective-permute-start | bytes 786440 | tf_op jit(solution)/shard_map/ppermute | solution.py:22
  5.8 0.8 slice.6
  6.6 0.9 collective-permute-start.2
  7.6 6.7 %own_part.2.pre_ref = f32[2048,512]{1,0:T(8,128)} custom-call(s32[16,128]{1,0:T(8,128)} %bitcast.2, s32[16,128]{1,0:T(8,128)} %bitcast.6, bf16[2048,512]{1,0:T(8,128)(2,1)} %edges_ref.1, bf16[2,3,512,512]{3,2,1,0:T(8,128)(2,1)} %wr_ref.3, f32[2,512]{1,0:T(2,128)} %bias_ref.4, bf16[256,512]{1,0:T(8,128)(2,1)} %nodes_ref.1, bf16[2,3,512,512]{3,2,1,0:T(8,128)(2,1)} %wr_ref.3, ...), custom_call_target="tpu_custom_call" | custom-call | flops 2147483648 | bytes 6291456 | tf_op jit(solution)/shard_map/own_part/pallas_call | solution.py:266
  15.6 3.7 %collective-permute-done.2.far_ref = bf16[32,512]{1,0:T(8,128)(2,1)S(1)} collective-permute-done((bf16[32,512]{1,0:T(8,128)(2,1)S(1)}, bf16[32,512]{1,0:T(8,128)(2,1)S(1)}, u32[]{:S(2)}, u32[]{:S(2)}) %collective-permute-start.2) | collective-permute-done | bytes 32800 | tf_op jit(solution)/shard_map/ppermute | solution.py:22
  20.0 0.7 copy-done.7
  20.7 12.7 %edge_part.2 = (bf16[2048,512]{1,0:T(8,128)(2,1)}, bf16[256,512]{1,0:T(8,128)(2,1)}, f32[256,512]{1,0:T(8,128)}, bf16[256,512]{1,0:T(8,128)(2,1)}) custom-call(s32[1]{0:T(128)S(6)} %copy.20.valid_ref, s32[2,1]{1,0:T(2,128)} %copy.18.owner_ref, s32[16,128]{1,0:T(8,128)} %bitcast.3, s32[16,128]{1,0:T(8,128)} %bitcast.7, bf16[2048,512]{1,0:T(8,128)(2,1)} %edges_ref.1, ...), custom_call_target="tpu_custom_call" | custom-call | flops 6442450944 | bytes 8388608 | tf_op jit(solution)/shard_map/edge_part/pallas_call | solution.py:278
  33.5 3.8 %collective-permute-start.4 = (bf16[256,512]{1,0:T(8,128)(2,1)}, bf16[256,512]{1,0:T(8,128)(2,1)S(1)}, u32[]{:S(2)}, u32[]{:S(2)}) collective-permute-start(bf16[256,512]{1,0:T(8,128)(2,1)} %get-tuple-element.12), channel_id=1, source_target_pairs={{1,0},{2,1},{3,2},{0,3},{5,4},{6,5},{7,6},{4,7},{9,8},{10,9},{11,1... | collective-permute-start | bytes 786440 | tf_op jit(solution)/shard_map/ppermute | solution.py:22
  37.3 7.4 %collective-permute-done.3.from_prev_ref = bf16[256,512]{1,0:T(8,128)(2,1)S(1)} collective-permute-done((bf16[256,512]{1,0:T(8,128)(2,1)}, bf16[256,512]{1,0:T(8,128)(2,1)S(1)}, u32[]{:S(2)}, u32[]{:S(2)}) %collective-permute-start.3) | collective-permute-done | bytes 262176 | tf_op jit(solution)/shard_map/ppermute | solution.py:22
  44.7 2.9 %collective-permute-done.4.from_next_ref = bf16[256,512]{1,0:T(8,128)(2,1)S(1)} collective-permute-done((bf16[256,512]{1,0:T(8,128)(2,1)}, bf16[256,512]{1,0:T(8,128)(2,1)S(1)}, u32[]{:S(2)}, u32[]{:S(2)}) %collective-permute-start.4) | collective-permute-done | bytes 262176 | tf_op jit(solution)/shard_map/ppermute | solution.py:22
  47.6 0.7 copy-done.3
  48.3 3.4 %node_part.2.refs_3_.own_ref.nodes_ref = bf16[256,512]{1,0:T(8,128)(2,1)} custom-call(bf16[256,512]{1,0:T(8,128)(2,1)} %nodes_ref.1, f32[256,512]{1,0:T(8,128)} %get-tuple-element.10.kept_ref, bf16[256,512]{1,0:T(8,128)(2,1)} %copy-done.1, bf16[256,512]{1,0:T(8,128)(2,1)} %copy-done.3, bf16[2,2,512,512]{3,2,1,0:T(8,128)(2,1)} %wa_ref.3, ...), custom_call_target="tpu_custom_call" | custom-call | flops 402653184 | bytes 1572864 | tf_op jit(solution)/shard_map/node_part/pallas_call | solution.py:344
  51.7 3.8 %collective-permute-start.6 = (bf16[256,512]{1,0:T(8,128)(2,1)}, bf16[256,512]{1,0:T(8,128)(2,1)S(1)}, u32[]{:S(2)}, u32[]{:S(2)}) collective-permute-start(bf16[256,512]{1,0:T(8,128)(2,1)} %node_part.2.refs_3_.own_ref.nodes_ref), channel_id=1, source_target_pairs={{1,0},{2,1},{3,2},{0,3},{5,4},{6,5},{7,6},{4,7},{9,8},{10,9},{11,1... | collective-permute-start | bytes 786440 | tf_op jit(solution)/shard_map/ppermute | solution.py:22
  55.5 5.2 %linear_part.1.refs_2_ = f32[2048,512]{1,0:T(8,128)} custom-call(bf16[2048,512]{1,0:T(8,128)(2,1)} %get-tuple-element.13.edges_ref, bf16[2,3,512,512]{3,2,1,0:T(8,128)(2,1)} %wr_ref.3, f32[2,512]{1,0:T(2,128)} %bias_ref.4), custom_call_target="tpu_custom_call" | custom-call | flops 1073741824 | bytes 6291456 | tf_op jit(solution)/shard_map/linear_part/pallas_call | solution.py:331
  60.7 0.8 slice.8
  62.0 6.5 %own_part.3.pre_ref = f32[2048,512]{1,0:T(8,128)} custom-call(s32[16,128]{1,0:T(8,128)} %bitcast.4, s32[16,128]{1,0:T(8,128)} %bitcast.8, f32[2048,512]{1,0:T(8,128)} %linear_part.1.refs_2_, bf16[256,512]{1,0:T(8,128)(2,1)} %node_part.2.refs_3_.own_ref.nodes_ref, bf16[2,3,512,512]{3,2,1,0:T(8,128)(2,1)} %wr_ref.3, bf16[2,3,512,512]{3,2,1,0:T(8,128)(2,1)} %wr_ref.3), custom_call_target="tpu_custom_call" | custom-call | flops 1073741824 | bytes 6291456 | tf_op jit(solution)/shard_map/own_part/pallas_call | solution.py:266
  69.3 0.7 copy-done.5
  70.0 12.7 %edge_part.3 = (bf16[2048,512]{1,0:T(8,128)(2,1)}, bf16[256,512]{1,0:T(8,128)(2,1)}, f32[256,512]{1,0:T(8,128)}, bf16[256,512]{1,0:T(8,128)(2,1)}) custom-call(s32[1]{0:T(128)S(6)} %copy.20.valid_ref, s32[2,1]{1,0:T(2,128)} %copy.18.owner_ref, s32[16,128]{1,0:T(8,128)} %bitcast.5, s32[16,128]{1,0:T(8,128)} %bitcast.9, ...), custom_call_target="tpu_custom_call" | custom-call | flops 6442450944 | bytes 8388608 | tf_op jit(solution)/shard_map/edge_part/pallas_call | solution.py:278
  82.9 3.6 %collective-permute-start.9 = (bf16[256,512]{1,0:T(8,128)(2,1)}, bf16[256,512]{1,0:T(8,128)(2,1)S(1)}, u32[]{:S(2)}, u32[]{:S(2)}) collective-permute-start(bf16[256,512]{1,0:T(8,128)(2,1)} %get-tuple-element.16), channel_id=1, source_target_pairs={{1,0},{2,1},{3,2},{0,3},{5,4},{6,5},{7,6},{4,7},{9,8},{10,9},{11,1... | collective-permute-start | bytes 786440 | tf_op jit(solution)/shard_map/ppermute | solution.py:22
  86.5 7.4 %collective-permute-done.8.from_prev_ref = bf16[256,512]{1,0:T(8,128)(2,1)S(1)} collective-permute-done((bf16[256,512]{1,0:T(8,128)(2,1)}, bf16[256,512]{1,0:T(8,128)(2,1)S(1)}, u32[]{:S(2)}, u32[]{:S(2)}) %collective-permute-start.8) | collective-permute-done | bytes 262176 | tf_op jit(solution)/shard_map/ppermute | solution.py:22
  93.9 2.4 %collective-permute-done.9.from_next_ref = bf16[256,512]{1,0:T(8,128)(2,1)S(1)} collective-permute-done((bf16[256,512]{1,0:T(8,128)(2,1)}, bf16[256,512]{1,0:T(8,128)(2,1)S(1)}, u32[]{:S(2)}, u32[]{:S(2)}) %collective-permute-start.9) | collective-permute-done | bytes 262176 | tf_op jit(solution)/shard_map/ppermute | solution.py:22
  96.3 0.7 copy-done.2
  97.0 3.4 %node_part.3 = bf16[256,512]{1,0:T(8,128)(2,1)} custom-call(bf16[256,512]{1,0:T(8,128)(2,1)} %node_part.2.refs_3_.own_ref.nodes_ref, f32[256,512]{1,0:T(8,128)} %get-tuple-element.14.kept_ref, bf16[256,512]{1,0:T(8,128)(2,1)} %copy-done, bf16[256,512]{1,0:T(8,128)(2,1)} %copy-done.2, bf16[2,2,512,512]{3,2,1,0:T(8,128)(2,1)} %wa_ref.3, ...), custom_call_target="tpu_custom_call" | custom-call | flops 402653184 | bytes 1572864 | tf_op jit(solution)/shard_map/node_part/pallas_call | solution.py:344
  (28 shorter events, 3.0 us)
Async XLA Ops:
  0.6 18.7 %collective-permute-start = (bf16[256,512]{1,0:T(8,128)(2,1)}, bf16[256,512]{1,0:T(8,128)(2,1)S(1)}, u32[]{:S(2)}, u32[]{:S(2)}) collective-permute-start(bf16[256,512]{1,0:T(8,128)(2,1)} %nodes_ref.1), channel_id=1, source_target_pairs={{3,0},{0,1},{1,2},{2,3},{7,4},{4,5},{5,6},{6,7},{11,8},{8,9},{9,10... | collective-permute-start | bytes 786440 | tf_op jit(solution)/shard_map/ppermute | solution.py:22
  3.7 15.6 %collective-permute-start.1 = (bf16[256,512]{1,0:T(8,128)(2,1)}, bf16[256,512]{1,0:T(8,128)(2,1)S(1)}, u32[]{:S(2)}, u32[]{:S(2)}) collective-permute-start(bf16[256,512]{1,0:T(8,128)(2,1)} %nodes_ref.1), channel_id=1, source_target_pairs={{1,0},{2,1},{3,2},{0,3},{5,4},{6,5},{7,6},{4,7},{9,8},{10,9},{11,1... | collective-permute-start | bytes 786440 | tf_op jit(solution)/shard_map/ppermute | solution.py:22
  6.6 12.7 %collective-permute-start.2 = (bf16[32,512]{1,0:T(8,128)(2,1)S(1)}, bf16[32,512]{1,0:T(8,128)(2,1)S(1)}, u32[]{:S(2)}, u32[]{:S(2)}) collective-permute-start(bf16[32,512]{1,0:T(8,128)(2,1)S(1)} %slice.6), channel_id=1, source_target_pairs={{2,0},{3,1},{0,2},{1,3},{6,4},{7,5},{4,6},{5,7},{10,8},{11,9},{8,1... | collective-permute-start | bytes 98312 | tf_op jit(solution)/shard_map/ppermute | solution.py:22
  7.6 6.7 %copy-start.10 = (s32[2,1]{0,1:T(1,128)S(1)}, s32[2,1]{0,1:T(1,128)}, u32[]{:S(2)}) copy-start(s32[2,1]{0,1:T(1,128)} %param.21) | copy-start | bytes 28
  19.3 0.6 copy-start.9
  19.3 0.7 copy-start.6
  20.0 0.7 copy-start.7
  33.4 11.3 %collective-permute-start.3 = (bf16[256,512]{1,0:T(8,128)(2,1)}, bf16[256,512]{1,0:T(8,128)(2,1)S(1)}, u32[]{:S(2)}, u32[]{:S(2)}) collective-permute-start(bf16[256,512]{1,0:T(8,128)(2,1)} %get-tuple-element.11), channel_id=1, source_target_pairs={{3,0},{0,1},{1,2},{2,3},{7,4},{4,5},{5,6},{6,7},{11,8},{8,9},{9,10... | collective-permute-start | bytes 786440 | tf_op jit(solution)/shard_map/ppermute | solution.py:22
  33.5 14.1 %collective-permute-start.4 = (bf16[256,512]{1,0:T(8,128)(2,1)}, bf16[256,512]{1,0:T(8,128)(2,1)S(1)}, u32[]{:S(2)}, u32[]{:S(2)}) collective-permute-start(bf16[256,512]{1,0:T(8,128)(2,1)} %get-tuple-element.12), channel_id=1, source_target_pairs={{1,0},{2,1},{3,2},{0,3},{5,4},{6,5},{7,6},{4,7},{9,8},{10,9},{11,1... | collective-permute-start | bytes 786440 | tf_op jit(solution)/shard_map/ppermute | solution.py:22
  44.7 2.9 %copy-start.1 = (bf16[256,512]{1,0:T(8,128)(2,1)}, bf16[256,512]{1,0:T(8,128)(2,1)S(1)}, u32[]{:S(2)}) copy-start(bf16[256,512]{1,0:T(8,128)(2,1)S(1)} %collective-permute-done.3.from_prev_ref) | copy-start | bytes 786436
  47.6 0.7 copy-start.3
  51.7 16.9 %collective-permute-start.5 = (bf16[256,512]{1,0:T(8,128)(2,1)}, bf16[256,512]{1,0:T(8,128)(2,1)S(1)}, u32[]{:S(2)}, u32[]{:S(2)}) collective-permute-start(bf16[256,512]{1,0:T(8,128)(2,1)} %node_part.2.refs_3_.own_ref.nodes_ref), channel_id=1, source_target_pairs={{3,0},{0,1},{1,2},{2,3},{7,4},{4,5},{5,6},{6,7},{11,8},{8,9},{9,10... | collective-permute-start | bytes 786440 | tf_op jit(solution)/shard_map/ppermute | solution.py:22
  51.7 16.9 %collective-permute-start.6 = (bf16[256,512]{1,0:T(8,128)(2,1)}, bf16[256,512]{1,0:T(8,128)(2,1)S(1)}, u32[]{:S(2)}, u32[]{:S(2)}) collective-permute-start(bf16[256,512]{1,0:T(8,128)(2,1)} %node_part.2.refs_3_.own_ref.nodes_ref), channel_id=1, source_target_pairs={{1,0},{2,1},{3,2},{0,3},{5,4},{6,5},{7,6},{4,7},{9,8},{10,9},{11,1... | collective-permute-start | bytes 786440 | tf_op jit(solution)/shard_map/ppermute | solution.py:22
  61.5 7.1 %collective-permute-start.7 = (bf16[32,512]{1,0:T(8,128)(2,1)S(1)}, bf16[32,512]{1,0:T(8,128)(2,1)S(1)}, u32[]{:S(2)}, u32[]{:S(2)}) collective-permute-start(bf16[32,512]{1,0:T(8,128)(2,1)S(1)} %slice.8), channel_id=1, source_target_pairs={{2,0},{3,1},{0,2},{1,3},{6,4},{7,5},{4,6},{5,7},{10,8},{11,9},{8,1... | collective-permute-start | bytes 98312 | tf_op jit(solution)/shard_map/ppermute | solution.py:22
  68.5 0.6 copy-start.8
  68.6 0.7 copy-start.4
  69.3 0.7 copy-start.5
  82.6 11.2 %collective-permute-start.8 = (bf16[256,512]{1,0:T(8,128)(2,1)}, bf16[256,512]{1,0:T(8,128)(2,1)S(1)}, u32[]{:S(2)}, u32[]{:S(2)}) collective-permute-start(bf16[256,512]{1,0:T(8,128)(2,1)} %get-tuple-element.15), channel_id=1, source_target_pairs={{3,0},{0,1},{1,2},{2,3},{7,4},{4,5},{5,6},{6,7},{11,8},{8,9},{9,10... | collective-permute-start | bytes 786440 | tf_op jit(solution)/shard_map/ppermute | solution.py:22
  82.9 13.4 %collective-permute-start.9 = (bf16[256,512]{1,0:T(8,128)(2,1)}, bf16[256,512]{1,0:T(8,128)(2,1)S(1)}, u32[]{:S(2)}, u32[]{:S(2)}) collective-permute-start(bf16[256,512]{1,0:T(8,128)(2,1)} %get-tuple-element.16), channel_id=1, source_target_pairs={{1,0},{2,1},{3,2},{0,3},{5,4},{6,5},{7,6},{4,7},{9,8},{10,9},{11,1... | collective-permute-start | bytes 786440 | tf_op jit(solution)/shard_map/ppermute | solution.py:22
  93.9 2.4 %copy-start = (bf16[256,512]{1,0:T(8,128)(2,1)}, bf16[256,512]{1,0:T(8,128)(2,1)S(1)}, u32[]{:S(2)}) copy-start(bf16[256,512]{1,0:T(8,128)(2,1)S(1)} %collective-permute-done.8.from_prev_ref) | copy-start | bytes 786436
  96.3 0.7 copy-start.2

commit v2 on v1

--- a/solution.py
+++ b/solution.py
@@ -10,6 +10,7 @@
 HUB = 32
 LAYERS = 2
 LANES = 128
+GRANT = 24 << 20
 
 epsilon = 1e-05
 
@@ -68,34 +69,83 @@
     out_ref[...] = dot(edges_ref[...], weight_ref[0, 0]) + bias_ref[layer : layer + 1, :]
 
 
-def own_kernel(rows, fused, layer, *refs):
-    if fused:
-        (send_ref, recv_ref, edges_ref, first_ref, bias_ref, nodes_ref, ws_ref, wr_ref) = refs[:8]
-    else:
-        (send_ref, recv_ref, pre_ref, nodes_ref, ws_ref, wr_ref) = refs[:6]
-    out_ref, table_ref = refs[-2:]
-    step = pl.program_id(0)
-
-    @pl.when(step == 0)
-    def _():
-        own = nodes_ref[...]
-        table_ref[:rows, :] = dot(own, ws_ref[0, 0]).astype(BF16)
-        table_ref[rows:, :] = dot(own, wr_ref[0, 0]).astype(BF16)
-
-    count = out_ref.shape[0] // LANES
-    picks = jnp.concatenate(
+def own_table(nodes, ws_ref, wr_ref, table_ref):
+    rows = nodes.shape[0]
+    table_ref[:rows, :] = dot(nodes, ws_ref[0, 0]).astype(BF16)
+    table_ref[rows:, :] = dot(nodes, wr_ref[0, 0]).astype(BF16)
+
+
+def own_picks(send_ref, recv_ref, first, count, rows):
+    return jnp.concatenate(
         [
-            one_hot(columns_of(send_ref, step * count, count), rows, rows),
-            one_hot(columns_of(recv_ref, step * count, count), rows, rows),
+            one_hot(columns_of(send_ref, first, count), rows, rows),
+            one_hot(columns_of(recv_ref, first, count), rows, rows),
         ],
         axis=1,
     )
-    total = dot(picks, table_ref[...])
-    if fused:
-        total = total + dot(edges_ref[...], first_ref[0, 0]) + bias_ref[layer : layer + 1, :]
-    else:
-        total = total + pre_ref[...]
-    out_ref[...] = total
+
+
+def own_kernel(send_ref, recv_ref, pre_ref, nodes_ref, ws_ref, wr_ref, out_ref, table_ref):
+    step = pl.program_id(0)
+    rows = nodes_ref.shape[0]
+
+    @pl.when(step == 0)
+    def _():
+        own_table(nodes_ref[...], ws_ref, wr_ref, table_ref)
+
+    count = out_ref.shape[0] // LANES
+    picks = own_picks(send_ref, recv_ref, step * count, count, rows)
+    out_ref[...] = pre_ref[...] + dot(picks, table_ref[...])
+
+
+def first_kernel(
+    parity,
+    layer,
+    steps,
+    send_ref,
+    recv_ref,
+    nodes_ref,
+    bias_ref,
+    edges_ref,
+    weights_ref,
+    *refs,
+):
+    out_ref, table_ref, weight_buf, edges_buf, out_buf, weight_sem, in_sem, out_sem = refs[-8:]
+    rows = nodes_ref.shape[0]
+    block = edges_buf.shape[0] // steps
+    count = block // LANES
+
+    def span(i):
+        return pl.ds(i * block, block)
+
+    def fetch(i):
+        return pltpu.make_async_copy(edges_ref.at[span(i)], edges_buf.at[span(i)], in_sem.at[i])
+
+    def weight(i):
+        return pltpu.make_async_copy(weights_ref.at[layer, i], weight_buf.at[i], weight_sem.at[i])
+
+    def put(i):
+        return pltpu.make_async_copy(out_buf.at[span(i)], out_ref.at[span(i)], out_sem.at[i])
+
+    @pl.when(lax.axis_index("region") % 2 == parity)
+    def _():
+        for i in (1, 2, 0):
+            weight(i).start()
+        for i in range(steps):
+            fetch(i).start()
+        weight(1).wait()
+        table_ref[:rows, :] = dot(nodes_ref[...], weight_buf[1]).astype(BF16)
+        weight(2).wait()
+        table_ref[rows:, :] = dot(nodes_ref[...], weight_buf[2]).astype(BF16)
+        weight(0).wait()
+        for i in range(steps):
+            fetch(i).wait()
+            picks = own_picks(send_ref, recv_ref, i * count, count, rows)
+            total = dot(picks, table_ref[...]) + dot(edges_buf[span(i), :], weight_buf[0])
+            out_buf[span(i), :] = total + bias_ref[layer : layer + 1, :]
+            put(i).start()
+        for i in range(steps):
+            put(i).wait()
 
 
 def edge_kernel(
@@ -190,8 +240,9 @@
     wo_ref,
     gain_ref,
     shift_ref,
-    out_ref,
+    *refs,
 ):
+    out_ref = refs[-1]
     nodes = nodes_ref[...]
     summed = from_prev_ref[...].astype(F32) + kept_ref[...] + from_next_ref[...].astype(F32)
     pre_node = dot(nodes, wh_ref[0, 0]) + dot(summed.astype(BF16), wa_ref[0, 0])
@@ -246,35 +297,56 @@
     recv = receivers.reshape(slots // LANES, LANES)
     by_block = pl.BlockSpec((block, width), lambda i: (i, 0))
     square = 2 * slots * width * width
-    pre = None
+    def start_edges(parity, held):
+        anywhere = pl.BlockSpec(memory_space=pltpu.HBM)
+        given = () if held is None else (held,)
+        return pl.pallas_call(
+            functools.partial(first_kernel, parity, 0, steps),
+            out_shape=jax.ShapeDtypeStruct((slots, width), F32),
+            in_specs=[whole(send.shape), whole(recv.shape), whole(nodes.shape)]
+            + [whole(edge_bias.shape), anywhere, anywhere]
+            + [anywhere] * len(given),
+            out_specs=anywhere,
+            grid=(1,),
+            input_output_aliases={6: 0} if given else {},
+            scratch_shapes=[
+                pltpu.VMEM((2 * rows, width), BF16),
+                pltpu.VMEM((3, width, width), BF16),
+                pltpu.VMEM((slots, width), BF16),
+                pltpu.VMEM((slots, width), F32),
+                pltpu.SemaphoreType.DMA((3,)),
+                pltpu.SemaphoreType.DMA((steps,)),
+                pltpu.SemaphoreType.DMA((steps,)),
+            ],
+            cost_estimate=cost(2 * square, 6 * slots * width),
+            name="first_part",
+        )(send, recv, nodes, edge_bias, edges, edge_in, *given)
+
+    early = start_edges(1, None)
+    nodes, early = lax.optimization_barrier((nodes, early))
     for layer in range(LAYERS):
         from_prev = from_behind(nodes, "patch", 1)
         from_next = from_behind(nodes, "patch", -1)
         top = nodes[:HUB]
         far = [from_behind(top, "patch", -d) for d in range(2, size - 1)]
         far = jnp.concatenate(far, axis=0) if len(far) > 1 else (far[0] if far else top)
-        w0 = picked(edge_in.shape, (layer, 0))
         ws = picked(edge_in.shape, (layer, 1))
         wr = picked(edge_in.shape, (layer, 2))
-        fused = pre is None
-        if fused:
-            head = (edges, edge_in, edge_bias)
-            head_specs = [by_block, w0, whole(edge_bias.shape)]
+        if layer == 0:
+            pre = start_edges(0, early)
         else:
-            head = (pre,)
-            head_specs = [by_block]
-        pre = pl.pallas_call(
-            functools.partial(own_kernel, rows, fused, layer),
-            out_shape=jax.ShapeDtypeStruct((slots, width), F32),
-            grid=(steps,),
-            in_specs=[whole(send.shape), whole(recv.shape)]
-            + head_specs
-            + [whole(nodes.shape), ws, wr],
-            out_specs=by_block,
-            scratch_shapes=[pltpu.VMEM((2 * rows, width), BF16)],
-            cost_estimate=cost(square * (2 if fused else 1), 6 * slots * width),
-            name="own_part",
-        )(send, recv, *head, nodes, edge_in, edge_in)
+            pre = pl.pallas_call(
+                own_kernel,
+                out_shape=jax.ShapeDtypeStruct((slots, width), F32),
+                grid=(steps,),
+                in_specs=[whole(send.shape), whole(recv.shape), by_block]
+                + [whole(nodes.shape), ws, wr],
+                out_specs=by_block,
+                scratch_shapes=[pltpu.VMEM((2 * rows, width), BF16)],
+                compiler_params=pltpu.CompilerParams(vmem_limit_bytes=GRANT),
+                cost_estimate=cost(square, 8 * slots * width),
+                name="own_part",
+            )(send, recv, pre, nodes, edge_in, edge_in)
         edges, to_prev, kept, to_next = pl.pallas_call(
             functools.partial(edge_kernel, rows, layer, size),
             out_shape=(
@@ -306,6 +378,7 @@
                 pltpu.VMEM((4 * rows + LANES, width), BF16),
                 pltpu.VMEM((3 * rows, width), F32),
             ],
+            compiler_params=pltpu.CompilerParams(vmem_limit_bytes=GRANT),
             cost_estimate=cost(6 * square, 8 * slots * width),
             name="edge_part",
         )(
@@ -327,6 +400,7 @@
         )
         sum_next = from_behind(to_prev, "patch", -1)
         sum_prev = from_behind(to_next, "patch", 1)
+        after = ()
         if layer + 1 < LAYERS:
             pre = pl.pallas_call(
                 functools.partial(linear_kernel, layer + 1),
@@ -338,9 +412,11 @@
                     whole(edge_bias.shape),
                 ],
                 out_specs=by_block,
+                compiler_params=pltpu.CompilerParams(vmem_limit_bytes=GRANT),
                 cost_estimate=cost(square, 6 * slots * width),
                 name="linear_part",
             )(edges, edge_in, edge_bias)
+            after = (pre,)
         nodes = pl.pallas_call(
             functools.partial(node_kernel, layer),
             out_shape=jax.ShapeDtypeStruct((rows, width), BF16),
@@ -353,8 +429,10 @@
                 picked(node_out.shape, (layer,)),
                 whole(node_gain.shape),
                 whole(node_shift.shape),
-            ],
+            ]
+            + [pl.BlockSpec(memory_space=pl.ANY)] * len(after),
             out_specs=whole((rows, width)),
+            compiler_params=pltpu.CompilerParams(vmem_limit_bytes=GRANT),
             cost_estimate=cost(6 * rows * width * width, 2 * width * width * 3),
             name="node_part",
         )(
@@ -368,6 +446,7 @@
             node_out,
             node_gain,
             node_shift,
+            *after,
         )
     return (nodes, edges)
 

time: 101 us -> 93.6 us (0.927)
  Pallas kernels: 50.6 us -> 36.5 us
  waiting for transfers between devices: 23.8 us -> 32.3 us
  starting transfers between devices: 18.3 us -> 17 us
    ppermute x10, waiting for transfers between devices: 23.8 us -> 32.3 us  [from_behind(): lax.ppermute(block, axis, [((i - distance) % size, i) for i in range(size)])]
    pallas_call x2, Pallas kernels: 25.4 us -> 21 us  [local(): pl.pallas_call(functools.partial(edge_kernel, rows, layer, size), out_sha...]
    pallas_call x1, Pallas kernels: 5.2 us -> 1.78 us  [local(): pl.pallas_call(functools.partial(linear_kernel, layer + 1), out_shape=jax...]
    pallas_call x2, Pallas kernels: 6.77 us -> 3.52 us  [local(): pl.pallas_call(functools.partial(node_kernel, layer), out_shape=jax.Shape...]
    pallas_call x2 -> x3, Pallas kernels: 13.2 us -> 10.2 us  [the longest x2 7.8 us: start_edges(): pl.pallas_call(functools.partial(first_kernel, parity, 0, steps), out_sha...]
    ppermute x10, starting transfers between devices: 18.3 us -> 17 us  [from_behind(): lax.ppermute(block, axis, [((i - distance) % size, i) for i in range(size)])]
    unnamed x23 -> x33, local copies, waits for them, and re-layouts: 4.88 us -> 5.15 us
  transfers between devices with their start and end apart: 10 -> 10, of which waited for: 5 -> 6; matrix products, arithmetic and copies ran while one was open for 2% -> 1% of each run, Pallas kernels for 18% -> 12%
where the time goes in v2:
time: 93.6 us; the launch traced here: 93.2 us
  Pallas kernels  36.5 us (39%)
  waiting for transfers between devices  32.3 us (35%)
  starting transfers between devices  17 us (18%)
  local copies, waits for them, and re-layouts  5.98 us (6%)
  between operations  1.45 us (2%)
    ppermute x10, waiting for transfers between devices, from_behind(): lax.ppermute(block, axis, [((i - distance) % size, i) for i in range(size)])  32.3 us
    pallas_call x2, Pallas kernels, local(): pl.pallas_call(functools.partial(edge_kernel, rows, layer, size), out_sha...  21 us
    ppermute x10, starting transfers between devices, from_behind(): lax.ppermute(block, axis, [((i - distance) % size, i) for i in range(size)])  17 us
    pallas_call x2, Pallas kernels, start_edges(): pl.pallas_call(functools.partial(first_kernel, parity, 0, steps), out_sha...  7.8 us
    unnamed x33, local copies, waits for them, and re-layouts  5.15 us
    pallas_call x2, Pallas kernels, local(): pl.pallas_call(functools.partial(node_kernel, layer), out_shape=jax.Shape...  3.52 us
    pallas_call x1, Pallas kernels, local(): pl.pallas_call(own_kernel, out_shape=jax.ShapeDtypeStruct((slots, width),...  2.43 us
  transfers between devices with their start and end apart: 10, of which 6 were waited for; matrix products, arithmetic and copies ran while one was open for 1% of the time, Pallas kernels for 12%

profile of v2, /device:TPU:0, one launch (start us, length us, event | category | flops | bytes accessed | tf_op | source)
XLA Modules:
  0.0 93.2 jit_solution(14028540750995296350)
XLA Ops:
  0.6 1.1 %first_part.2.refs_0_ = f32[2048,512]{1,0:T(8,128)} custom-call(s32[16,128]{1,0:T(8,128)} %bitcast.2, s32[16,128]{1,0:T(8,128)} %bitcast.7, bf16[256,512]{1,0:T(8,128)(2,1)} %nodes_ref.3, f32[2,512]{1,0:T(2,128)} %bias_ref.7, bf16[2048,512]{1,0:T(8,128)(2,1)} %edges_ref.5, bf16[2,3,512,512]{3,2,1,0:T(8,128)(2,1)} %wr_ref.5), custom_call_target="tpu_custom_call" | custom-call | flops 2147483648 | bytes 6291456 | tf_op jit(solution)/shard_map/first_part/pallas_call | solution.py:303
  1.7 5.1 %collective-permute-start.1 = (bf16[256,512]{1,0:T(8,128)(2,1)}, bf16[256,512]{1,0:T(8,128)(2,1)S(1)}, u32[]{:S(2)}, u32[]{:S(2)}) collective-permute-start(bf16[256,512]{1,0:T(8,128)(2,1)} %nodes_ref.3), channel_id=1, source_target_pairs={{1,0},{2,1},{3,2},{0,3},{5,4},{6,5},{7,6},{4,7},{9,8},{10,9},{11,1... | collective-permute-start | bytes 786440 | tf_op jit(solution)/shard_map/ppermute | solution.py:23
  6.9 0.8 slice.6
  7.7 1.0 %collective-permute-start.2 = (bf16[32,512]{1,0:T(8,128)(2,1)S(1)}, bf16[32,512]{1,0:T(8,128)(2,1)S(1)}, u32[]{:S(2)}, u32[]{:S(2)}) collective-permute-start(bf16[32,512]{1,0:T(8,128)(2,1)S(1)} %slice.6), channel_id=1, source_target_pairs={{2,0},{3,1},{0,2},{1,3},{6,4},{7,5},{4,6},{5,7},{10,8},{11,9},{8,1... | collective-permute-start | bytes 98312 | tf_op jit(solution)/shard_map/ppermute | solution.py:23
  8.8 6.7 %first_part.3.pre_ref = f32[2048,512]{1,0:T(8,128)} custom-call(s32[16,128]{1,0:T(8,128)} %bitcast.3, s32[16,128]{1,0:T(8,128)} %bitcast.8, bf16[256,512]{1,0:T(8,128)(2,1)} %nodes_ref.3, f32[2,512]{1,0:T(2,128)} %bias_ref.7, bf16[2048,512]{1,0:T(8,128)(2,1)} %edges_ref.5, bf16[2,3,512,512]{3,2,1,0:T(8,128)(2,1)} %wr_ref.5, ...), custom_call_target="tpu_custom_call", output_to_operand_aliasing={{}: (6, {})} | custom-call | flops 2147483648 | bytes 6291456 | tf_op jit(solution)/shard_map/first_part/pallas_call | solution.py:303
  16.2 0.9 collective-permute-done.prev_ref
  17.2 2.2 %copy-done.2 = f32[2048,512]{1,0:T(8,128)S(1)} copy-done((f32[2048,512]{1,0:T(8,128)S(1)}, f32[2048,512]{1,0:T(8,128)}, u32[]{:S(2)}) %copy-start.2) | copy-done | bytes 4194328
  19.4 1.6 %copy-done.3 = bf16[2048,512]{1,0:T(8,128)(2,1)S(1)} copy-done((bf16[2048,512]{1,0:T(8,128)(2,1)S(1)}, bf16[2048,512]{1,0:T(8,128)(2,1)}, u32[]{:S(2)}) %copy-start.3) | copy-done | bytes 2097176
  20.9 1.2 %copy-done.11 = bf16[2,512,512]{2,1,0:T(8,128)(2,1)S(1)} copy-done((bf16[2,512,512]{2,1,0:T(8,128)(2,1)S(1)}, bf16[2,512,512]{2,1,0:T(8,128)(2,1)}, u32[]{:S(2)}) %copy-start.11) | copy-done | bytes 1048600
  22.2 10.3 %edge_part.2 = (bf16[2048,512]{1,0:T(8,128)(2,1)S(1)}, bf16[256,512]{1,0:T(8,128)(2,1)S(1)}, f32[256,512]{1,0:T(8,128)S(1)}, bf16[256,512]{1,0:T(8,128)(2,1)S(1)}) custom-call(s32[1]{0:T(128)S(6)} %copy.22.valid_ref, s32[2,1]{1,0:T(2,128)S(1)} %copy.19.owner_ref, s32[16,128]{1,0:T(8,128)S(1)} %bitcast.4, s32[16,128]{1,0:T(8,128)S(1)} %bitcast.9, ...), custom_call_target="tpu_custom_call" | custom-call | flops 6442450944 | bytes 8388608 | tf_op jit(solution)/shard_map/edge_part/pallas_call | solution.py:350
  32.5 2.6 %collective-permute-start.3 = (bf16[256,512]{1,0:T(8,128)(2,1)S(1)}, bf16[256,512]{1,0:T(8,128)(2,1)S(1)}, u32[]{:S(2)}, u32[]{:S(2)}) collective-permute-start(bf16[256,512]{1,0:T(8,128)(2,1)S(1)} %get-tuple-element.15), channel_id=1, source_target_pairs={{3,0},{0,1},{1,2},{2,3},{7,4},{4,5},{5,6},{6,7},{11,8},{8,9},{9,10... | collective-permute-start | bytes 786440 | tf_op jit(solution)/shard_map/ppermute | solution.py:23
  35.1 2.1 %collective-permute-start.4 = (bf16[256,512]{1,0:T(8,128)(2,1)S(1)}, bf16[256,512]{1,0:T(8,128)(2,1)S(1)}, u32[]{:S(2)}, u32[]{:S(2)}) collective-permute-start(bf16[256,512]{1,0:T(8,128)(2,1)S(1)} %get-tuple-element.16), channel_id=1, source_target_pairs={{1,0},{2,1},{3,2},{0,3},{5,4},{6,5},{7,6},{4,7},{9,8},{10,9},{11,1... | collective-permute-start | bytes 786440 | tf_op jit(solution)/shard_map/ppermute | solution.py:23
  37.2 1.8 %linear_part.1.refs_0_.pre_ref = f32[2048,512]{1,0:T(8,128)S(1)} custom-call(bf16[2048,512]{1,0:T(8,128)(2,1)S(1)} %get-tuple-element.17.edges_ref, bf16[2,3,512,512]{3,2,1,0:T(8,128)(2,1)S(1)} %copy-done, f32[2,512]{1,0:T(2,128)S(1)} %copy-done.7), custom_call_target="tpu_custom_call" | custom-call | flops 1073741824 | bytes 6291456 | tf_op jit(solution)/shard_map/linear_part/pallas_call | solution.py:405
  39.0 2.6 %collective-permute-done.3.from_prev_ref = bf16[256,512]{1,0:T(8,128)(2,1)S(1)} collective-permute-done((bf16[256,512]{1,0:T(8,128)(2,1)S(1)}, bf16[256,512]{1,0:T(8,128)(2,1)S(1)}, u32[]{:S(2)}, u32[]{:S(2)}) %collective-permute-start.3) | collective-permute-done | bytes 262176 | tf_op jit(solution)/shard_map/ppermute | solution.py:23
  41.6 8.1 %collective-permute-done.4.from_next_ref = bf16[256,512]{1,0:T(8,128)(2,1)S(1)} collective-permute-done((bf16[256,512]{1,0:T(8,128)(2,1)S(1)}, bf16[256,512]{1,0:T(8,128)(2,1)S(1)}, u32[]{:S(2)}, u32[]{:S(2)}) %collective-permute-start.4) | collective-permute-done | bytes 262176 | tf_op jit(solution)/shard_map/ppermute | solution.py:23
  49.8 1.9 %node_part.2.nodes_ref.own_ref = bf16[256,512]{1,0:T(8,128)(2,1)S(1)} custom-call(bf16[256,512]{1,0:T(8,128)(2,1)} %nodes_ref.3, f32[256,512]{1,0:T(8,128)S(1)} %get-tuple-element.14.kept_ref, bf16[256,512]{1,0:T(8,128)(2,1)S(1)} %collective-permute-done.3.from_prev_ref, bf16[256,512]{1,0:T(8,128)(2,1)S(1)} %collective-permute-done.4.from_next_ref, ...), custom_call_target="tpu_custom_call" | custom-call | flops 402653184 | bytes 1572864 | tf_op jit(solution)/shard_map/node_part/pallas_call | solution.py:420
  52.1 1.6 %collective-permute-start.5 = (bf16[256,512]{1,0:T(8,128)(2,1)S(1)}, bf16[256,512]{1,0:T(8,128)(2,1)S(1)}, u32[]{:S(2)}, u32[]{:S(2)}) collective-permute-start(bf16[256,512]{1,0:T(8,128)(2,1)S(1)} %node_part.2.nodes_ref.own_ref), channel_id=1, source_target_pairs={{3,0},{0,1},{1,2},{2,3},{7,4},{4,5},{5,6},{6,7},{11,8},{8,9},{9,10... | collective-permute-start | bytes 786440 | tf_op jit(solution)/shard_map/ppermute | solution.py:23
  53.9 2.4 %own_part.1.pre_ref = f32[2048,512]{1,0:T(8,128)S(1)} custom-call(s32[16,128]{1,0:T(8,128)S(1)} %bitcast.5, s32[16,128]{1,0:T(8,128)S(1)} %bitcast.10, f32[2048,512]{1,0:T(8,128)S(1)} %linear_part.1.refs_0_.pre_ref, bf16[256,512]{1,0:T(8,128)(2,1)S(1)} %node_part.2.nodes_ref.own_ref, bf16[2,3,512,512]{3,2,1,0:T(8,128)(2,1)S(1)} %copy-done, ...), custom_call_target="tpu_custom_call" | custom-call | flops 1073741824 | bytes 8388608 | tf_op jit(solution)/shard_map/own_part/pallas_call | solution.py:338
  56.3 10.8 %collective-permute-done.7.far_ref = bf16[32,512]{1,0:T(8,128)(2,1)S(1)} collective-permute-done((bf16[32,512]{1,0:T(8,128)(2,1)S(1)}, bf16[32,512]{1,0:T(8,128)(2,1)S(1)}, u32[]{:S(2)}, u32[]{:S(2)}) %collective-permute-start.7) | collective-permute-done | bytes 32800 | tf_op jit(solution)/shard_map/ppermute | solution.py:23
  67.1 10.7 %edge_part.3 = (bf16[2048,512]{1,0:T(8,128)(2,1)}, bf16[256,512]{1,0:T(8,128)(2,1)S(1)}, f32[256,512]{1,0:T(8,128)S(1)}, bf16[256,512]{1,0:T(8,128)(2,1)S(1)}) custom-call(s32[1]{0:T(128)S(6)} %copy.22.valid_ref, s32[2,1]{1,0:T(2,128)S(1)} %copy.19.owner_ref, s32[16,128]{1,0:T(8,128)S(1)} %bitcast.6, s32[16,128]{1,0:T(8,128)S(1)} %bitcast.11, ...), custom_call_target="tpu_custom_call" | custom-call | flops 6442450944 | bytes 8388608 | tf_op jit(solution)/shard_map/edge_part/pallas_call | solution.py:350
  78.0 3.6 %collective-permute-start.9 = (bf16[256,512]{1,0:T(8,128)(2,1)S(1)}, bf16[256,512]{1,0:T(8,128)(2,1)S(1)}, u32[]{:S(2)}, u32[]{:S(2)}) collective-permute-start(bf16[256,512]{1,0:T(8,128)(2,1)S(1)} %get-tuple-element.20), channel_id=1, source_target_pairs={{1,0},{2,1},{3,2},{0,3},{5,4},{6,5},{7,6},{4,7},{9,8},{10,9},{11,1... | collective-permute-start | bytes 786440 | tf_op jit(solution)/shard_map/ppermute | solution.py:23
  81.7 7.2 %collective-permute-done.8.from_prev_ref = bf16[256,512]{1,0:T(8,128)(2,1)S(1)} collective-permute-done((bf16[256,512]{1,0:T(8,128)(2,1)S(1)}, bf16[256,512]{1,0:T(8,128)(2,1)S(1)}, u32[]{:S(2)}, u32[]{:S(2)}) %collective-permute-start.8) | collective-permute-done | bytes 262176 | tf_op jit(solution)/shard_map/ppermute | solution.py:23
  88.8 2.8 %collective-permute-done.9.from_next_ref = bf16[256,512]{1,0:T(8,128)(2,1)S(1)} collective-permute-done((bf16[256,512]{1,0:T(8,128)(2,1)S(1)}, bf16[256,512]{1,0:T(8,128)(2,1)S(1)}, u32[]{:S(2)}, u32[]{:S(2)}) %collective-permute-start.9) | collective-permute-done | bytes 262176 | tf_op jit(solution)/shard_map/ppermute | solution.py:23
  91.6 1.6 %node_part.3 = bf16[256,512]{1,0:T(8,128)(2,1)} custom-call(bf16[256,512]{1,0:T(8,128)(2,1)S(1)} %node_part.2.nodes_ref.own_ref, f32[256,512]{1,0:T(8,128)S(1)} %get-tuple-element.18.kept_ref, bf16[256,512]{1,0:T(8,128)(2,1)S(1)} %collective-permute-done.8.from_prev_ref, bf16[256,512]{1,0:T(8,128)(2,1)S(1)} %collective-permute-done.9.from_next_ref, ...), custom_call_target="tpu_custom_call" | custom-call | flops 402653184 | bytes 1572864 | tf_op jit(solution)/shard_map/node_part/pallas_call | solution.py:420
  (39 shorter events, 1.0 us)
Async XLA Ops:
  1.7 14.5 %collective-permute-start.1 = (bf16[256,512]{1,0:T(8,128)(2,1)}, bf16[256,512]{1,0:T(8,128)(2,1)S(1)}, u32[]{:S(2)}, u32[]{:S(2)}) collective-permute-start(bf16[256,512]{1,0:T(8,128)(2,1)} %nodes_ref.3), channel_id=1, source_target_pairs={{1,0},{2,1},{3,2},{0,3},{5,4},{6,5},{7,6},{4,7},{9,8},{10,9},{11,1... | collective-permute-start | bytes 786440 | tf_op jit(solution)/shard_map/ppermute | solution.py:23
  6.9 10.3 %collective-permute-start = (bf16[256,512]{1,0:T(8,128)(2,1)}, bf16[256,512]{1,0:T(8,128)(2,1)}, u32[]{:S(2)}, u32[]{:S(2)}) collective-permute-start(bf16[256,512]{1,0:T(8,128)(2,1)} %nodes_ref.3), channel_id=1, source_target_pairs={{3,0},{0,1},{1,2},{2,3},{7,4},{4,5},{5,6},{6,7},{11,8},{8,9},{9,10... | collective-permute-start | bytes 786440 | tf_op jit(solution)/shard_map/ppermute | solution.py:23
  7.7 8.5 %copy-start.15 = (s32[2,1]{0,1:T(1,128)S(1)}, s32[2,1]{0,1:T(1,128)}, u32[]{:S(2)}) copy-start(s32[2,1]{0,1:T(1,128)} %param.21) | copy-start | bytes 28
  7.7 9.4 %copy-start = (bf16[2,3,512,512]{3,2,1,0:T(8,128)(2,1)S(1)}, bf16[2,3,512,512]{3,2,1,0:T(8,128)(2,1)}, u32[]{:S(2)}) copy-start(bf16[2,3,512,512]{3,2,1,0:T(8,128)(2,1)} %wr_ref.5) | copy-start | bytes 9437188
  7.7 9.4 %copy-start.5 = (s32[2048]{0:T(1024)S(1)}, s32[2048]{0:T(1024)}, u32[]{:S(2)}) copy-start(s32[2048]{0:T(1024)} %param.18) | copy-start | bytes 24580
  7.7 9.4 %copy-start.6 = (s32[2048]{0:T(1024)S(1)}, s32[2048]{0:T(1024)}, u32[]{:S(2)}) copy-start(s32[2048]{0:T(1024)} %param.19) | copy-start | bytes 24580
  7.7 9.4 %copy-start.13 = (f32[2,512]{1,0:T(2,128)S(1)}, f32[2,512]{1,0:T(2,128)}, u32[]{:S(2)}) copy-start(f32[2,512]{1,0:T(2,128)} %gain_ref.6) | copy-start | bytes 12292
  7.7 9.4 %copy-start.14 = (f32[2,512]{1,0:T(2,128)S(1)}, f32[2,512]{1,0:T(2,128)}, u32[]{:S(2)}) copy-start(f32[2,512]{1,0:T(2,128)} %shift_ref.6) | copy-start | bytes 12292
  7.7 8.5 %collective-permute-start.2 = (bf16[32,512]{1,0:T(8,128)(2,1)S(1)}, bf16[32,512]{1,0:T(8,128)(2,1)S(1)}, u32[]{:S(2)}, u32[]{:S(2)}) collective-permute-start(bf16[32,512]{1,0:T(8,128)(2,1)S(1)} %slice.6), channel_id=1, source_target_pairs={{2,0},{3,1},{0,2},{1,3},{6,4},{7,5},{4,6},{5,7},{10,8},{11,9},{8,1... | collective-permute-start | bytes 98312 | tf_op jit(solution)/shard_map/ppermute | solution.py:23
  17.2 2.2 %copy-start.2 = (f32[2048,512]{1,0:T(8,128)S(1)}, f32[2048,512]{1,0:T(8,128)}, u32[]{:S(2)}) copy-start(f32[2048,512]{1,0:T(8,128)} %first_part.3.pre_ref) | copy-start | bytes 12582916
  22.2 15.0 %copy-start.7 = (f32[2,512]{1,0:T(2,128)S(1)}, f32[2,512]{1,0:T(2,128)}, u32[]{:S(2)}) copy-start(f32[2,512]{1,0:T(2,128)} %bias_ref.7) | copy-start | bytes 12292
  32.5 9.1 %collective-permute-start.3 = (bf16[256,512]{1,0:T(8,128)(2,1)S(1)}, bf16[256,512]{1,0:T(8,128)(2,1)S(1)}, u32[]{:S(2)}, u32[]{:S(2)}) collective-permute-start(bf16[256,512]{1,0:T(8,128)(2,1)S(1)} %get-tuple-element.15), channel_id=1, source_target_pairs={{3,0},{0,1},{1,2},{2,3},{7,4},{4,5},{5,6},{6,7},{11,8},{8,9},{9,10... | collective-permute-start | bytes 786440 | tf_op jit(solution)/shard_map/ppermute | solution.py:23
  35.1 14.7 %collective-permute-start.4 = (bf16[256,512]{1,0:T(8,128)(2,1)S(1)}, bf16[256,512]{1,0:T(8,128)(2,1)S(1)}, u32[]{:S(2)}, u32[]{:S(2)}) collective-permute-start(bf16[256,512]{1,0:T(8,128)(2,1)S(1)} %get-tuple-element.16), channel_id=1, source_target_pairs={{1,0},{2,1},{3,2},{0,3},{5,4},{6,5},{7,6},{4,7},{9,8},{10,9},{11,1... | collective-permute-start | bytes 786440 | tf_op jit(solution)/shard_map/ppermute | solution.py:23
  37.2 12.5 %copy-start.1 = (bf16[2,2,512,512]{3,2,1,0:T(8,128)(2,1)S(1)}, bf16[2,2,512,512]{3,2,1,0:T(8,128)(2,1)}, u32[]{:S(2)}) copy-start(bf16[2,2,512,512]{3,2,1,0:T(8,128)(2,1)} %wa_ref.3) | copy-start | bytes 6291460
  37.2 12.5 %copy-start.4 = (bf16[2,512,512]{2,1,0:T(8,128)(2,1)S(1)}, bf16[2,512,512]{2,1,0:T(8,128)(2,1)}, u32[]{:S(2)}) copy-start(bf16[2,512,512]{2,1,0:T(8,128)(2,1)} %wo_ref.7) | copy-start | bytes 3145732
  37.2 12.5 %copy-start.8 = (f32[2,512]{1,0:T(2,128)S(1)}, f32[2,512]{1,0:T(2,128)}, u32[]{:S(2)}) copy-start(f32[2,512]{1,0:T(2,128)} %bias_ref.9) | copy-start | bytes 12292
  37.2 12.5 %copy-start.9 = (f32[2,512]{1,0:T(2,128)S(1)}, f32[2,512]{1,0:T(2,128)}, u32[]{:S(2)}) copy-start(f32[2,512]{1,0:T(2,128)} %gain_ref.7) | copy-start | bytes 12292
  37.2 12.5 %copy-start.10 = (f32[2,512]{1,0:T(2,128)S(1)}, f32[2,512]{1,0:T(2,128)}, u32[]{:S(2)}) copy-start(f32[2,512]{1,0:T(2,128)} %shift_ref.7) | copy-start | bytes 12292
  51.6 15.5 %collective-permute-start.6 = (bf16[256,512]{1,0:T(8,128)(2,1)S(1)}, bf16[256,512]{1,0:T(8,128)(2,1)S(1)}, u32[]{:S(2)}, u32[]{:S(2)}) collective-permute-start(bf16[256,512]{1,0:T(8,128)(2,1)S(1)} %node_part.2.nodes_ref.own_ref), channel_id=1, source_target_pairs={{1,0},{2,1},{3,2},{0,3},{5,4},{6,5},{7,6},{4,7},{9,8},{10,9},{11,1... | collective-permute-start | bytes 786440 | tf_op jit(solution)/shard_map/ppermute | solution.py:23
  52.1 15.1 %collective-permute-start.5 = (bf16[256,512]{1,0:T(8,128)(2,1)S(1)}, bf16[256,512]{1,0:T(8,128)(2,1)S(1)}, u32[]{:S(2)}, u32[]{:S(2)}) collective-permute-start(bf16[256,512]{1,0:T(8,128)(2,1)S(1)} %node_part.2.nodes_ref.own_ref), channel_id=1, source_target_pairs={{3,0},{0,1},{1,2},{2,3},{7,4},{4,5},{5,6},{6,7},{11,8},{8,9},{9,10... | collective-permute-start | bytes 786440 | tf_op jit(solution)/shard_map/ppermute | solution.py:23
  53.7 13.4 %copy-start.12 = (bf16[2,512,512]{2,1,0:T(8,128)(2,1)S(1)}, bf16[2,512,512]{2,1,0:T(8,128)(2,1)}, u32[]{:S(2)}) copy-start(bf16[2,512,512]{2,1,0:T(8,128)(2,1)} %wo_ref.6) | copy-start | bytes 3145732
  53.7 13.4 %collective-permute-start.7 = (bf16[32,512]{1,0:T(8,128)(2,1)S(1)}, bf16[32,512]{1,0:T(8,128)(2,1)S(1)}, u32[]{:S(2)}, u32[]{:S(2)}) collective-permute-start(bf16[32,512]{1,0:T(8,128)(2,1)S(1)} %slice.8), channel_id=1, source_target_pairs={{2,0},{3,1},{0,2},{1,3},{6,4},{7,5},{4,6},{5,7},{10,8},{11,9},{8,1... | collective-permute-start | bytes 98312 | tf_op jit(solution)/shard_map/ppermute | solution.py:23
  77.8 11.0 %collective-permute-start.8 = (bf16[256,512]{1,0:T(8,128)(2,1)S(1)}, bf16[256,512]{1,0:T(8,128)(2,1)S(1)}, u32[]{:S(2)}, u32[]{:S(2)}) collective-permute-start(bf16[256,512]{1,0:T(8,128)(2,1)S(1)} %get-tuple-element.19), channel_id=1, source_target_pairs={{3,0},{0,1},{1,2},{2,3},{7,4},{4,5},{5,6},{6,7},{11,8},{8,9},{9,10... | collective-permute-start | bytes 786440 | tf_op jit(solution)/shard_map/ppermute | solution.py:23
  78.0 13.6 %collective-permute-start.9 = (bf16[256,512]{1,0:T(8,128)(2,1)S(1)}, bf16[256,512]{1,0:T(8,128)(2,1)S(1)}, u32[]{:S(2)}, u32[]{:S(2)}) collective-permute-start(bf16[256,512]{1,0:T(8,128)(2,1)S(1)} %get-tuple-element.20), channel_id=1, source_target_pairs={{1,0},{2,1},{3,2},{0,3},{5,4},{6,5},{7,6},{4,7},{9,8},{10,9},{11,1... | collective-permute-start | bytes 786440 | tf_op jit(solution)/shard_map/ppermute | solution.py:23
  (2 other events, 2.8 us)

commit v3 on v2

--- a/solution.py
+++ b/solution.py
@@ -38,31 +38,34 @@
     return center * lax.rsqrt(spread + epsilon) * gain + shift
 
 
-def columns_of(codes_ref, first, count):
-    rows = [
-        jnp.broadcast_to(codes_ref[pl.ds(first + i, 1), :], (LANES, LANES)).T
-        for i in range(count)
-    ]
-    return jnp.concatenate(rows, axis=0)
-
-
-def one_hot(codes, start, width):
-    lane = lax.broadcasted_iota(jnp.int32, codes.shape, 1)
-    offset = codes - lane
-    parts = [
-        jnp.where(offset == start + t * LANES, 1.0, 0.0).astype(BF16)
-        for t in range(width // LANES)
-    ]
-    return jnp.concatenate(parts, axis=1)
-
-
-def one_hot_rows(codes_ref, first, count, width):
-    parts = []
+def selector(codes_ref, first, count, starts):
+    groups = []
     for i in range(count):
         row = codes_ref[pl.ds(first + i, 1), :]
-        sub = lax.broadcasted_iota(jnp.int32, (width, LANES), 0)
-        parts.append(jnp.where(sub == row, 1.0, 0.0).astype(BF16))
-    return jnp.concatenate(parts, axis=1)
+        parts = []
+        for start, width in starts:
+            near = jnp.clip(row - start, -1, width).astype(F32)
+            near = jnp.broadcast_to(near, (LANES, LANES)).T.astype(BF16)
+            for t in range(width // LANES):
+                lane = lax.broadcasted_iota(jnp.int32, (LANES, LANES), 1) + t * LANES
+                parts.append(jnp.where(near == lane.astype(BF16), BF16(1), BF16(0)))
+        groups.append(jnp.concatenate(parts, axis=1))
+    return jnp.concatenate(groups, axis=0)
+
+
+def selector_rows(codes_ref, first, count, width):
+    tile = 2 * LANES
+    groups = []
+    for i in range(count):
+        row = codes_ref[pl.ds(first + i, 1), :]
+        parts = []
+        for start in range(0, width, tile):
+            near = jnp.clip(row - start, -1, tile).astype(F32)
+            near = jnp.broadcast_to(near, (tile, LANES)).astype(BF16)
+            sub = lax.broadcasted_iota(jnp.int32, (tile, LANES), 0).astype(BF16)
+            parts.append(jnp.where(near == sub, BF16(1), BF16(0)))
+        groups.append(jnp.concatenate(parts, axis=0))
+    return jnp.concatenate(groups, axis=1)
 
 
 def linear_kernel(layer, edges_ref, weight_ref, bias_ref, out_ref):
@@ -76,76 +79,54 @@
 
 
 def own_picks(send_ref, recv_ref, first, count, rows):
+    spans = tuple((rows + at, 2 * LANES) for at in range(0, rows, 2 * LANES))
     return jnp.concatenate(
-        [
-            one_hot(columns_of(send_ref, first, count), rows, rows),
-            one_hot(columns_of(recv_ref, first, count), rows, rows),
-        ],
+        [selector(send_ref, first, count, spans), selector(recv_ref, first, count, spans)],
         axis=1,
     )
 
 
-def own_kernel(send_ref, recv_ref, pre_ref, nodes_ref, ws_ref, wr_ref, out_ref, table_ref):
-    step = pl.program_id(0)
+def own_sum(step, send_ref, recv_ref, nodes_ref, ws_ref, wr_ref, table_ref, edges):
     rows = nodes_ref.shape[0]
 
     @pl.when(step == 0)
     def _():
         own_table(nodes_ref[...], ws_ref, wr_ref, table_ref)
 
-    count = out_ref.shape[0] // LANES
-    picks = own_picks(send_ref, recv_ref, step * count, count, rows)
-    out_ref[...] = pre_ref[...] + dot(picks, table_ref[...])
-
-
-def first_kernel(
-    parity,
-    layer,
-    steps,
-    send_ref,
-    recv_ref,
-    nodes_ref,
-    bias_ref,
-    edges_ref,
-    weights_ref,
-    *refs,
-):
-    out_ref, table_ref, weight_buf, edges_buf, out_buf, weight_sem, in_sem, out_sem = refs[-8:]
-    rows = nodes_ref.shape[0]
-    block = edges_buf.shape[0] // steps
-    count = block // LANES
-
-    def span(i):
-        return pl.ds(i * block, block)
-
-    def fetch(i):
-        return pltpu.make_async_copy(edges_ref.at[span(i)], edges_buf.at[span(i)], in_sem.at[i])
-
-    def weight(i):
-        return pltpu.make_async_copy(weights_ref.at[layer, i], weight_buf.at[i], weight_sem.at[i])
-
-    def put(i):
-        return pltpu.make_async_copy(out_buf.at[span(i)], out_ref.at[span(i)], out_sem.at[i])
-
-    @pl.when(lax.axis_index("region") % 2 == parity)
+    count = edges // LANES
+    return dot(own_picks(send_ref, recv_ref, step * count, count, rows), table_ref[...])
+
+
+def own_kernel(send_ref, recv_ref, nodes_ref, ws_ref, wr_ref, pre_ref, out_ref, table_ref):
+    gathered = own_sum(
+        pl.program_id(0), send_ref, recv_ref, nodes_ref, ws_ref, wr_ref, table_ref, out_ref.shape[0]
+    )
+    out_ref[...] = pre_ref[...] + gathered
+
+
+def is_odd():
+    return lax.axis_index("region") % 2 == 1
+
+
+def first_kernel(late, layer, send_ref, recv_ref, nodes_ref, ws_ref, wr_ref, *refs):
+    edges_ref, first_ref, bias_ref = refs[:3]
+    out_ref, table_ref = refs[-2:]
+    step = pl.program_id(0)
+    odd = is_odd()
+
+    @pl.when(jnp.logical_not(odd) if late else odd)
     def _():
-        for i in (1, 2, 0):
-            weight(i).start()
-        for i in range(steps):
-            fetch(i).start()
-        weight(1).wait()
-        table_ref[:rows, :] = dot(nodes_ref[...], weight_buf[1]).astype(BF16)
-        weight(2).wait()
-        table_ref[rows:, :] = dot(nodes_ref[...], weight_buf[2]).astype(BF16)
-        weight(0).wait()
-        for i in range(steps):
-            fetch(i).wait()
-            picks = own_picks(send_ref, recv_ref, i * count, count, rows)
-            total = dot(picks, table_ref[...]) + dot(edges_buf[span(i), :], weight_buf[0])
-            out_buf[span(i), :] = total + bias_ref[layer : layer + 1, :]
-            put(i).start()
-        for i in range(steps):
-            put(i).wait()
+        gathered = own_sum(
+            step, send_ref, recv_ref, nodes_ref, ws_ref, wr_ref, table_ref, out_ref.shape[0]
+        )
+        ahead = dot(edges_ref[...], first_ref[0, 0]) + bias_ref[layer : layer + 1, :]
+        out_ref[...] = ahead + gathered
+
+    if late:
+
+        @pl.when(odd)
+        def _():
+            out_ref[...] = refs[3][...]
 
 
 def edge_kernel(
@@ -186,7 +167,7 @@
         table_ref[1 * rows : 2 * rows, :] = dot(after, weight_s).astype(BF16)
         table_ref[2 * rows : 3 * rows, :] = dot(before, weight_r).astype(BF16)
         table_ref[3 * rows : 4 * rows, :] = dot(after, weight_r).astype(BF16)
-        away = owner_ref[layer, 0] - lax.axis_index("patch")
+        away = owner_ref[layer] - lax.axis_index("patch")
         away = jnp.where(away < 0, away + size, away)
         hub = own_ref[:HUB, :]
         if size > 3:
@@ -201,15 +182,15 @@
 
     block = out_ref.shape[0]
     count = block // LANES
-    send = columns_of(send_ref, step * count, count)
-    recv = columns_of(recv_ref, step * count, count)
+    spans = [
+        tuple((start + at, 2 * LANES) for at in range(0, rows, 2 * LANES)) for start in (0, 2 * rows)
+    ]
+    hubs = ((3 * rows, LANES),)
     picks = jnp.concatenate(
         [
-            one_hot(send, 0, rows),
-            one_hot(send, 2 * rows, rows),
-            one_hot(recv, 0, rows),
-            one_hot(recv, 2 * rows, rows),
-            one_hot(send, 3 * rows, LANES),
+            selector(send_ref, step * count, count, spans[0] + spans[1]),
+            selector(recv_ref, step * count, count, spans[0] + spans[1]),
+            selector(send_ref, step * count, count, hubs),
         ],
         axis=1,
     )
@@ -219,7 +200,7 @@
     spot = step * block + lax.broadcasted_iota(jnp.int32, (block, 1), 0)
     updated = jnp.where(spot < valid_ref[0], edges_ref[...].astype(F32) + normed, 0.0).astype(BF16)
     out_ref[...] = updated
-    total_ref[...] += dot(one_hot_rows(recv_ref, step * count, count, 3 * rows), updated)
+    total_ref[...] += dot(selector_rows(recv_ref, step * count, count, 3 * rows), updated)
 
     @pl.when(step == pl.num_programs(0) - 1)
     def _():
@@ -297,32 +278,33 @@
     recv = receivers.reshape(slots // LANES, LANES)
     by_block = pl.BlockSpec((block, width), lambda i: (i, 0))
     square = 2 * slots * width * width
-    def start_edges(parity, held):
-        anywhere = pl.BlockSpec(memory_space=pltpu.HBM)
-        given = () if held is None else (held,)
+    def start_edges(early):
+        late = early is not None
+
+        def active(i):
+            return jnp.where(is_odd(), 0, i) if late else jnp.where(is_odd(), i, 0)
+
+        def passive(i):
+            return jnp.where(is_odd(), i, 0)
+
+        given = (early,) if late else ()
         return pl.pallas_call(
-            functools.partial(first_kernel, parity, 0, steps),
+            functools.partial(first_kernel, late, 0),
             out_shape=jax.ShapeDtypeStruct((slots, width), F32),
+            grid=(steps,),
             in_specs=[whole(send.shape), whole(recv.shape), whole(nodes.shape)]
-            + [whole(edge_bias.shape), anywhere, anywhere]
-            + [anywhere] * len(given),
-            out_specs=anywhere,
-            grid=(1,),
-            input_output_aliases={6: 0} if given else {},
-            scratch_shapes=[
-                pltpu.VMEM((2 * rows, width), BF16),
-                pltpu.VMEM((3, width, width), BF16),
-                pltpu.VMEM((slots, width), BF16),
-                pltpu.VMEM((slots, width), F32),
-                pltpu.SemaphoreType.DMA((3,)),
-                pltpu.SemaphoreType.DMA((steps,)),
-                pltpu.SemaphoreType.DMA((steps,)),
-            ],
+            + [picked(edge_in.shape, (0, 1)), picked(edge_in.shape, (0, 2))]
+            + [pl.BlockSpec((block, width), lambda i: (active(i), 0))]
+            + [picked(edge_in.shape, (0, 0)), whole(edge_bias.shape)]
+            + [pl.BlockSpec((block, width), lambda i: (passive(i), 0))] * len(given),
+            out_specs=pl.BlockSpec((block, width), lambda i: (i if late else active(i), 0)),
+            scratch_shapes=[pltpu.VMEM((2 * rows, width), BF16)],
+            compiler_params=pltpu.CompilerParams(vmem_limit_bytes=GRANT if late else None),
             cost_estimate=cost(2 * square, 6 * slots * width),
-            name="first_part",
-        )(send, recv, nodes, edge_bias, edges, edge_in, *given)
-
-    early = start_edges(1, None)
+            name="late_part" if late else "early_part",
+        )(send, recv, nodes, edge_in, edge_in, edges, edge_in, edge_bias, *given)
+
+    early = start_edges(None)
     nodes, early = lax.optimization_barrier((nodes, early))
     for layer in range(LAYERS):
         from_prev = from_behind(nodes, "patch", 1)
@@ -333,20 +315,20 @@
         ws = picked(edge_in.shape, (layer, 1))
         wr = picked(edge_in.shape, (layer, 2))
         if layer == 0:
-            pre = start_edges(0, early)
+            pre = start_edges(early)
         else:
             pre = pl.pallas_call(
                 own_kernel,
                 out_shape=jax.ShapeDtypeStruct((slots, width), F32),
                 grid=(steps,),
-                in_specs=[whole(send.shape), whole(recv.shape), by_block]
-                + [whole(nodes.shape), ws, wr],
+                in_specs=[whole(send.shape), whole(recv.shape), whole(nodes.shape), ws, wr]
+                + [by_block],
                 out_specs=by_block,
                 scratch_shapes=[pltpu.VMEM((2 * rows, width), BF16)],
                 compiler_params=pltpu.CompilerParams(vmem_limit_bytes=GRANT),
                 cost_estimate=cost(square, 8 * slots * width),
                 name="own_part",
-            )(send, recv, pre, nodes, edge_in, edge_in)
+            )(send, recv, nodes, edge_in, edge_in, pre)
         edges, to_prev, kept, to_next = pl.pallas_call(
             functools.partial(edge_kernel, rows, layer, size),
             out_shape=(
@@ -383,7 +365,7 @@
             name="edge_part",
         )(
             valid_counts,
-            hub_owner,
+            hub_owner.reshape(-1),
             send,
             recv,
             edges,

time: 93.6 us -> 88.7 us (0.948)
  Pallas kernels: 36.5 us -> 33.9 us
  local copies, waits for them, and re-layouts: 5.98 us -> 3.83 us
    unnamed x33 -> x32, local copies, waits for them, and re-layouts: 5.15 us -> 3.83 us
    pallas_call x2, Pallas kernels: 7.8 us -> 6.48 us  [start_edges(): pl.pallas_call(functools.partial(first_kernel, late, 0), out_shape=jax.Sh...]
    pallas_call x2, Pallas kernels: 3.52 us -> 2.57 us  [local(): pl.pallas_call(functools.partial(node_kernel, layer), out_shape=jax.Shape...]
  transfers between devices with their start and end apart: 10 -> 10, of which waited for: 6 -> 7; matrix products, arithmetic and copies ran while one was open for 1% -> 0% of each run, Pallas kernels for 12% -> 9%
where the time goes in v3:
time: 88.7 us; the launch traced here: 88.4 us
  Pallas kernels  33.9 us (38%)
  waiting for transfers between devices  33 us (37%)
  starting transfers between devices  16.3 us (18%)
  local copies, waits for them, and re-layouts  3.83 us (4%)
  between operations  1.43 us (2%)
    ppermute x10, waiting for transfers between devices, from_behind(): lax.ppermute(block, axis, [((i - distance) % size, i) for i in range(size)])  33 us
    pallas_call x2, Pallas kernels, local(): pl.pallas_call(functools.partial(edge_kernel, rows, layer, size), out_sha...  20.6 us
    ppermute x10, starting transfers between devices, from_behind(): lax.ppermute(block, axis, [((i - distance) % size, i) for i in range(size)])  16.3 us
    pallas_call x2, Pallas kernels, start_edges(): pl.pallas_call(functools.partial(first_kernel, late, 0), out_shape=jax.Sh...  6.48 us
    unnamed x32, local copies, waits for them, and re-layouts  3.83 us
    pallas_call x2, Pallas kernels, local(): pl.pallas_call(functools.partial(node_kernel, layer), out_shape=jax.Shape...  2.57 us
    pallas_call x1, Pallas kernels, local(): pl.pallas_call(own_kernel, out_shape=jax.ShapeDtypeStruct((slots, width),...  2.47 us
    pallas_call x1, Pallas kernels, local(): pl.pallas_call(functools.partial(linear_kernel, layer + 1), out_shape=jax...  1.78 us
  transfers between devices with their start and end apart: 10, of which 7 were waited for; matrix products, arithmetic and copies ran while one was open for 0% of the time, Pallas kernels for 9%

profile of v3, /device:TPU:0, one launch (start us, length us, event | category | flops | bytes accessed | tf_op | source)
XLA Modules:
  0.0 88.4 jit_solution(6317823353712959243)
XLA Ops:
  0.7 2.8 %early_part.1.refs_3_ = f32[2048,512]{1,0:T(8,128)} custom-call(s32[16,128]{1,0:T(8,128)} %bitcast.3, s32[16,128]{1,0:T(8,128)} %bitcast.8, bf16[256,512]{1,0:T(8,128)(2,1)} %nodes_ref.3, bf16[2,3,512,512]{3,2,1,0:T(8,128)(2,1)} %wr_ref.9, bf16[2,3,512,512]{3,2,1,0:T(8,128)(2,1)} %wr_ref.9, bf16[2048,512]{1,0:T(8,128)(2,1)} %edges_ref.1, ...), custom_call_target="tpu_custom_call" | custom-call | flops 2147483648 | bytes 6291456 | tf_op jit(solution)/shard_map/early_part/pallas_call | solution.py:291
  3.5 5.1 %collective-permute-start.1 = (bf16[256,512]{1,0:T(8,128)(2,1)S(1)}, bf16[256,512]{1,0:T(8,128)(2,1)S(1)}, u32[]{:S(2)}, u32[]{:S(2)}) collective-permute-start(bf16[256,512]{1,0:T(8,128)(2,1)S(1)} %copy-done.5), channel_id=1, source_target_pairs={{1,0},{2,1},{3,2},{0,3},{5,4},{6,5},{7,6},{4,7},{9,8},{10,9},{11,1... | collective-permute-start | bytes 786440 | tf_op jit(solution)/shard_map/ppermute | solution.py:23
  8.6 1.0 %collective-permute-start.2 = (bf16[32,512]{1,0:T(8,128)(2,1)S(1)}, bf16[32,512]{1,0:T(8,128)(2,1)S(1)}, u32[]{:S(2)}, u32[]{:S(2)}) collective-permute-start(bf16[32,512]{1,0:T(8,128)(2,1)S(1)} %slice.6), channel_id=1, source_target_pairs={{2,0},{3,1},{0,2},{1,3},{6,4},{7,5},{4,6},{5,7},{10,8},{11,9},{8,1... | collective-permute-start | bytes 98312 | tf_op jit(solution)/shard_map/ppermute | solution.py:23
  9.6 2.2 %copy-done.2 = f32[2048,512]{1,0:T(8,128)S(1)} copy-done((f32[2048,512]{1,0:T(8,128)S(1)}, f32[2048,512]{1,0:T(8,128)}, u32[]{:S(2)}) %copy-start.2) | copy-done | bytes 4194328
  11.8 1.6 %copy-done.3 = bf16[2048,512]{1,0:T(8,128)(2,1)S(1)} copy-done((bf16[2048,512]{1,0:T(8,128)(2,1)S(1)}, bf16[2048,512]{1,0:T(8,128)(2,1)}, u32[]{:S(2)}) %copy-start.3) | copy-done | bytes 2097176
  13.4 3.6 %late_part.1.pre_ref = f32[2048,512]{1,0:T(8,128)S(1)} custom-call(s32[16,128]{1,0:T(8,128)S(1)} %bitcast.4, s32[16,128]{1,0:T(8,128)S(1)} %bitcast.9, bf16[256,512]{1,0:T(8,128)(2,1)S(1)} %copy-done.5, bf16[2,3,512,512]{3,2,1,0:T(8,128)(2,1)S(1)} %copy-done, bf16[2,3,512,512]{3,2,1,0:T(8,128)(2,1)S(1)} %copy-done, bf16[2048,512]{1,0:T(8,128)(2,1)S(1)} %copy-done.3, ...), custom_call_target="tpu_custom_call" | custom-call | flops 2147483648 | bytes 6291456 | tf_op jit(solution)/shard_map/late_part/pallas_call | solution.py:291
  17.7 0.9 collective-permute-done.2.far_ref
  18.6 1.0 %collective-permute-done.prev_ref = bf16[256,512]{1,0:T(8,128)(2,1)S(1)} collective-permute-done((bf16[256,512]{1,0:T(8,128)(2,1)S(1)}, bf16[256,512]{1,0:T(8,128)(2,1)S(1)}, u32[]{:S(2)}, u32[]{:S(2)}) %collective-permute-start) | collective-permute-done | bytes 262176 | tf_op jit(solution)/shard_map/ppermute | solution.py:23
  19.6 9.9 %edge_part.2 = (bf16[2048,512]{1,0:T(8,128)(2,1)S(1)}, bf16[256,512]{1,0:T(8,128)(2,1)S(1)}, f32[256,512]{1,0:T(8,128)S(1)}, bf16[256,512]{1,0:T(8,128)(2,1)S(1)}) custom-call(s32[1]{0:T(128)S(6)} %copy.18.valid_ref, s32[2]{0:T(128)S(1)} %bitcast.13, s32[16,128]{1,0:T(8,128)S(1)} %bitcast.5, s32[16,128]{1,0:T(8,128)S(1)} %bitcast.10, ...), custom_call_target="tpu_custom_call" | custom-call | flops 6442450944 | bytes 8388608 | tf_op jit(solution)/shard_map/edge_part/pallas_call | solution.py:332
  29.5 1.6 %collective-permute-start.3 = (bf16[256,512]{1,0:T(8,128)(2,1)S(1)}, bf16[256,512]{1,0:T(8,128)(2,1)S(1)}, u32[]{:S(2)}, u32[]{:S(2)}) collective-permute-start(bf16[256,512]{1,0:T(8,128)(2,1)S(1)} %get-tuple-element.15), channel_id=1, source_target_pairs={{3,0},{0,1},{1,2},{2,3},{7,4},{4,5},{5,6},{6,7},{11,8},{8,9},{9,10... | collective-permute-start | bytes 786440 | tf_op jit(solution)/shard_map/ppermute | solution.py:23
  31.1 2.2 %collective-permute-start.4 = (bf16[256,512]{1,0:T(8,128)(2,1)S(1)}, bf16[256,512]{1,0:T(8,128)(2,1)S(1)}, u32[]{:S(2)}, u32[]{:S(2)}) collective-permute-start(bf16[256,512]{1,0:T(8,128)(2,1)S(1)} %get-tuple-element.16), channel_id=1, source_target_pairs={{1,0},{2,1},{3,2},{0,3},{5,4},{6,5},{7,6},{4,7},{9,8},{10,9},{11,1... | collective-permute-start | bytes 786440 | tf_op jit(solution)/shard_map/ppermute | solution.py:23
  33.4 1.8 %linear_part.1.refs_0_.pre_ref = f32[2048,512]{1,0:T(8,128)S(1)} custom-call(bf16[2048,512]{1,0:T(8,128)(2,1)S(1)} %get-tuple-element.17.edges_ref, bf16[2,3,512,512]{3,2,1,0:T(8,128)(2,1)S(1)} %copy-done, f32[2,512]{1,0:T(2,128)S(1)} %copy-done.8), custom_call_target="tpu_custom_call" | custom-call | flops 1073741824 | bytes 6291456 | tf_op jit(solution)/shard_map/linear_part/pallas_call | solution.py:387
  35.2 3.7 %collective-permute-done.3.from_prev_ref = bf16[256,512]{1,0:T(8,128)(2,1)S(1)} collective-permute-done((bf16[256,512]{1,0:T(8,128)(2,1)S(1)}, bf16[256,512]{1,0:T(8,128)(2,1)S(1)}, u32[]{:S(2)}, u32[]{:S(2)}) %collective-permute-start.3) | collective-permute-done | bytes 262176 | tf_op jit(solution)/shard_map/ppermute | solution.py:23
  38.9 6.7 %collective-permute-done.4.from_next_ref = bf16[256,512]{1,0:T(8,128)(2,1)S(1)} collective-permute-done((bf16[256,512]{1,0:T(8,128)(2,1)S(1)}, bf16[256,512]{1,0:T(8,128)(2,1)S(1)}, u32[]{:S(2)}, u32[]{:S(2)}) %collective-permute-start.4) | collective-permute-done | bytes 262176 | tf_op jit(solution)/shard_map/ppermute | solution.py:23
  45.6 0.9 %node_part.2.nodes_ref.own_ref = bf16[256,512]{1,0:T(8,128)(2,1)S(1)} custom-call(bf16[256,512]{1,0:T(8,128)(2,1)S(1)} %copy-done.5, f32[256,512]{1,0:T(8,128)S(1)} %get-tuple-element.14.kept_ref, bf16[256,512]{1,0:T(8,128)(2,1)S(1)} %collective-permute-done.3.from_prev_ref, bf16[256,512]{1,0:T(8,128)(2,1)S(1)} %collective-permute-done.4.from_next_ref, ...), custom_call_target="tpu_custom_call" | custom-call | flops 402653184 | bytes 1572864 | tf_op jit(solution)/shard_map/node_part/pallas_call | solution.py:402
  46.6 0.7 collective-permute-start.6
  47.3 1.4 %collective-permute-start.5 = (bf16[256,512]{1,0:T(8,128)(2,1)S(1)}, bf16[256,512]{1,0:T(8,128)(2,1)S(1)}, u32[]{:S(2)}, u32[]{:S(2)}) collective-permute-start(bf16[256,512]{1,0:T(8,128)(2,1)S(1)} %node_part.2.nodes_ref.own_ref), channel_id=1, source_target_pairs={{3,0},{0,1},{1,2},{2,3},{7,4},{4,5},{5,6},{6,7},{11,8},{8,9},{9,10... | collective-permute-start | bytes 786440 | tf_op jit(solution)/shard_map/ppermute | solution.py:23
  49.1 2.5 %own_part.1.pre_ref = f32[2048,512]{1,0:T(8,128)S(1)} custom-call(s32[16,128]{1,0:T(8,128)S(1)} %bitcast.6, s32[16,128]{1,0:T(8,128)S(1)} %bitcast.11, bf16[256,512]{1,0:T(8,128)(2,1)S(1)} %node_part.2.nodes_ref.own_ref, bf16[2,3,512,512]{3,2,1,0:T(8,128)(2,1)S(1)} %copy-done, bf16[2,3,512,512]{3,2,1,0:T(8,128)(2,1)S(1)} %copy-done, ...), custom_call_target="tpu_custom_call" | custom-call | flops 1073741824 | bytes 8388608 | tf_op jit(solution)/shard_map/own_part/pallas_call | solution.py:320
  51.6 10.8 %collective-permute-done.7.far_ref = bf16[32,512]{1,0:T(8,128)(2,1)S(1)} collective-permute-done((bf16[32,512]{1,0:T(8,128)(2,1)S(1)}, bf16[32,512]{1,0:T(8,128)(2,1)S(1)}, u32[]{:S(2)}, u32[]{:S(2)}) %collective-permute-start.7) | collective-permute-done | bytes 32800 | tf_op jit(solution)/shard_map/ppermute | solution.py:23
  62.4 10.7 %edge_part.3 = (bf16[2048,512]{1,0:T(8,128)(2,1)}, bf16[256,512]{1,0:T(8,128)(2,1)S(1)}, f32[256,512]{1,0:T(8,128)S(1)}, bf16[256,512]{1,0:T(8,128)(2,1)S(1)}) custom-call(s32[1]{0:T(128)S(6)} %copy.18.valid_ref, s32[2]{0:T(128)S(1)} %bitcast.14, s32[16,128]{1,0:T(8,128)S(1)} %bitcast.7, s32[16,128]{1,0:T(8,128)S(1)} %bitcast.12, ...), custom_call_target="tpu_custom_call" | custom-call | flops 6442450944 | bytes 8388608 | tf_op jit(solution)/shard_map/edge_part/pallas_call | solution.py:332
  73.3 3.6 %collective-permute-start.9 = (bf16[256,512]{1,0:T(8,128)(2,1)S(1)}, bf16[256,512]{1,0:T(8,128)(2,1)S(1)}, u32[]{:S(2)}, u32[]{:S(2)}) collective-permute-start(bf16[256,512]{1,0:T(8,128)(2,1)S(1)} %get-tuple-element.20), channel_id=1, source_target_pairs={{1,0},{2,1},{3,2},{0,3},{5,4},{6,5},{7,6},{4,7},{9,8},{10,9},{11,1... | collective-permute-start | bytes 786440 | tf_op jit(solution)/shard_map/ppermute | solution.py:23
  76.9 7.2 %collective-permute-done.8.from_prev_ref = bf16[256,512]{1,0:T(8,128)(2,1)S(1)} collective-permute-done((bf16[256,512]{1,0:T(8,128)(2,1)S(1)}, bf16[256,512]{1,0:T(8,128)(2,1)S(1)}, u32[]{:S(2)}, u32[]{:S(2)}) %collective-permute-start.8) | collective-permute-done | bytes 262176 | tf_op jit(solution)/shard_map/ppermute | solution.py:23
  84.1 2.7 %collective-permute-done.9.from_next_ref = bf16[256,512]{1,0:T(8,128)(2,1)S(1)} collective-permute-done((bf16[256,512]{1,0:T(8,128)(2,1)S(1)}, bf16[256,512]{1,0:T(8,128)(2,1)S(1)}, u32[]{:S(2)}, u32[]{:S(2)}) %collective-permute-start.9) | collective-permute-done | bytes 262176 | tf_op jit(solution)/shard_map/ppermute | solution.py:23
  86.8 1.7 %node_part.3 = bf16[256,512]{1,0:T(8,128)(2,1)} custom-call(bf16[256,512]{1,0:T(8,128)(2,1)S(1)} %node_part.2.nodes_ref.own_ref, f32[256,512]{1,0:T(8,128)S(1)} %get-tuple-element.18.kept_ref, bf16[256,512]{1,0:T(8,128)(2,1)S(1)} %collective-permute-done.8.from_prev_ref, bf16[256,512]{1,0:T(8,128)(2,1)S(1)} %collective-permute-done.9.from_next_ref, ...), custom_call_target="tpu_custom_call" | custom-call | flops 402653184 | bytes 1572864 | tf_op jit(solution)/shard_map/node_part/pallas_call | solution.py:402
  (38 shorter events, 0.7 us)
Async XLA Ops:
  0.6 2.9 %copy-start.5 = (bf16[256,512]{1,0:T(8,128)(2,1)S(1)}, bf16[256,512]{1,0:T(8,128)(2,1)}, u32[]{:S(2)}) copy-start(bf16[256,512]{1,0:T(8,128)(2,1)} %nodes_ref.3) | copy-start | bytes 786436
  0.6 9.0 %copy-start = (bf16[2,3,512,512]{3,2,1,0:T(8,128)(2,1)S(1)}, bf16[2,3,512,512]{3,2,1,0:T(8,128)(2,1)}, u32[]{:S(2)}) copy-start(bf16[2,3,512,512]{3,2,1,0:T(8,128)(2,1)} %wr_ref.9) | copy-start | bytes 9437188
  0.7 9.0 %copy-start.6 = (s32[2048]{0:T(1024)S(1)}, s32[2048]{0:T(1024)}, u32[]{:S(2)}) copy-start(s32[2048]{0:T(1024)} %param.18) | copy-start | bytes 24580
  0.7 9.0 %copy-start.7 = (s32[2048]{0:T(1024)S(1)}, s32[2048]{0:T(1024)}, u32[]{:S(2)}) copy-start(s32[2048]{0:T(1024)} %param.19) | copy-start | bytes 24580
  0.7 9.0 %copy-start.8 = (f32[2,512]{1,0:T(2,128)S(1)}, f32[2,512]{1,0:T(2,128)}, u32[]{:S(2)}) copy-start(f32[2,512]{1,0:T(2,128)} %bias_ref.3) | copy-start | bytes 12292
  3.5 15.1 %collective-permute-start.1 = (bf16[256,512]{1,0:T(8,128)(2,1)S(1)}, bf16[256,512]{1,0:T(8,128)(2,1)S(1)}, u32[]{:S(2)}, u32[]{:S(2)}) collective-permute-start(bf16[256,512]{1,0:T(8,128)(2,1)S(1)} %copy-done.5), channel_id=1, source_target_pairs={{1,0},{2,1},{3,2},{0,3},{5,4},{6,5},{7,6},{4,7},{9,8},{10,9},{11,1... | collective-permute-start | bytes 786440 | tf_op jit(solution)/shard_map/ppermute | solution.py:23
  8.6 11.0 %collective-permute-start = (bf16[256,512]{1,0:T(8,128)(2,1)S(1)}, bf16[256,512]{1,0:T(8,128)(2,1)S(1)}, u32[]{:S(2)}, u32[]{:S(2)}) collective-permute-start(bf16[256,512]{1,0:T(8,128)(2,1)S(1)} %copy-done.5), channel_id=1, source_target_pairs={{3,0},{0,1},{1,2},{2,3},{7,4},{4,5},{5,6},{6,7},{11,8},{8,9},{9,10... | collective-permute-start | bytes 786440 | tf_op jit(solution)/shard_map/ppermute | solution.py:23
  8.6 10.0 %collective-permute-start.2 = (bf16[32,512]{1,0:T(8,128)(2,1)S(1)}, bf16[32,512]{1,0:T(8,128)(2,1)S(1)}, u32[]{:S(2)}, u32[]{:S(2)}) collective-permute-start(bf16[32,512]{1,0:T(8,128)(2,1)S(1)} %slice.6), channel_id=1, source_target_pairs={{2,0},{3,1},{0,2},{1,3},{6,4},{7,5},{4,6},{5,7},{10,8},{11,9},{8,1... | collective-permute-start | bytes 98312 | tf_op jit(solution)/shard_map/ppermute | solution.py:23
  13.4 6.2 %copy-start.12 = (bf16[2,512,512]{2,1,0:T(8,128)(2,1)S(1)}, bf16[2,512,512]{2,1,0:T(8,128)(2,1)}, u32[]{:S(2)}) copy-start(bf16[2,512,512]{2,1,0:T(8,128)(2,1)} %wo_ref.6) | copy-start | bytes 3145732
  13.4 6.2 %copy-start.13 = (f32[2,512]{1,0:T(2,128)S(1)}, f32[2,512]{1,0:T(2,128)}, u32[]{:S(2)}) copy-start(f32[2,512]{1,0:T(2,128)} %gain_ref.6) | copy-start | bytes 12292
  13.4 6.2 %copy-start.14 = (f32[2,512]{1,0:T(2,128)S(1)}, f32[2,512]{1,0:T(2,128)}, u32[]{:S(2)}) copy-start(f32[2,512]{1,0:T(2,128)} %shift_ref.6) | copy-start | bytes 12292
  13.4 6.2 %copy-start.15 = (s32[2,1]{0,1:T(1,128)S(1)}, s32[2,1]{0,1:T(1,128)}, u32[]{:S(2)}) copy-start(s32[2,1]{0,1:T(1,128)} %param.21) | copy-start | bytes 28
  29.5 9.4 %collective-permute-start.3 = (bf16[256,512]{1,0:T(8,128)(2,1)S(1)}, bf16[256,512]{1,0:T(8,128)(2,1)S(1)}, u32[]{:S(2)}, u32[]{:S(2)}) collective-permute-start(bf16[256,512]{1,0:T(8,128)(2,1)S(1)} %get-tuple-element.15), channel_id=1, source_target_pairs={{3,0},{0,1},{1,2},{2,3},{7,4},{4,5},{5,6},{6,7},{11,8},{8,9},{9,10... | collective-permute-start | bytes 786440 | tf_op jit(solution)/shard_map/ppermute | solution.py:23
  31.1 14.5 %collective-permute-start.4 = (bf16[256,512]{1,0:T(8,128)(2,1)S(1)}, bf16[256,512]{1,0:T(8,128)(2,1)S(1)}, u32[]{:S(2)}, u32[]{:S(2)}) collective-permute-start(bf16[256,512]{1,0:T(8,128)(2,1)S(1)} %get-tuple-element.16), channel_id=1, source_target_pairs={{1,0},{2,1},{3,2},{0,3},{5,4},{6,5},{7,6},{4,7},{9,8},{10,9},{11,1... | collective-permute-start | bytes 786440 | tf_op jit(solution)/shard_map/ppermute | solution.py:23
  33.4 12.2 %copy-start.1 = (bf16[2,2,512,512]{3,2,1,0:T(8,128)(2,1)S(1)}, bf16[2,2,512,512]{3,2,1,0:T(8,128)(2,1)}, u32[]{:S(2)}) copy-start(bf16[2,2,512,512]{3,2,1,0:T(8,128)(2,1)} %wa_ref.3) | copy-start | bytes 6291460
  33.4 12.2 %copy-start.4 = (bf16[2,512,512]{2,1,0:T(8,128)(2,1)S(1)}, bf16[2,512,512]{2,1,0:T(8,128)(2,1)}, u32[]{:S(2)}) copy-start(bf16[2,512,512]{2,1,0:T(8,128)(2,1)} %wo_ref.7) | copy-start | bytes 3145732
  33.4 12.2 %copy-start.9 = (f32[2,512]{1,0:T(2,128)S(1)}, f32[2,512]{1,0:T(2,128)}, u32[]{:S(2)}) copy-start(f32[2,512]{1,0:T(2,128)} %bias_ref.5) | copy-start | bytes 12292
  33.4 12.2 %copy-start.10 = (f32[2,512]{1,0:T(2,128)S(1)}, f32[2,512]{1,0:T(2,128)}, u32[]{:S(2)}) copy-start(f32[2,512]{1,0:T(2,128)} %gain_ref.7) | copy-start | bytes 12292
  33.4 12.2 %copy-start.11 = (f32[2,512]{1,0:T(2,128)S(1)}, f32[2,512]{1,0:T(2,128)}, u32[]{:S(2)}) copy-start(f32[2,512]{1,0:T(2,128)} %shift_ref.7) | copy-start | bytes 12292
  46.6 15.9 %collective-permute-start.6 = (bf16[256,512]{1,0:T(8,128)(2,1)S(1)}, bf16[256,512]{1,0:T(8,128)(2,1)S(1)}, u32[]{:S(2)}, u32[]{:S(2)}) collective-permute-start(bf16[256,512]{1,0:T(8,128)(2,1)S(1)} %node_part.2.nodes_ref.own_ref), channel_id=1, source_target_pairs={{1,0},{2,1},{3,2},{0,3},{5,4},{6,5},{7,6},{4,7},{9,8},{10,9},{11,1... | collective-permute-start | bytes 786440 | tf_op jit(solution)/shard_map/ppermute | solution.py:23
  47.3 15.2 %collective-permute-start.5 = (bf16[256,512]{1,0:T(8,128)(2,1)S(1)}, bf16[256,512]{1,0:T(8,128)(2,1)S(1)}, u32[]{:S(2)}, u32[]{:S(2)}) collective-permute-start(bf16[256,512]{1,0:T(8,128)(2,1)S(1)} %node_part.2.nodes_ref.own_ref), channel_id=1, source_target_pairs={{3,0},{0,1},{1,2},{2,3},{7,4},{4,5},{5,6},{6,7},{11,8},{8,9},{9,10... | collective-permute-start | bytes 786440 | tf_op jit(solution)/shard_map/ppermute | solution.py:23
  48.6 13.8 %collective-permute-start.7 = (bf16[32,512]{1,0:T(8,128)(2,1)S(1)}, bf16[32,512]{1,0:T(8,128)(2,1)S(1)}, u32[]{:S(2)}, u32[]{:S(2)}) collective-permute-start(bf16[32,512]{1,0:T(8,128)(2,1)S(1)} %slice.8), channel_id=1, source_target_pairs={{2,0},{3,1},{0,2},{1,3},{6,4},{7,5},{4,6},{5,7},{10,8},{11,9},{8,1... | collective-permute-start | bytes 98312 | tf_op jit(solution)/shard_map/ppermute | solution.py:23
  73.1 11.0 %collective-permute-start.8 = (bf16[256,512]{1,0:T(8,128)(2,1)S(1)}, bf16[256,512]{1,0:T(8,128)(2,1)S(1)}, u32[]{:S(2)}, u32[]{:S(2)}) collective-permute-start(bf16[256,512]{1,0:T(8,128)(2,1)S(1)} %get-tuple-element.19), channel_id=1, source_target_pairs={{3,0},{0,1},{1,2},{2,3},{7,4},{4,5},{5,6},{6,7},{11,8},{8,9},{9,10... | collective-permute-start | bytes 786440 | tf_op jit(solution)/shard_map/ppermute | solution.py:23
  73.3 13.5 %collective-permute-start.9 = (bf16[256,512]{1,0:T(8,128)(2,1)S(1)}, bf16[256,512]{1,0:T(8,128)(2,1)S(1)}, u32[]{:S(2)}, u32[]{:S(2)}) collective-permute-start(bf16[256,512]{1,0:T(8,128)(2,1)S(1)} %get-tuple-element.20), channel_id=1, source_target_pairs={{1,0},{2,1},{3,2},{0,3},{5,4},{6,5},{7,6},{4,7},{9,8},{10,9},{11,1... | collective-permute-start | bytes 786440 | tf_op jit(solution)/shard_map/ppermute | solution.py:23
  (2 other events, 3.8 us)

commit v4 on v3

--- a/solution.py
+++ b/solution.py
@@ -7,6 +7,7 @@
 from jax.experimental.pallas import tpu as pltpu
 from jax.sharding import PartitionSpec as P
 
+
 HUB = 32
 LAYERS = 2
 LANES = 128
@@ -21,6 +22,15 @@
 def from_behind(block, axis, distance):
     size = lax.axis_size(axis)
     return lax.ppermute(block, axis, [((i - distance) % size, i) for i in range(size)])
+
+
+def from_behind_by_parity(block, distance, parity):
+    regions = range(parity, lax.axis_size("region"), 2)
+    size = lax.axis_size("patch")
+    route = [
+        (r * size + (i - distance) % size, r * size + i) for r in regions for i in range(size)
+    ]
+    return lax.ppermute(block, ("region", "patch"), route)
 
 
 def dot(left, right):
@@ -108,73 +118,47 @@
     return lax.axis_index("region") % 2 == 1
 
 
-def first_kernel(late, layer, send_ref, recv_ref, nodes_ref, ws_ref, wr_ref, *refs):
-    edges_ref, first_ref, bias_ref = refs[:3]
-    out_ref, table_ref = refs[-2:]
-    step = pl.program_id(0)
-    odd = is_odd()
-
-    @pl.when(jnp.logical_not(odd) if late else odd)
-    def _():
-        gathered = own_sum(
-            step, send_ref, recv_ref, nodes_ref, ws_ref, wr_ref, table_ref, out_ref.shape[0]
-        )
-        ahead = dot(edges_ref[...], first_ref[0, 0]) + bias_ref[layer : layer + 1, :]
-        out_ref[...] = ahead + gathered
-
-    if late:
-
-        @pl.when(odd)
-        def _():
-            out_ref[...] = refs[3][...]
-
-
-def edge_kernel(
-    rows,
-    layer,
-    size,
-    valid_ref,
-    owner_ref,
-    send_ref,
-    recv_ref,
-    edges_ref,
-    pre_ref,
-    own_ref,
-    prev_ref,
-    next_ref,
-    far_ref,
-    ws_ref,
-    wr_ref,
-    wo_ref,
-    gain_ref,
-    shift_ref,
-    out_ref,
-    to_prev_ref,
-    kept_ref,
-    to_next_ref,
-    table_ref,
-    total_ref,
-):
+def first_kernel(layer, send_ref, recv_ref, nodes_ref, ws_ref, wr_ref, *refs):
+    edges_ref, first_ref, bias_ref, out_ref, table_ref = refs
+    gathered = own_sum(
+        pl.program_id(0), send_ref, recv_ref, nodes_ref, ws_ref, wr_ref, table_ref, out_ref.shape[0]
+    )
+    ahead = dot(edges_ref[...], first_ref[0, 0]) + bias_ref[layer : layer + 1, :]
+    out_ref[...] = ahead + gathered
+
+
+def is_odd():
+    return lax.axis_index("region") % 2 == 1
+
+
+def edge_kernel(rows, layer, size, *refs):
+    valid_ref, owner_ref, send_ref, recv_ref, edges_ref, pre_ref, own_ref = refs[:7]
+    near = refs[7:-13]
+    far_ref, ws_ref, wr_ref, wo_ref, gain_ref, shift_ref = refs[-13:-7]
+    out_ref, to_prev_ref, kept_ref, to_next_ref = refs[-7:-3]
+    near_ref, table_ref, total_ref = refs[-3:]
     step = pl.program_id(0)
 
     @pl.when(step == 0)
     def _():
+        odd = is_odd()
+        for side in range(2):
+            block = near[side][...]
+            if len(near) > 2:
+                block = jnp.where(odd, near[side + 2][...], block)
+            near_ref[side * rows : (side + 1) * rows, :] = block
+        blocks = near_ref[...]
         weight_s = ws_ref[0, 0]
-        weight_r = wr_ref[0, 0]
-        before = prev_ref[...]
-        after = next_ref[...]
-        table_ref[0 * rows : 1 * rows, :] = dot(before, weight_s).astype(BF16)
-        table_ref[1 * rows : 2 * rows, :] = dot(after, weight_s).astype(BF16)
-        table_ref[2 * rows : 3 * rows, :] = dot(before, weight_r).astype(BF16)
-        table_ref[3 * rows : 4 * rows, :] = dot(after, weight_r).astype(BF16)
+        table_ref[: 2 * rows, :] = dot(blocks, weight_s).astype(BF16)
+        table_ref[2 * rows : 4 * rows, :] = dot(blocks, wr_ref[0, 0]).astype(BF16)
         away = owner_ref[layer] - lax.axis_index("patch")
         away = jnp.where(away < 0, away + size, away)
         hub = own_ref[:HUB, :]
         if size > 3:
             spot = jnp.clip(away - 2, 0, size - 4)
             hub = jnp.where(away > 1, far_ref[pl.ds(pl.multiple_of(spot * HUB, HUB), HUB), :], hub)
-        hub = jnp.where(away == size - 1, prev_ref[:HUB, :], hub)
-        hub = jnp.where(away == 1, next_ref[:HUB, :], hub)
+        hub = jnp.where(away == size - 1, near_ref[:HUB, :], hub)
+        hub = jnp.where(away == 1, near_ref[rows : rows + HUB, :], hub)
         hub = jnp.where(away == 0, own_ref[:HUB, :], hub)
         table_ref[4 * rows : 4 * rows + HUB, :] = dot(hub, weight_s).astype(BF16)
         table_ref[4 * rows + HUB :, :] = jnp.zeros_like(table_ref[4 * rows + HUB :, :])
@@ -278,44 +262,36 @@
     recv = receivers.reshape(slots // LANES, LANES)
     by_block = pl.BlockSpec((block, width), lambda i: (i, 0))
     square = 2 * slots * width * width
-    def start_edges(early):
-        late = early is not None
-
-        def active(i):
-            return jnp.where(is_odd(), 0, i) if late else jnp.where(is_odd(), i, 0)
-
-        def passive(i):
-            return jnp.where(is_odd(), i, 0)
-
-        given = (early,) if late else ()
+
+    def start_edges():
         return pl.pallas_call(
-            functools.partial(first_kernel, late, 0),
+            functools.partial(first_kernel, 0),
             out_shape=jax.ShapeDtypeStruct((slots, width), F32),
             grid=(steps,),
             in_specs=[whole(send.shape), whole(recv.shape), whole(nodes.shape)]
-            + [picked(edge_in.shape, (0, 1)), picked(edge_in.shape, (0, 2))]
-            + [pl.BlockSpec((block, width), lambda i: (active(i), 0))]
-            + [picked(edge_in.shape, (0, 0)), whole(edge_bias.shape)]
-            + [pl.BlockSpec((block, width), lambda i: (passive(i), 0))] * len(given),
-            out_specs=pl.BlockSpec((block, width), lambda i: (i if late else active(i), 0)),
+            + [picked(edge_in.shape, (0, 1)), picked(edge_in.shape, (0, 2)), by_block]
+            + [picked(edge_in.shape, (0, 0)), whole(edge_bias.shape)],
+            out_specs=by_block,
             scratch_shapes=[pltpu.VMEM((2 * rows, width), BF16)],
-            compiler_params=pltpu.CompilerParams(vmem_limit_bytes=GRANT if late else None),
+            compiler_params=pltpu.CompilerParams(vmem_limit_bytes=GRANT),
             cost_estimate=cost(2 * square, 6 * slots * width),
-            name="late_part" if late else "early_part",
-        )(send, recv, nodes, edge_in, edge_in, edges, edge_in, edge_bias, *given)
-
-    early = start_edges(None)
-    nodes, early = lax.optimization_barrier((nodes, early))
+            name="first_part",
+        )(send, recv, nodes, edge_in, edge_in, edges, edge_in, edge_bias)
+
     for layer in range(LAYERS):
-        from_prev = from_behind(nodes, "patch", 1)
-        from_next = from_behind(nodes, "patch", -1)
+        if layer == 0:
+            near = [from_behind_by_parity(nodes, d, 0) for d in (1, -1)]
+        else:
+            near = [from_behind(nodes, "patch", d) for d in (1, -1)]
         top = nodes[:HUB]
         far = [from_behind(top, "patch", -d) for d in range(2, size - 1)]
         far = jnp.concatenate(far, axis=0) if len(far) > 1 else (far[0] if far else top)
         ws = picked(edge_in.shape, (layer, 1))
         wr = picked(edge_in.shape, (layer, 2))
         if layer == 0:
-            pre = start_edges(early)
+            pre = start_edges()
+            nodes, pre = lax.optimization_barrier((nodes, pre))
+            near += [from_behind_by_parity(nodes, d, 1) for d in (1, -1)]
         else:
             pre = pl.pallas_call(
                 own_kernel,
@@ -345,9 +321,9 @@
                 whole(recv.shape),
                 by_block,
                 by_block,
-                whole(nodes.shape),
-                whole(nodes.shape),
-                whole(nodes.shape),
+            ]
+            + [whole(nodes.shape)] * (1 + len(near))
+            + [
                 whole(far.shape),
                 ws,
                 wr,
@@ -357,6 +333,7 @@
             ],
             out_specs=(by_block,) + (whole((rows, width)),) * 3,
             scratch_shapes=[
+                pltpu.VMEM((2 * rows, width), BF16),
                 pltpu.VMEM((4 * rows + LANES, width), BF16),
                 pltpu.VMEM((3 * rows, width), F32),
             ],
@@ -371,8 +348,7 @@
             edges,
             pre,
             nodes,
-            from_prev,
-            from_next,
+            *near,
             far,
             edge_in,
             edge_in,

time: 88.7 us -> 93.8 us (1.057)
  starting transfers between devices: 16.3 us -> 22.8 us
  Pallas kernels: 33.9 us -> 31 us
  local copies, waits for them, and re-layouts: 3.83 us -> 6.57 us
  waiting for transfers between devices: 33 us -> 31.5 us
    ppermute x0 -> x4, starting transfers between devices: none -> 10.3 us  [from_behind_by_parity(): return lax.ppermute(block, ('region', 'patch'), route)]
    ppermute x10 -> x8, starting transfers between devices: 16.3 us -> 12.5 us  [from_behind(): lax.ppermute(block, axis, [((i - distance) % size, i) for i in range(size)])]
    pallas_call x2 -> x1, Pallas kernels: 6.48 us -> 3.55 us  [start_edges(): pl.pallas_call(functools.partial(first_kernel, 0), out_shape=jax.ShapeDty...]
    unnamed x32 -> x38, local copies, waits for them, and re-layouts: 3.83 us -> 6.57 us
    ppermute x10 -> x8, waiting for transfers between devices: 33 us -> 31.5 us  [from_behind(): lax.ppermute(block, axis, [((i - distance) % size, i) for i in range(size)])]
  transfers between devices with their start and end apart: 10 -> 12, of which waited for: 7 -> 6; matrix products, arithmetic and copies ran while one was open for 0% -> 0% of each run, Pallas kernels for 9% -> 8%
where the time goes in v4:
time: 93.8 us; the launch traced here: 93.4 us
  waiting for transfers between devices  31.5 us (34%)
  Pallas kernels  31 us (33%)
  starting transfers between devices  22.8 us (24%)
  local copies, waits for them, and re-layouts  6.57 us (7%)
  between operations  1.52 us (2%)
    ppermute x8, waiting for transfers between devices, from_behind(): lax.ppermute(block, axis, [((i - distance) % size, i) for i in range(size)])  31.5 us
    pallas_call x2, Pallas kernels, local(): pl.pallas_call(functools.partial(edge_kernel, rows, layer, size), out_sha...  20.6 us
    ppermute x8, starting transfers between devices, from_behind(): lax.ppermute(block, axis, [((i - distance) % size, i) for i in range(size)])  12.5 us
    ppermute x4, starting transfers between devices, from_behind_by_parity(): return lax.ppermute(block, ('region', 'patch'), route)  10.3 us
    unnamed x38, local copies, waits for them, and re-layouts  6.57 us
    pallas_call x1, Pallas kernels, start_edges(): pl.pallas_call(functools.partial(first_kernel, 0), out_shape=jax.ShapeDty...  3.55 us
    pallas_call x2, Pallas kernels, local(): pl.pallas_call(functools.partial(node_kernel, layer), out_shape=jax.Shape...  2.59 us
    pallas_call x1, Pallas kernels, local(): pl.pallas_call(own_kernel, out_shape=jax.ShapeDtypeStruct((slots, width),...  2.47 us
  transfers between devices with their start and end apart: 12, of which 6 were waited for; matrix products, arithmetic and copies ran while one was open for 0% of the time, Pallas kernels for 8%

profile of v4, /device:TPU:0, one launch (start us, length us, event | category | flops | bytes accessed | tf_op | source)
XLA Modules:
  0.0 93.4 jit_solution(1513622873708395422)
XLA Ops:
  0.6 5.0 %collective-permute-start = (bf16[256,512]{1,0:T(8,128)(2,1)}, bf16[256,512]{1,0:T(8,128)(2,1)S(1)}, u32[]{:S(2)}, u32[]{:S(2)}) collective-permute-start(bf16[256,512]{1,0:T(8,128)(2,1)} %nodes_ref.2), channel_id=1, source_target_pairs={{3,0},{0,1},{1,2},{2,3},{11,8},{8,9},{9,10},{10,11},{19,16},{16,17... | collective-permute-start | bytes 786440 | tf_op jit(solution)/shard_map/ppermute | solution.py:33
  5.6 3.9 %collective-permute-start.1 = (bf16[256,512]{1,0:T(8,128)(2,1)}, bf16[256,512]{1,0:T(8,128)(2,1)S(1)}, u32[]{:S(2)}, u32[]{:S(2)}) collective-permute-start(bf16[256,512]{1,0:T(8,128)(2,1)} %nodes_ref.2), channel_id=1, source_target_pairs={{1,0},{2,1},{3,2},{0,3},{9,8},{10,9},{11,10},{8,11},{17,16},{18,17... | collective-permute-start | bytes 786440 | tf_op jit(solution)/shard_map/ppermute | solution.py:33
  9.6 1.9 %copy-done = bf16[2,3,512,512]{3,2,1,0:T(8,128)(2,1)S(1)} copy-done((bf16[2,3,512,512]{3,2,1,0:T(8,128)(2,1)S(1)}, bf16[2,3,512,512]{3,2,1,0:T(8,128)(2,1)}, u32[]{:S(2)}) %copy-start) | copy-done | bytes 3145752
  11.5 1.6 %copy-done.4 = bf16[2048,512]{1,0:T(8,128)(2,1)S(1)} copy-done((bf16[2048,512]{1,0:T(8,128)(2,1)S(1)}, bf16[2048,512]{1,0:T(8,128)(2,1)}, u32[]{:S(2)}) %copy-start.4) | copy-done | bytes 2097176
  13.0 0.9 %copy-done.5 = bf16[256,512]{1,0:T(8,128)(2,1)S(1)} copy-done((bf16[256,512]{1,0:T(8,128)(2,1)S(1)}, bf16[256,512]{1,0:T(8,128)(2,1)}, u32[]{:S(2)}) %copy-start.5) | copy-done | bytes 262168
  16.1 3.5 %first_part.1.refs_5_ = f32[2048,512]{1,0:T(8,128)S(1)} custom-call(s32[16,128]{1,0:T(8,128)S(1)} %bitcast.3, s32[16,128]{1,0:T(8,128)S(1)} %bitcast.7, bf16[256,512]{1,0:T(8,128)(2,1)S(1)} %copy-done.5, bf16[2,3,512,512]{3,2,1,0:T(8,128)(2,1)S(1)} %copy-done, bf16[2,3,512,512]{3,2,1,0:T(8,128)(2,1)S(1)} %copy-done, bf16[2048,512]{1,0:T(8,128)(2,1)S(1)} %copy-done.4, ...), custom_call_target="tpu_custom_call" | custom-call | flops 2147483648 | bytes 6291456 | tf_op jit(solution)/shard_map/first_part/pallas_call | solution.py:267
  21.0 1.1 %collective-permute-start.4 = (bf16[32,512]{1,0:T(8,128)(2,1)S(1)}, bf16[32,512]{1,0:T(8,128)(2,1)S(1)}, u32[]{:S(2)}, u32[]{:S(2)}) collective-permute-start(bf16[32,512]{1,0:T(8,128)(2,1)S(1)} %slice.6), channel_id=1, source_target_pairs={{2,0},{3,1},{0,2},{1,3},{6,4},{7,5},{4,6},{5,7},{10,8},{11,9},{8,1... | collective-permute-start | bytes 98312 | tf_op jit(solution)/shard_map/ppermute | solution.py:24
  22.7 6.0 %collective-permute-done.4.refs_11_ = bf16[32,512]{1,0:T(8,128)(2,1)S(1)} collective-permute-done((bf16[32,512]{1,0:T(8,128)(2,1)S(1)}, bf16[32,512]{1,0:T(8,128)(2,1)S(1)}, u32[]{:S(2)}, u32[]{:S(2)}) %collective-permute-start.4) | collective-permute-done | bytes 32800 | tf_op jit(solution)/shard_map/ppermute | solution.py:24
  28.9 9.9 %edge_part.2 = (bf16[2048,512]{1,0:T(8,128)(2,1)S(1)}, bf16[256,512]{1,0:T(8,128)(2,1)S(1)}, f32[256,512]{1,0:T(8,128)S(1)}, bf16[256,512]{1,0:T(8,128)(2,1)S(1)}) custom-call(s32[1]{0:T(128)S(6)} %copy.18.refs_0_, s32[2]{0:T(128)S(1)} %bitcast.11, s32[16,128]{1,0:T(8,128)S(1)} %bitcast.4, s32[16,128]{1,0:T(8,128)S(1)} %bitcast.8, ...), custom_call_target="tpu_custom_call" | custom-call | flops 6442450944 | bytes 8388608 | tf_op jit(solution)/shard_map/edge_part/pallas_call | solution.py:308
  38.8 3.8 %collective-permute-start.6 = (bf16[256,512]{1,0:T(8,128)(2,1)S(1)}, bf16[256,512]{1,0:T(8,128)(2,1)S(1)}, u32[]{:S(2)}, u32[]{:S(2)}) collective-permute-start(bf16[256,512]{1,0:T(8,128)(2,1)S(1)} %get-tuple-element.16), channel_id=1, source_target_pairs={{1,0},{2,1},{3,2},{0,3},{5,4},{6,5},{7,6},{4,7},{9,8},{10,9},{11,1... | collective-permute-start | bytes 786440 | tf_op jit(solution)/shard_map/ppermute | solution.py:24
  42.7 1.8 %linear_part.1.refs_0_.pre_ref = f32[2048,512]{1,0:T(8,128)S(1)} custom-call(bf16[2048,512]{1,0:T(8,128)(2,1)S(1)} %get-tuple-element.17.edges_ref.refs_4_, bf16[2,3,512,512]{3,2,1,0:T(8,128)(2,1)S(1)} %copy-done.1, f32[2,512]{1,0:T(2,128)S(1)} %copy-done.14), custom_call_target="tpu_custom_call" | custom-call | flops 1073741824 | bytes 6291456 | tf_op jit(solution)/shard_map/linear_part/pallas_call | solution.py:363
  44.5 5.3 %collective-permute-done.5.from_prev_ref = bf16[256,512]{1,0:T(8,128)(2,1)S(1)} collective-permute-done((bf16[256,512]{1,0:T(8,128)(2,1)S(1)}, bf16[256,512]{1,0:T(8,128)(2,1)S(1)}, u32[]{:S(2)}, u32[]{:S(2)}) %collective-permute-start.5) | collective-permute-done | bytes 262176 | tf_op jit(solution)/shard_map/ppermute | solution.py:24
  49.8 2.7 %collective-permute-done.6.from_next_ref = bf16[256,512]{1,0:T(8,128)(2,1)S(1)} collective-permute-done((bf16[256,512]{1,0:T(8,128)(2,1)S(1)}, bf16[256,512]{1,0:T(8,128)(2,1)S(1)}, u32[]{:S(2)}, u32[]{:S(2)}) %collective-permute-start.6) | collective-permute-done | bytes 262176 | tf_op jit(solution)/shard_map/ppermute | solution.py:24
  52.6 0.9 %node_part.2.nodes_ref.refs_6_ = bf16[256,512]{1,0:T(8,128)(2,1)S(1)} custom-call(bf16[256,512]{1,0:T(8,128)(2,1)S(1)} %copy-done.6, f32[256,512]{1,0:T(8,128)S(1)} %get-tuple-element.14.kept_ref, bf16[256,512]{1,0:T(8,128)(2,1)S(1)} %collective-permute-done.5.from_prev_ref, bf16[256,512]{1,0:T(8,128)(2,1)S(1)} %collective-permute-done.6.from_next_ref, ...), custom_call_target="tpu_custom_call" | custom-call | flops 402653184 | bytes 1572864 | tf_op jit(solution)/shard_map/node_part/pallas_call | solution.py:378
  53.5 2.1 %collective-permute-start.8 = (bf16[256,512]{1,0:T(8,128)(2,1)S(1)}, bf16[256,512]{1,0:T(8,128)(2,1)S(1)}, u32[]{:S(2)}, u32[]{:S(2)}) collective-permute-start(bf16[256,512]{1,0:T(8,128)(2,1)S(1)} %node_part.2.nodes_ref.refs_6_), channel_id=1, source_target_pairs={{1,0},{2,1},{3,2},{0,3},{5,4},{6,5},{7,6},{4,7},{9,8},{10,9},{11,1... | collective-permute-start | bytes 786440 | tf_op jit(solution)/shard_map/ppermute | solution.py:24
  55.7 1.6 %collective-permute-start.9 = (bf16[32,512]{1,0:T(8,128)(2,1)S(1)}, bf16[32,512]{1,0:T(8,128)(2,1)S(1)}, u32[]{:S(2)}, u32[]{:S(2)}) collective-permute-start(bf16[32,512]{1,0:T(8,128)(2,1)S(1)} %slice.8), channel_id=1, source_target_pairs={{2,0},{3,1},{0,2},{1,3},{6,4},{7,5},{4,6},{5,7},{10,8},{11,9},{8,1... | collective-permute-start | bytes 98312 | tf_op jit(solution)/shard_map/ppermute | solution.py:24
  57.3 2.5 %own_part.1.refs_5_ = f32[2048,512]{1,0:T(8,128)S(1)} custom-call(s32[16,128]{1,0:T(8,128)S(1)} %bitcast.5, s32[16,128]{1,0:T(8,128)S(1)} %bitcast.9, bf16[256,512]{1,0:T(8,128)(2,1)S(1)} %node_part.2.nodes_ref.refs_6_, bf16[2,3,512,512]{3,2,1,0:T(8,128)(2,1)S(1)} %copy-done.1, bf16[2,3,512,512]{3,2,1,0:T(8,128)(2,1)S(1)} %copy-done.1, ...), custom_call_target="tpu_custom_call" | custom-call | flops 1073741824 | bytes 8388608 | tf_op jit(solution)/shard_map/own_part/pallas_call | solution.py:296
  59.8 8.4 %collective-permute-done.9.refs_9_ = bf16[32,512]{1,0:T(8,128)(2,1)S(1)} collective-permute-done((bf16[32,512]{1,0:T(8,128)(2,1)S(1)}, bf16[32,512]{1,0:T(8,128)(2,1)S(1)}, u32[]{:S(2)}, u32[]{:S(2)}) %collective-permute-start.9) | collective-permute-done | bytes 32800 | tf_op jit(solution)/shard_map/ppermute | solution.py:24
  68.3 10.7 %edge_part.3 = (bf16[2048,512]{1,0:T(8,128)(2,1)}, bf16[256,512]{1,0:T(8,128)(2,1)S(1)}, f32[256,512]{1,0:T(8,128)S(1)}, bf16[256,512]{1,0:T(8,128)(2,1)S(1)}) custom-call(s32[1]{0:T(128)S(6)} %copy.18.refs_0_, s32[2]{0:T(128)S(1)} %bitcast.12, s32[16,128]{1,0:T(8,128)S(1)} %bitcast.6, s32[16,128]{1,0:T(8,128)S(1)} %bitcast.10, ...), custom_call_target="tpu_custom_call" | custom-call | flops 6442450944 | bytes 8388608 | tf_op jit(solution)/shard_map/edge_part/pallas_call | solution.py:308
  79.0 0.9 collective-permute-start.10
  79.9 2.9 %collective-permute-start.11 = (bf16[256,512]{1,0:T(8,128)(2,1)S(1)}, bf16[256,512]{1,0:T(8,128)(2,1)S(1)}, u32[]{:S(2)}, u32[]{:S(2)}) collective-permute-start(bf16[256,512]{1,0:T(8,128)(2,1)S(1)} %get-tuple-element.20), channel_id=1, source_target_pairs={{1,0},{2,1},{3,2},{0,3},{5,4},{6,5},{7,6},{4,7},{9,8},{10,9},{11,1... | collective-permute-start | bytes 786440 | tf_op jit(solution)/shard_map/ppermute | solution.py:24
  82.8 6.4 %collective-permute-done.10.from_prev_ref = bf16[256,512]{1,0:T(8,128)(2,1)S(1)} collective-permute-done((bf16[256,512]{1,0:T(8,128)(2,1)S(1)}, bf16[256,512]{1,0:T(8,128)(2,1)S(1)}, u32[]{:S(2)}, u32[]{:S(2)}) %collective-permute-start.10) | collective-permute-done | bytes 262176 | tf_op jit(solution)/shard_map/ppermute | solution.py:24
  89.3 2.5 %collective-permute-done.11.from_next_ref = bf16[256,512]{1,0:T(8,128)(2,1)S(1)} collective-permute-done((bf16[256,512]{1,0:T(8,128)(2,1)S(1)}, bf16[256,512]{1,0:T(8,128)(2,1)S(1)}, u32[]{:S(2)}, u32[]{:S(2)}) %collective-permute-start.11) | collective-permute-done | bytes 262176 | tf_op jit(solution)/shard_map/ppermute | solution.py:24
  91.8 1.6 %node_part.3 = bf16[256,512]{1,0:T(8,128)(2,1)} custom-call(bf16[256,512]{1,0:T(8,128)(2,1)S(1)} %node_part.2.nodes_ref.refs_6_, f32[256,512]{1,0:T(8,128)S(1)} %get-tuple-element.18.kept_ref, bf16[256,512]{1,0:T(8,128)(2,1)S(1)} %collective-permute-done.10.from_prev_ref, bf16[256,512]{1,0:T(8,128)(2,1)S(1)} %collective-permute-done.11.from_next_ref, ...), custom_call_target="tpu_custom_call" | custom-call | flops 402653184 | bytes 1572864 | tf_op jit(solution)/shard_map/node_part/pallas_call | solution.py:378
  (47 shorter events, 3.6 us)
Async XLA Ops:
  0.6 28.2 %collective-permute-start = (bf16[256,512]{1,0:T(8,128)(2,1)}, bf16[256,512]{1,0:T(8,128)(2,1)S(1)}, u32[]{:S(2)}, u32[]{:S(2)}) collective-permute-start(bf16[256,512]{1,0:T(8,128)(2,1)} %nodes_ref.2), channel_id=1, source_target_pairs={{3,0},{0,1},{1,2},{2,3},{11,8},{8,9},{9,10},{10,11},{19,16},{16,17... | collective-permute-start | bytes 786440 | tf_op jit(solution)/shard_map/ppermute | solution.py:33
  5.6 23.2 %collective-permute-start.1 = (bf16[256,512]{1,0:T(8,128)(2,1)}, bf16[256,512]{1,0:T(8,128)(2,1)S(1)}, u32[]{:S(2)}, u32[]{:S(2)}) collective-permute-start(bf16[256,512]{1,0:T(8,128)(2,1)} %nodes_ref.2), channel_id=1, source_target_pairs={{1,0},{2,1},{3,2},{0,3},{9,8},{10,9},{11,10},{8,11},{17,16},{18,17... | collective-permute-start | bytes 786440 | tf_op jit(solution)/shard_map/ppermute | solution.py:33
  16.1 12.7 %copy-start.15 = (bf16[2,512,512]{2,1,0:T(8,128)(2,1)S(1)}, bf16[2,512,512]{2,1,0:T(8,128)(2,1)}, u32[]{:S(2)}) copy-start(bf16[2,512,512]{2,1,0:T(8,128)(2,1)} %refs_12_.3) | copy-start | bytes 3145732
  16.1 12.7 %copy-start.16 = (f32[2,512]{1,0:T(2,128)S(1)}, f32[2,512]{1,0:T(2,128)}, u32[]{:S(2)}) copy-start(f32[2,512]{1,0:T(2,128)} %refs_13_.3) | copy-start | bytes 12292
  16.1 12.7 %copy-start.17 = (f32[2,512]{1,0:T(2,128)S(1)}, f32[2,512]{1,0:T(2,128)}, u32[]{:S(2)}) copy-start(f32[2,512]{1,0:T(2,128)} %refs_14_.3) | copy-start | bytes 12292
  16.1 12.8 %copy-start.18 = (s32[2,1]{0,1:T(1,128)S(1)}, s32[2,1]{0,1:T(1,128)}, u32[]{:S(2)}) copy-start(s32[2,1]{0,1:T(1,128)} %param.21) | copy-start | bytes 28
  19.6 9.1 %collective-permute-start.3 = (bf16[256,512]{1,0:T(8,128)(2,1)S(1)}, bf16[256,512]{1,0:T(8,128)(2,1)S(1)}, u32[]{:S(2)}, u32[]{:S(2)}) collective-permute-start(bf16[256,512]{1,0:T(8,128)(2,1)S(1)} %copy-done.5), channel_id=1, source_target_pairs={{5,4},{6,5},{7,6},{4,7},{13,12},{14,13},{15,14},{12,15},{21,20},{2... | collective-permute-start | bytes 786440 | tf_op jit(solution)/shard_map/ppermute | solution.py:33
  20.3 8.5 %collective-permute-start.2 = (bf16[256,512]{1,0:T(8,128)(2,1)S(1)}, bf16[256,512]{1,0:T(8,128)(2,1)S(1)}, u32[]{:S(2)}, u32[]{:S(2)}) collective-permute-start(bf16[256,512]{1,0:T(8,128)(2,1)S(1)} %copy-done.5), channel_id=1, source_target_pairs={{7,4},{4,5},{5,6},{6,7},{15,12},{12,13},{13,14},{14,15},{23,20},{2... | collective-permute-start | bytes 786440 | tf_op jit(solution)/shard_map/ppermute | solution.py:33
  21.0 7.8 %collective-permute-start.4 = (bf16[32,512]{1,0:T(8,128)(2,1)S(1)}, bf16[32,512]{1,0:T(8,128)(2,1)S(1)}, u32[]{:S(2)}, u32[]{:S(2)}) collective-permute-start(bf16[32,512]{1,0:T(8,128)(2,1)S(1)} %slice.6), channel_id=1, source_target_pairs={{2,0},{3,1},{0,2},{1,3},{6,4},{7,5},{4,6},{5,7},{10,8},{11,9},{8,1... | collective-permute-start | bytes 98312 | tf_op jit(solution)/shard_map/ppermute | solution.py:24
  28.8 13.8 %copy-start.1 = (bf16[2,3,512,512]{3,2,1,0:T(8,128)(2,1)S(1)}, bf16[2,3,512,512]{3,2,1,0:T(8,128)(2,1)}, u32[]{:S(2)}) copy-start(bf16[2,3,512,512]{3,2,1,0:T(8,128)(2,1)} %refs_11_.1) | copy-start | bytes 9437188
  38.8 11.0 %collective-permute-start.5 = (bf16[256,512]{1,0:T(8,128)(2,1)S(1)}, bf16[256,512]{1,0:T(8,128)(2,1)S(1)}, u32[]{:S(2)}, u32[]{:S(2)}) collective-permute-start(bf16[256,512]{1,0:T(8,128)(2,1)S(1)} %get-tuple-element.15), channel_id=1, source_target_pairs={{3,0},{0,1},{1,2},{2,3},{7,4},{4,5},{5,6},{6,7},{11,8},{8,9},{9,10... | collective-permute-start | bytes 786440 | tf_op jit(solution)/shard_map/ppermute | solution.py:24
  38.8 13.7 %collective-permute-start.6 = (bf16[256,512]{1,0:T(8,128)(2,1)S(1)}, bf16[256,512]{1,0:T(8,128)(2,1)S(1)}, u32[]{:S(2)}, u32[]{:S(2)}) collective-permute-start(bf16[256,512]{1,0:T(8,128)(2,1)S(1)} %get-tuple-element.16), channel_id=1, source_target_pairs={{1,0},{2,1},{3,2},{0,3},{5,4},{6,5},{7,6},{4,7},{9,8},{10,9},{11,1... | collective-permute-start | bytes 786440 | tf_op jit(solution)/shard_map/ppermute | solution.py:24
  42.6 9.9 %copy-start.2 = (bf16[2,2,512,512]{3,2,1,0:T(8,128)(2,1)S(1)}, bf16[2,2,512,512]{3,2,1,0:T(8,128)(2,1)}, u32[]{:S(2)}) copy-start(bf16[2,2,512,512]{3,2,1,0:T(8,128)(2,1)} %wa_ref.3) | copy-start | bytes 6291460
  42.6 9.9 %copy-start.3 = (bf16[2,512,512]{2,1,0:T(8,128)(2,1)S(1)}, bf16[2,512,512]{2,1,0:T(8,128)(2,1)}, u32[]{:S(2)}) copy-start(bf16[2,512,512]{2,1,0:T(8,128)(2,1)} %wo_ref.3) | copy-start | bytes 3145732
  42.6 9.9 %copy-start.6 = (bf16[256,512]{1,0:T(8,128)(2,1)S(1)}, bf16[256,512]{1,0:T(8,128)(2,1)}, u32[]{:S(2)}) copy-start(bf16[256,512]{1,0:T(8,128)(2,1)} %nodes_ref.2) | copy-start | bytes 786436
  42.6 9.9 %copy-start.11 = (f32[2,512]{1,0:T(2,128)S(1)}, f32[2,512]{1,0:T(2,128)}, u32[]{:S(2)}) copy-start(f32[2,512]{1,0:T(2,128)} %bias_ref.5) | copy-start | bytes 12292
  42.7 9.9 %copy-start.12 = (f32[2,512]{1,0:T(2,128)S(1)}, f32[2,512]{1,0:T(2,128)}, u32[]{:S(2)}) copy-start(f32[2,512]{1,0:T(2,128)} %gain_ref.3) | copy-start | bytes 12292
  42.7 9.9 %copy-start.13 = (f32[2,512]{1,0:T(2,128)S(1)}, f32[2,512]{1,0:T(2,128)}, u32[]{:S(2)}) copy-start(f32[2,512]{1,0:T(2,128)} %shift_ref.3) | copy-start | bytes 12292
  52.6 4.8 %copy-start.8 = (s32[2048]{0:T(1024)S(1)}, s32[2048]{0:T(1024)}, u32[]{:S(2)}) copy-start(s32[2048]{0:T(1024)} %param.18) | copy-start | bytes 24580
  53.5 14.7 %collective-permute-start.8 = (bf16[256,512]{1,0:T(8,128)(2,1)S(1)}, bf16[256,512]{1,0:T(8,128)(2,1)S(1)}, u32[]{:S(2)}, u32[]{:S(2)}) collective-permute-start(bf16[256,512]{1,0:T(8,128)(2,1)S(1)} %node_part.2.nodes_ref.refs_6_), channel_id=1, source_target_pairs={{1,0},{2,1},{3,2},{0,3},{5,4},{6,5},{7,6},{4,7},{9,8},{10,9},{11,1... | collective-permute-start | bytes 786440 | tf_op jit(solution)/shard_map/ppermute | solution.py:24
  55.7 12.6 %collective-permute-start.7 = (bf16[256,512]{1,0:T(8,128)(2,1)S(1)}, bf16[256,512]{1,0:T(8,128)(2,1)S(1)}, u32[]{:S(2)}, u32[]{:S(2)}) collective-permute-start(bf16[256,512]{1,0:T(8,128)(2,1)S(1)} %node_part.2.nodes_ref.refs_6_), channel_id=1, source_target_pairs={{3,0},{0,1},{1,2},{2,3},{7,4},{4,5},{5,6},{6,7},{11,8},{8,9},{9,10... | collective-permute-start | bytes 786440 | tf_op jit(solution)/shard_map/ppermute | solution.py:24
  55.7 12.6 %collective-permute-start.9 = (bf16[32,512]{1,0:T(8,128)(2,1)S(1)}, bf16[32,512]{1,0:T(8,128)(2,1)S(1)}, u32[]{:S(2)}, u32[]{:S(2)}) collective-permute-start(bf16[32,512]{1,0:T(8,128)(2,1)S(1)} %slice.8), channel_id=1, source_target_pairs={{2,0},{3,1},{0,2},{1,3},{6,4},{7,5},{4,6},{5,7},{10,8},{11,9},{8,1... | collective-permute-start | bytes 98312 | tf_op jit(solution)/shard_map/ppermute | solution.py:24
  79.0 10.3 %collective-permute-start.10 = (bf16[256,512]{1,0:T(8,128)(2,1)S(1)}, bf16[256,512]{1,0:T(8,128)(2,1)S(1)}, u32[]{:S(2)}, u32[]{:S(2)}) collective-permute-start(bf16[256,512]{1,0:T(8,128)(2,1)S(1)} %get-tuple-element.19), channel_id=1, source_target_pairs={{3,0},{0,1},{1,2},{2,3},{7,4},{4,5},{5,6},{6,7},{11,8},{8,9},{9,10... | collective-permute-start | bytes 786440 | tf_op jit(solution)/shard_map/ppermute | solution.py:24
  79.9 11.8 %collective-permute-start.11 = (bf16[256,512]{1,0:T(8,128)(2,1)S(1)}, bf16[256,512]{1,0:T(8,128)(2,1)S(1)}, u32[]{:S(2)}, u32[]{:S(2)}) collective-permute-start(bf16[256,512]{1,0:T(8,128)(2,1)S(1)} %get-tuple-element.20), channel_id=1, source_target_pairs={{1,0},{2,1},{3,2},{0,3},{5,4},{6,5},{7,6},{4,7},{9,8},{10,9},{11,1... | collective-permute-start | bytes 786440 | tf_op jit(solution)/shard_map/ppermute | solution.py:24
  (7 other events, 11.3 us)

commit v5 on v4

--- a/solution.py
+++ b/solution.py
@@ -22,15 +22,6 @@
 def from_behind(block, axis, distance):
     size = lax.axis_size(axis)
     return lax.ppermute(block, axis, [((i - distance) % size, i) for i in range(size)])
-
-
-def from_behind_by_parity(block, distance, parity):
-    regions = range(parity, lax.axis_size("region"), 2)
-    size = lax.axis_size("patch")
-    route = [
-        (r * size + (i - distance) % size, r * size + i) for r in regions for i in range(size)
-    ]
-    return lax.ppermute(block, ("region", "patch"), route)
 
 
 def dot(left, right):
@@ -114,21 +105,56 @@
     out_ref[...] = pre_ref[...] + gathered
 
 
-def is_odd():
-    return lax.axis_index("region") % 2 == 1
-
-
-def first_kernel(layer, send_ref, recv_ref, nodes_ref, ws_ref, wr_ref, *refs):
-    edges_ref, first_ref, bias_ref, out_ref, table_ref = refs
-    gathered = own_sum(
-        pl.program_id(0), send_ref, recv_ref, nodes_ref, ws_ref, wr_ref, table_ref, out_ref.shape[0]
-    )
-    ahead = dot(edges_ref[...], first_ref[0, 0]) + bias_ref[layer : layer + 1, :]
-    out_ref[...] = ahead + gathered
-
-
-def is_odd():
-    return lax.axis_index("region") % 2 == 1
+def first_kernel(late, layer, steps, *refs):
+    send_ref, recv_ref, nodes_ref, bias_ref, edges_ref, weights_ref = refs[:6]
+    out_ref, table_ref, weight_buf, edges_buf, out_buf, weight_sem, in_sem, out_sem = refs[-8:]
+    rows = nodes_ref.shape[0]
+    block = edges_buf.shape[0] // steps
+    count = block // LANES
+
+    def span(i):
+        return pl.ds(i * block, block)
+
+    def fetch(i):
+        return pltpu.make_async_copy(edges_ref.at[span(i)], edges_buf.at[span(i)], in_sem.at[i])
+
+    def weight(i):
+        return pltpu.make_async_copy(weights_ref.at[layer, i], weight_buf.at[i], weight_sem.at[i])
+
+    def put(i):
+        return pltpu.make_async_copy(out_buf.at[span(i)], out_ref.at[span(i)], out_sem.at[i])
+
+    def work(span_of):
+        for i in (1, 2, 0):
+            weight(i).start()
+        for i in span_of:
+            fetch(i).start()
+        weight(1).wait()
+        table_ref[:rows, :] = dot(nodes_ref[...], weight_buf[1]).astype(BF16)
+        weight(2).wait()
+        table_ref[rows:, :] = dot(nodes_ref[...], weight_buf[2]).astype(BF16)
+        weight(0).wait()
+        for i in span_of:
+            fetch(i).wait()
+            picks = own_picks(send_ref, recv_ref, i * count, count, rows)
+            total = dot(picks, table_ref[...]) + dot(edges_buf[span(i), :], weight_buf[0])
+            out_buf[span(i), :] = total + bias_ref[layer : layer + 1, :]
+            put(i).start()
+        for i in span_of:
+            put(i).wait()
+
+    even = lax.axis_index("region") % 2 == 0
+    early = steps // 2
+
+    @pl.when(even)
+    def _():
+        work(range(early, steps) if late else range(early))
+
+    if late:
+
+        @pl.when(jnp.logical_not(even))
+        def _():
+            work(range(steps))
 
 
 def edge_kernel(rows, layer, size, *refs):
@@ -141,12 +167,8 @@
 
     @pl.when(step == 0)
     def _():
-        odd = is_odd()
         for side in range(2):
-            block = near[side][...]
-            if len(near) > 2:
-                block = jnp.where(odd, near[side + 2][...], block)
-            near_ref[side * rows : (side + 1) * rows, :] = block
+            near_ref[side * rows : (side + 1) * rows, :] = near[side][...]
         blocks = near_ref[...]
         weight_s = ws_ref[0, 0]
         table_ref[: 2 * rows, :] = dot(blocks, weight_s).astype(BF16)
@@ -263,35 +285,48 @@
     by_block = pl.BlockSpec((block, width), lambda i: (i, 0))
     square = 2 * slots * width * width
 
-    def start_edges():
+    def start_edges(held):
+        late = held is not None
+        anywhere = pl.BlockSpec(memory_space=pl.ANY)
+        given = (held,) if late else ()
+        fixed = [
+            pltpu.with_memory_space_constraint(value, pltpu.HBM)
+            for value in (send, recv, nodes, edge_bias, edges, edge_in)
+        ]
         return pl.pallas_call(
-            functools.partial(first_kernel, 0),
+            functools.partial(first_kernel, late, 0, steps),
             out_shape=jax.ShapeDtypeStruct((slots, width), F32),
-            grid=(steps,),
             in_specs=[whole(send.shape), whole(recv.shape), whole(nodes.shape)]
-            + [picked(edge_in.shape, (0, 1)), picked(edge_in.shape, (0, 2)), by_block]
-            + [picked(edge_in.shape, (0, 0)), whole(edge_bias.shape)],
-            out_specs=by_block,
-            scratch_shapes=[pltpu.VMEM((2 * rows, width), BF16)],
+            + [whole(edge_bias.shape), anywhere, anywhere]
+            + [anywhere] * len(given),
+            out_specs=anywhere,
+            grid=(1,),
+            input_output_aliases={6: 0} if late else {},
+            scratch_shapes=[
+                pltpu.VMEM((2 * rows, width), BF16),
+                pltpu.VMEM((3, width, width), BF16),
+                pltpu.VMEM((slots, width), BF16),
+                pltpu.VMEM((slots, width), F32),
+                pltpu.SemaphoreType.DMA((3,)),
+                pltpu.SemaphoreType.DMA((steps,)),
+                pltpu.SemaphoreType.DMA((steps,)),
+            ],
             compiler_params=pltpu.CompilerParams(vmem_limit_bytes=GRANT),
             cost_estimate=cost(2 * square, 6 * slots * width),
-            name="first_part",
-        )(send, recv, nodes, edge_in, edge_in, edges, edge_in, edge_bias)
-
+            name="late_part" if late else "early_part",
+        )(*fixed, *given)
+
+    early = start_edges(None)
+    sent, early = lax.optimization_barrier((nodes, early))
     for layer in range(LAYERS):
-        if layer == 0:
-            near = [from_behind_by_parity(nodes, d, 0) for d in (1, -1)]
-        else:
-            near = [from_behind(nodes, "patch", d) for d in (1, -1)]
-        top = nodes[:HUB]
+        near = [from_behind(sent, "patch", d) for d in (1, -1)]
+        top = sent[:HUB]
         far = [from_behind(top, "patch", -d) for d in range(2, size - 1)]
         far = jnp.concatenate(far, axis=0) if len(far) > 1 else (far[0] if far else top)
         ws = picked(edge_in.shape, (layer, 1))
         wr = picked(edge_in.shape, (layer, 2))
         if layer == 0:
-            pre = start_edges()
-            nodes, pre = lax.optimization_barrier((nodes, pre))
-            near += [from_behind_by_parity(nodes, d, 1) for d in (1, -1)]
+            pre = start_edges(early)
         else:
             pre = pl.pallas_call(
                 own_kernel,
@@ -406,6 +441,7 @@
             node_shift,
             *after,
         )
+        sent = nodes
     return (nodes, edges)
 
 

time: 93.8 us -> 77.8 us (0.83)
  waiting for transfers between devices: 31.5 us -> 19.1 us
  Pallas kernels: 31 us -> 38.1 us
  local copies, waits for them, and re-layouts: 6.57 us -> 0.9 us
  starting transfers between devices: 22.8 us -> 18 us
    ppermute x8 -> x10, waiting for transfers between devices: 31.5 us -> 19.1 us  [from_behind(): lax.ppermute(block, axis, [((i - distance) % size, i) for i in range(size)])]
    ppermute x4 -> x0, starting transfers between devices: 10.3 us -> none  [from_behind_by_parity(): return lax.ppermute(block, ('region', 'patch'), route)]
    unnamed x38 -> x28, local copies, waits for them, and re-layouts: 6.57 us -> 0.07 us
    pallas_call x1 -> x2, Pallas kernels: 3.55 us -> 9.19 us  [start_edges(): pl.pallas_call(functools.partial(first_kernel, late, 0, steps), out_shape...]
    ppermute x8 -> x10, starting transfers between devices: 12.5 us -> 18 us  [from_behind(): lax.ppermute(block, axis, [((i - distance) % size, i) for i in range(size)])]
    pallas_call x2, Pallas kernels: 2.59 us -> 3.53 us  [local(): pl.pallas_call(functools.partial(node_kernel, layer), out_shape=jax.Shape...]
  transfers between devices with their start and end apart: 12 -> 10, of which waited for: 6 -> 6; matrix products, arithmetic and copies ran while one was open for 0% -> 1% of each run, Pallas kernels for 8% -> 12%
where the time goes in v5:
time: 77.8 us; the launch traced here: 77.5 us
  Pallas kernels  38.1 us (49%)
  waiting for transfers between devices  19.1 us (25%)
  starting transfers between devices  18 us (23%)
  between operations  1.48 us (2%)
  local copies, waits for them, and re-layouts  0.9 us (1%)
    pallas_call x2, Pallas kernels, local(): pl.pallas_call(functools.partial(edge_kernel, rows, layer, size), out_sha...  21.1 us
    ppermute x10, waiting for transfers between devices, from_behind(): lax.ppermute(block, axis, [((i - distance) % size, i) for i in range(size)])  19.1 us
    ppermute x10, starting transfers between devices, from_behind(): lax.ppermute(block, axis, [((i - distance) % size, i) for i in range(size)])  18 us
    pallas_call x2, Pallas kernels, start_edges(): pl.pallas_call(functools.partial(first_kernel, late, 0, steps), out_shape...  9.19 us
    pallas_call x2, Pallas kernels, local(): pl.pallas_call(functools.partial(node_kernel, layer), out_shape=jax.Shape...  3.53 us
    pallas_call x1, Pallas kernels, local(): pl.pallas_call(own_kernel, out_shape=jax.ShapeDtypeStruct((slots, width),...  2.47 us
    pallas_call x1, Pallas kernels, local(): pl.pallas_call(functools.partial(linear_kernel, layer + 1), out_shape=jax...  1.78 us
  transfers between devices with their start and end apart: 10, of which 6 were waited for; matrix products, arithmetic and copies ran while one was open for 1% of the time, Pallas kernels for 12%

profile of v5, /device:TPU:0, one launch (start us, length us, event | category | flops | bytes accessed | tf_op | source)
XLA Modules:
  0.0 77.5 jit_solution(484874915456742167)
XLA Ops:
  0.6 4.3 %early_part.1.refs_6_ = f32[2048,512]{1,0:T(8,128)S(1)} custom-call(s32[16,128]{1,0:T(8,128)} %bitcast.3, s32[16,128]{1,0:T(8,128)} %bitcast.8, bf16[256,512]{1,0:T(8,128)(2,1)} %nodes_ref.1, f32[2,512]{1,0:T(2,128)} %bias_ref.3, bf16[2048,512]{1,0:T(8,128)(2,1)} %refs_4_.5, bf16[2,3,512,512]{3,2,1,0:T(8,128)(2,1)} %refs_11_.3), custom_call_target="tpu_custom_call" | custom-call | flops 2147483648 | bytes 6291456 | tf_op jit(solution)/shard_map/early_part/pallas_call | solution.py:296
  5.0 5.1 %collective-permute-start.1 = (bf16[256,512]{1,0:T(8,128)(2,1)}, bf16[256,512]{1,0:T(8,128)(2,1)S(1)}, u32[]{:S(2)}, u32[]{:S(2)}) collective-permute-start(bf16[256,512]{1,0:T(8,128)(2,1)} %nodes_ref.1), channel_id=1, source_target_pairs={{1,0},{2,1},{3,2},{0,3},{5,4},{6,5},{7,6},{4,7},{9,8},{10,9},{11,1... | collective-permute-start | bytes 786440 | tf_op jit(solution)/shard_map/ppermute | solution.py:24
  10.1 0.8 %slice.6 = bf16[32,512]{1,0:T(8,128)(2,1)S(1)} slice(bf16[256,512]{1,0:T(8,128)(2,1)} %nodes_ref.1), slice={[0:32], [0:512]} | slice | bytes 65536 | tf_op jit(solution)/shard_map/slice | solution.py:323
  11.0 1.0 %collective-permute-start.2 = (bf16[32,512]{1,0:T(8,128)(2,1)S(1)}, bf16[32,512]{1,0:T(8,128)(2,1)S(1)}, u32[]{:S(2)}, u32[]{:S(2)}) collective-permute-start(bf16[32,512]{1,0:T(8,128)(2,1)S(1)} %slice.6), channel_id=1, source_target_pairs={{2,0},{3,1},{0,2},{1,3},{6,4},{7,5},{4,6},{5,7},{10,8},{11,9},{8,1... | collective-permute-start | bytes 98312 | tf_op jit(solution)/shard_map/ppermute | solution.py:24
  12.0 4.9 %late_part.1.refs_5_ = f32[2048,512]{1,0:T(8,128)S(1)} custom-call(s32[16,128]{1,0:T(8,128)} %bitcast.4, s32[16,128]{1,0:T(8,128)} %bitcast.9, bf16[256,512]{1,0:T(8,128)(2,1)} %nodes_ref.1, f32[2,512]{1,0:T(2,128)} %bias_ref.3, bf16[2048,512]{1,0:T(8,128)(2,1)} %refs_4_.5, bf16[2,3,512,512]{3,2,1,0:T(8,128)(2,1)} %refs_11_.3, ...), custom_call_target="tpu_custom_call", output_to_operand_aliasing={{}: (6, {})} | custom-call | flops 2147483648 | bytes 6291456 | tf_op jit(solution)/shard_map/late_part/pallas_call | solution.py:296
  17.6 3.2 %collective-permute-done.2.refs_9_ = bf16[32,512]{1,0:T(8,128)(2,1)S(1)} collective-permute-done((bf16[32,512]{1,0:T(8,128)(2,1)S(1)}, bf16[32,512]{1,0:T(8,128)(2,1)S(1)}, u32[]{:S(2)}, u32[]{:S(2)}) %collective-permute-start.2) | collective-permute-done | bytes 32800 | tf_op jit(solution)/shard_map/ppermute | solution.py:24
  20.8 10.3 %edge_part.2 = (bf16[2048,512]{1,0:T(8,128)(2,1)S(1)}, bf16[256,512]{1,0:T(8,128)(2,1)S(1)}, f32[256,512]{1,0:T(8,128)S(1)}, bf16[256,512]{1,0:T(8,128)(2,1)S(1)}) custom-call(s32[1]{0:T(128)S(6)} %copy.20.refs_0_, s32[2]{0:T(128)S(1)} %bitcast.13, s32[16,128]{1,0:T(8,128)S(1)} %bitcast.5, s32[16,128]{1,0:T(8,128)S(1)} %bitcast.10, ...), custom_call_target="tpu_custom_call" | custom-call | flops 6442450944 | bytes 8388608 | tf_op jit(solution)/shard_map/edge_part/pallas_call | solution.py:343
  31.2 0.5 collective-permute-start.3
  31.6 3.4 %collective-permute-start.4 = (bf16[256,512]{1,0:T(8,128)(2,1)S(1)}, bf16[256,512]{1,0:T(8,128)(2,1)S(1)}, u32[]{:S(2)}, u32[]{:S(2)}) collective-permute-start(bf16[256,512]{1,0:T(8,128)(2,1)S(1)} %get-tuple-element.16), channel_id=1, source_target_pairs={{1,0},{2,1},{3,2},{0,3},{5,4},{6,5},{7,6},{4,7},{9,8},{10,9},{11,1... | collective-permute-start | bytes 786440 | tf_op jit(solution)/shard_map/ppermute | solution.py:24
  35.1 1.8 %linear_part.1.refs_0_.pre_ref = f32[2048,512]{1,0:T(8,128)S(1)} custom-call(bf16[2048,512]{1,0:T(8,128)(2,1)S(1)} %get-tuple-element.17.edges_ref.refs_4_, bf16[2,3,512,512]{3,2,1,0:T(8,128)(2,1)S(1)} %copy-done, f32[2,512]{1,0:T(2,128)S(1)} %copy-done.6), custom_call_target="tpu_custom_call" | custom-call | flops 1073741824 | bytes 6291456 | tf_op jit(solution)/shard_map/linear_part/pallas_call | solution.py:398
  36.9 2.6 %collective-permute-done.3.from_prev_ref = bf16[256,512]{1,0:T(8,128)(2,1)S(1)} collective-permute-done((bf16[256,512]{1,0:T(8,128)(2,1)S(1)}, bf16[256,512]{1,0:T(8,128)(2,1)S(1)}, u32[]{:S(2)}, u32[]{:S(2)}) %collective-permute-start.3) | collective-permute-done | bytes 262176 | tf_op jit(solution)/shard_map/ppermute | solution.py:24
  39.5 2.2 %collective-permute-done.4.from_next_ref = bf16[256,512]{1,0:T(8,128)(2,1)S(1)} collective-permute-done((bf16[256,512]{1,0:T(8,128)(2,1)S(1)}, bf16[256,512]{1,0:T(8,128)(2,1)S(1)}, u32[]{:S(2)}, u32[]{:S(2)}) %collective-permute-start.4) | collective-permute-done | bytes 262176 | tf_op jit(solution)/shard_map/ppermute | solution.py:24
  41.8 1.9 %node_part.2.nodes_ref.refs_6_ = bf16[256,512]{1,0:T(8,128)(2,1)S(1)} custom-call(bf16[256,512]{1,0:T(8,128)(2,1)} %nodes_ref.1, f32[256,512]{1,0:T(8,128)S(1)} %get-tuple-element.14.kept_ref, bf16[256,512]{1,0:T(8,128)(2,1)S(1)} %collective-permute-done.3.from_prev_ref, bf16[256,512]{1,0:T(8,128)(2,1)S(1)} %collective-permute-done.4.from_next_ref, ...), custom_call_target="tpu_custom_call" | custom-call | flops 402653184 | bytes 1572864 | tf_op jit(solution)/shard_map/node_part/pallas_call | solution.py:413
  43.7 2.5 %collective-permute-start.6 = (bf16[256,512]{1,0:T(8,128)(2,1)S(1)}, bf16[256,512]{1,0:T(8,128)(2,1)S(1)}, u32[]{:S(2)}, u32[]{:S(2)}) collective-permute-start(bf16[256,512]{1,0:T(8,128)(2,1)S(1)} %node_part.2.nodes_ref.refs_6_), channel_id=1, source_target_pairs={{1,0},{2,1},{3,2},{0,3},{5,4},{6,5},{7,6},{4,7},{9,8},{10,9},{11,1... | collective-permute-start | bytes 786440 | tf_op jit(solution)/shard_map/ppermute | solution.py:24
  46.1 0.4 collective-permute-start.5
  46.5 1.2 %collective-permute-start.7 = (bf16[32,512]{1,0:T(8,128)(2,1)S(1)}, bf16[32,512]{1,0:T(8,128)(2,1)S(1)}, u32[]{:S(2)}, u32[]{:S(2)}) collective-permute-start(bf16[32,512]{1,0:T(8,128)(2,1)S(1)} %slice.8), channel_id=1, source_target_pairs={{2,0},{3,1},{0,2},{1,3},{6,4},{7,5},{4,6},{5,7},{10,8},{11,9},{8,1... | collective-permute-start | bytes 98312 | tf_op jit(solution)/shard_map/ppermute | solution.py:24
  47.8 2.5 %own_part.1.refs_5_ = f32[2048,512]{1,0:T(8,128)S(1)} custom-call(s32[16,128]{1,0:T(8,128)S(1)} %bitcast.6, s32[16,128]{1,0:T(8,128)S(1)} %bitcast.11, bf16[256,512]{1,0:T(8,128)(2,1)S(1)} %node_part.2.nodes_ref.refs_6_, bf16[2,3,512,512]{3,2,1,0:T(8,128)(2,1)S(1)} %copy-done, bf16[2,3,512,512]{3,2,1,0:T(8,128)(2,1)S(1)} %copy-done, ...), custom_call_target="tpu_custom_call" | custom-call | flops 1073741824 | bytes 8388608 | tf_op jit(solution)/shard_map/own_part/pallas_call | solution.py:331
  50.2 5.5 %collective-permute-done.7.refs_9_ = bf16[32,512]{1,0:T(8,128)(2,1)S(1)} collective-permute-done((bf16[32,512]{1,0:T(8,128)(2,1)S(1)}, bf16[32,512]{1,0:T(8,128)(2,1)S(1)}, u32[]{:S(2)}, u32[]{:S(2)}) %collective-permute-start.7) | collective-permute-done | bytes 32800 | tf_op jit(solution)/shard_map/ppermute | solution.py:24
  55.7 10.8 %edge_part.3 = (bf16[2048,512]{1,0:T(8,128)(2,1)}, bf16[256,512]{1,0:T(8,128)(2,1)S(1)}, f32[256,512]{1,0:T(8,128)S(1)}, bf16[256,512]{1,0:T(8,128)(2,1)S(1)}) custom-call(s32[1]{0:T(128)S(6)} %copy.20.refs_0_, s32[2]{0:T(128)S(1)} %bitcast.14, s32[16,128]{1,0:T(8,128)S(1)} %bitcast.7, s32[16,128]{1,0:T(8,128)S(1)} %bitcast.12, ...), custom_call_target="tpu_custom_call" | custom-call | flops 6442450944 | bytes 8388608 | tf_op jit(solution)/shard_map/edge_part/pallas_call | solution.py:343
  66.5 0.2 collective-permute-start.8
  66.7 3.6 %collective-permute-start.9 = (bf16[256,512]{1,0:T(8,128)(2,1)S(1)}, bf16[256,512]{1,0:T(8,128)(2,1)S(1)}, u32[]{:S(2)}, u32[]{:S(2)}) collective-permute-start(bf16[256,512]{1,0:T(8,128)(2,1)S(1)} %get-tuple-element.20), channel_id=1, source_target_pairs={{1,0},{2,1},{3,2},{0,3},{5,4},{6,5},{7,6},{4,7},{9,8},{10,9},{11,1... | collective-permute-start | bytes 786440 | tf_op jit(solution)/shard_map/ppermute | solution.py:24
  70.3 4.4 %collective-permute-done.8.from_prev_ref = bf16[256,512]{1,0:T(8,128)(2,1)S(1)} collective-permute-done((bf16[256,512]{1,0:T(8,128)(2,1)S(1)}, bf16[256,512]{1,0:T(8,128)(2,1)S(1)}, u32[]{:S(2)}, u32[]{:S(2)}) %collective-permute-start.8) | collective-permute-done | bytes 262176 | tf_op jit(solution)/shard_map/ppermute | solution.py:24
  74.8 1.1 %collective-permute-done.9.from_next_ref = bf16[256,512]{1,0:T(8,128)(2,1)S(1)} collective-permute-done((bf16[256,512]{1,0:T(8,128)(2,1)S(1)}, bf16[256,512]{1,0:T(8,128)(2,1)S(1)}, u32[]{:S(2)}, u32[]{:S(2)}) %collective-permute-start.9) | collective-permute-done | bytes 262176 | tf_op jit(solution)/shard_map/ppermute | solution.py:24
  75.9 1.6 %node_part.3 = bf16[256,512]{1,0:T(8,128)(2,1)} custom-call(bf16[256,512]{1,0:T(8,128)(2,1)S(1)} %node_part.2.nodes_ref.refs_6_, f32[256,512]{1,0:T(8,128)S(1)} %get-tuple-element.18.kept_ref, bf16[256,512]{1,0:T(8,128)(2,1)S(1)} %collective-permute-done.8.from_prev_ref, bf16[256,512]{1,0:T(8,128)(2,1)S(1)} %collective-permute-done.9.from_next_ref, ...), custom_call_target="tpu_custom_call" | custom-call | flops 402653184 | bytes 1572864 | tf_op jit(solution)/shard_map/node_part/pallas_call | solution.py:413
  (34 shorter events, 0.1 us)
Async XLA Ops:
  5.0 15.8 %collective-permute-start.1 = (bf16[256,512]{1,0:T(8,128)(2,1)}, bf16[256,512]{1,0:T(8,128)(2,1)S(1)}, u32[]{:S(2)}, u32[]{:S(2)}) collective-permute-start(bf16[256,512]{1,0:T(8,128)(2,1)} %nodes_ref.1), channel_id=1, source_target_pairs={{1,0},{2,1},{3,2},{0,3},{5,4},{6,5},{7,6},{4,7},{9,8},{10,9},{11,1... | collective-permute-start | bytes 786440 | tf_op jit(solution)/shard_map/ppermute | solution.py:24
  10.1 10.7 %collective-permute-start = (bf16[256,512]{1,0:T(8,128)(2,1)}, bf16[256,512]{1,0:T(8,128)(2,1)S(1)}, u32[]{:S(2)}, u32[]{:S(2)}) collective-permute-start(bf16[256,512]{1,0:T(8,128)(2,1)} %nodes_ref.1), channel_id=1, source_target_pairs={{3,0},{0,1},{1,2},{2,3},{7,4},{4,5},{5,6},{6,7},{11,8},{8,9},{9,10... | collective-permute-start | bytes 786440 | tf_op jit(solution)/shard_map/ppermute | solution.py:24
  10.9 9.8 %copy-start = (bf16[2,3,512,512]{3,2,1,0:T(8,128)(2,1)S(1)}, bf16[2,3,512,512]{3,2,1,0:T(8,128)(2,1)}, u32[]{:S(2)}) copy-start(bf16[2,3,512,512]{3,2,1,0:T(8,128)(2,1)} %refs_11_.3) | copy-start | bytes 9437188
  10.9 9.8 %copy-start.2 = (bf16[2048,512]{1,0:T(8,128)(2,1)S(1)}, bf16[2048,512]{1,0:T(8,128)(2,1)}, u32[]{:S(2)}) copy-start(bf16[2048,512]{1,0:T(8,128)(2,1)} %refs_4_.5) | copy-start | bytes 6291460
  10.9 9.8 %copy-start.4 = (s32[2048]{0:T(1024)S(1)}, s32[2048]{0:T(1024)}, u32[]{:S(2)}) copy-start(s32[2048]{0:T(1024)} %param.18) | copy-start | bytes 24580
  10.9 9.8 %copy-start.5 = (s32[2048]{0:T(1024)S(1)}, s32[2048]{0:T(1024)}, u32[]{:S(2)}) copy-start(s32[2048]{0:T(1024)} %param.19) | copy-start | bytes 24580
  10.9 9.8 %copy-start.10 = (bf16[2,512,512]{2,1,0:T(8,128)(2,1)S(1)}, bf16[2,512,512]{2,1,0:T(8,128)(2,1)}, u32[]{:S(2)}) copy-start(bf16[2,512,512]{2,1,0:T(8,128)(2,1)} %refs_12_.3) | copy-start | bytes 3145732
  11.0 9.8 %copy-start.11 = (f32[2,512]{1,0:T(2,128)S(1)}, f32[2,512]{1,0:T(2,128)}, u32[]{:S(2)}) copy-start(f32[2,512]{1,0:T(2,128)} %refs_13_.3) | copy-start | bytes 12292
  11.0 9.8 %copy-start.12 = (f32[2,512]{1,0:T(2,128)S(1)}, f32[2,512]{1,0:T(2,128)}, u32[]{:S(2)}) copy-start(f32[2,512]{1,0:T(2,128)} %refs_14_.3) | copy-start | bytes 12292
  11.0 9.8 %copy-start.13 = (s32[2,1]{0,1:T(1,128)S(1)}, s32[2,1]{0,1:T(1,128)}, u32[]{:S(2)}) copy-start(s32[2,1]{0,1:T(1,128)} %param.21) | copy-start | bytes 28
  11.0 9.8 %collective-permute-start.2 = (bf16[32,512]{1,0:T(8,128)(2,1)S(1)}, bf16[32,512]{1,0:T(8,128)(2,1)S(1)}, u32[]{:S(2)}, u32[]{:S(2)}) collective-permute-start(bf16[32,512]{1,0:T(8,128)(2,1)S(1)} %slice.6), channel_id=1, source_target_pairs={{2,0},{3,1},{0,2},{1,3},{6,4},{7,5},{4,6},{5,7},{10,8},{11,9},{8,1... | collective-permute-start | bytes 98312 | tf_op jit(solution)/shard_map/ppermute | solution.py:24
  20.8 14.2 %copy-start.6 = (f32[2,512]{1,0:T(2,128)S(1)}, f32[2,512]{1,0:T(2,128)}, u32[]{:S(2)}) copy-start(f32[2,512]{1,0:T(2,128)} %bias_ref.3) | copy-start | bytes 12292
  31.2 8.3 %collective-permute-start.3 = (bf16[256,512]{1,0:T(8,128)(2,1)S(1)}, bf16[256,512]{1,0:T(8,128)(2,1)S(1)}, u32[]{:S(2)}, u32[]{:S(2)}) collective-permute-start(bf16[256,512]{1,0:T(8,128)(2,1)S(1)} %get-tuple-element.15), channel_id=1, source_target_pairs={{3,0},{0,1},{1,2},{2,3},{7,4},{4,5},{5,6},{6,7},{11,8},{8,9},{9,10... | collective-permute-start | bytes 786440 | tf_op jit(solution)/shard_map/ppermute | solution.py:24
  31.6 10.1 %collective-permute-start.4 = (bf16[256,512]{1,0:T(8,128)(2,1)S(1)}, bf16[256,512]{1,0:T(8,128)(2,1)S(1)}, u32[]{:S(2)}, u32[]{:S(2)}) collective-permute-start(bf16[256,512]{1,0:T(8,128)(2,1)S(1)} %get-tuple-element.16), channel_id=1, source_target_pairs={{1,0},{2,1},{3,2},{0,3},{5,4},{6,5},{7,6},{4,7},{9,8},{10,9},{11,1... | collective-permute-start | bytes 786440 | tf_op jit(solution)/shard_map/ppermute | solution.py:24
  35.1 6.7 %copy-start.1 = (bf16[2,2,512,512]{3,2,1,0:T(8,128)(2,1)S(1)}, bf16[2,2,512,512]{3,2,1,0:T(8,128)(2,1)}, u32[]{:S(2)}) copy-start(bf16[2,2,512,512]{3,2,1,0:T(8,128)(2,1)} %wa_ref.3) | copy-start | bytes 6291460
  35.1 6.7 %copy-start.3 = (bf16[2,512,512]{2,1,0:T(8,128)(2,1)S(1)}, bf16[2,512,512]{2,1,0:T(8,128)(2,1)}, u32[]{:S(2)}) copy-start(bf16[2,512,512]{2,1,0:T(8,128)(2,1)} %wo_ref.3) | copy-start | bytes 3145732
  35.1 6.7 %copy-start.7 = (f32[2,512]{1,0:T(2,128)S(1)}, f32[2,512]{1,0:T(2,128)}, u32[]{:S(2)}) copy-start(f32[2,512]{1,0:T(2,128)} %bias_ref.5) | copy-start | bytes 12292
  35.1 6.7 %copy-start.8 = (f32[2,512]{1,0:T(2,128)S(1)}, f32[2,512]{1,0:T(2,128)}, u32[]{:S(2)}) copy-start(f32[2,512]{1,0:T(2,128)} %gain_ref.3) | copy-start | bytes 12292
  35.1 6.7 %copy-start.9 = (f32[2,512]{1,0:T(2,128)S(1)}, f32[2,512]{1,0:T(2,128)}, u32[]{:S(2)}) copy-start(f32[2,512]{1,0:T(2,128)} %shift_ref.3) | copy-start | bytes 12292
  43.7 12.1 %collective-permute-start.6 = (bf16[256,512]{1,0:T(8,128)(2,1)S(1)}, bf16[256,512]{1,0:T(8,128)(2,1)S(1)}, u32[]{:S(2)}, u32[]{:S(2)}) collective-permute-start(bf16[256,512]{1,0:T(8,128)(2,1)S(1)} %node_part.2.nodes_ref.refs_6_), channel_id=1, source_target_pairs={{1,0},{2,1},{3,2},{0,3},{5,4},{6,5},{7,6},{4,7},{9,8},{10,9},{11,1... | collective-permute-start | bytes 786440 | tf_op jit(solution)/shard_map/ppermute | solution.py:24
  46.1 9.6 %collective-permute-start.5 = (bf16[256,512]{1,0:T(8,128)(2,1)S(1)}, bf16[256,512]{1,0:T(8,128)(2,1)S(1)}, u32[]{:S(2)}, u32[]{:S(2)}) collective-permute-start(bf16[256,512]{1,0:T(8,128)(2,1)S(1)} %node_part.2.nodes_ref.refs_6_), channel_id=1, source_target_pairs={{3,0},{0,1},{1,2},{2,3},{7,4},{4,5},{5,6},{6,7},{11,8},{8,9},{9,10... | collective-permute-start | bytes 786440 | tf_op jit(solution)/shard_map/ppermute | solution.py:24
  46.5 9.2 %collective-permute-start.7 = (bf16[32,512]{1,0:T(8,128)(2,1)S(1)}, bf16[32,512]{1,0:T(8,128)(2,1)S(1)}, u32[]{:S(2)}, u32[]{:S(2)}) collective-permute-start(bf16[32,512]{1,0:T(8,128)(2,1)S(1)} %slice.8), channel_id=1, source_target_pairs={{2,0},{3,1},{0,2},{1,3},{6,4},{7,5},{4,6},{5,7},{10,8},{11,9},{8,1... | collective-permute-start | bytes 98312 | tf_op jit(solution)/shard_map/ppermute | solution.py:24
  66.5 8.3 %collective-permute-start.8 = (bf16[256,512]{1,0:T(8,128)(2,1)S(1)}, bf16[256,512]{1,0:T(8,128)(2,1)S(1)}, u32[]{:S(2)}, u32[]{:S(2)}) collective-permute-start(bf16[256,512]{1,0:T(8,128)(2,1)S(1)} %get-tuple-element.19), channel_id=1, source_target_pairs={{3,0},{0,1},{1,2},{2,3},{7,4},{4,5},{5,6},{6,7},{11,8},{8,9},{9,10... | collective-permute-start | bytes 786440 | tf_op jit(solution)/shard_map/ppermute | solution.py:24
  66.7 9.2 %collective-permute-start.9 = (bf16[256,512]{1,0:T(8,128)(2,1)S(1)}, bf16[256,512]{1,0:T(8,128)(2,1)S(1)}, u32[]{:S(2)}, u32[]{:S(2)}) collective-permute-start(bf16[256,512]{1,0:T(8,128)(2,1)S(1)} %get-tuple-element.20), channel_id=1, source_target_pairs={{1,0},{2,1},{3,2},{0,3},{5,4},{6,5},{7,6},{4,7},{9,8},{10,9},{11,1... | collective-permute-start | bytes 786440 | tf_op jit(solution)/shard_map/ppermute | solution.py:24

commit v6 on v5

--- a/solution.py
+++ b/solution.py
@@ -28,9 +28,12 @@
     return jnp.dot(left, right, preferred_element_type=F32)
 
 
-def silu(value):
-    half = value * 0.5
+def silu_of_half(half):
     return half + half * jnp.tanh(half)
+
+
+def half_table(rows, weight):
+    return (dot(rows, weight) * 0.5).astype(BF16)
 
 
 def layer_norm(value, gain, shift):
@@ -54,11 +57,12 @@
     return jnp.concatenate(groups, axis=0)
 
 
-def selector_rows(codes_ref, first, count, width):
+def selector_rows(codes_ref, first, count, width, valid):
     tile = 2 * LANES
     groups = []
     for i in range(count):
-        row = codes_ref[pl.ds(first + i, 1), :]
+        slot = (first + i) * LANES + lax.broadcasted_iota(jnp.int32, (1, LANES), 1)
+        row = jnp.where(slot < valid, codes_ref[pl.ds(first + i, 1), :], -1)
         parts = []
         for start in range(0, width, tile):
             near = jnp.clip(row - start, -1, tile).astype(F32)
@@ -70,13 +74,14 @@
 
 
 def linear_kernel(layer, edges_ref, weight_ref, bias_ref, out_ref):
-    out_ref[...] = dot(edges_ref[...], weight_ref[0, 0]) + bias_ref[layer : layer + 1, :]
+    ahead = dot(edges_ref[...], weight_ref[0, 0]) + bias_ref[layer : layer + 1, :]
+    out_ref[...] = ahead * 0.5
 
 
 def own_table(nodes, ws_ref, wr_ref, table_ref):
     rows = nodes.shape[0]
-    table_ref[:rows, :] = dot(nodes, ws_ref[0, 0]).astype(BF16)
-    table_ref[rows:, :] = dot(nodes, wr_ref[0, 0]).astype(BF16)
+    table_ref[:rows, :] = half_table(nodes, ws_ref[0, 0])
+    table_ref[rows:, :] = half_table(nodes, wr_ref[0, 0])
 
 
 def own_picks(send_ref, recv_ref, first, count, rows):
@@ -130,15 +135,15 @@
         for i in span_of:
             fetch(i).start()
         weight(1).wait()
-        table_ref[:rows, :] = dot(nodes_ref[...], weight_buf[1]).astype(BF16)
+        table_ref[:rows, :] = half_table(nodes_ref[...], weight_buf[1])
         weight(2).wait()
-        table_ref[rows:, :] = dot(nodes_ref[...], weight_buf[2]).astype(BF16)
+        table_ref[rows:, :] = half_table(nodes_ref[...], weight_buf[2])
         weight(0).wait()
         for i in span_of:
             fetch(i).wait()
             picks = own_picks(send_ref, recv_ref, i * count, count, rows)
-            total = dot(picks, table_ref[...]) + dot(edges_buf[span(i), :], weight_buf[0])
-            out_buf[span(i), :] = total + bias_ref[layer : layer + 1, :]
+            ahead = dot(edges_buf[span(i), :], weight_buf[0]) + bias_ref[layer : layer + 1, :]
+            out_buf[span(i), :] = ahead * 0.5 + dot(picks, table_ref[...])
             put(i).start()
         for i in span_of:
             put(i).wait()
@@ -171,8 +176,8 @@
             near_ref[side * rows : (side + 1) * rows, :] = near[side][...]
         blocks = near_ref[...]
         weight_s = ws_ref[0, 0]
-        table_ref[: 2 * rows, :] = dot(blocks, weight_s).astype(BF16)
-        table_ref[2 * rows : 4 * rows, :] = dot(blocks, wr_ref[0, 0]).astype(BF16)
+        table_ref[: 2 * rows, :] = half_table(blocks, weight_s)
+        table_ref[2 * rows : 4 * rows, :] = half_table(blocks, wr_ref[0, 0])
         away = owner_ref[layer] - lax.axis_index("patch")
         away = jnp.where(away < 0, away + size, away)
         hub = own_ref[:HUB, :]
@@ -182,31 +187,45 @@
         hub = jnp.where(away == size - 1, near_ref[:HUB, :], hub)
         hub = jnp.where(away == 1, near_ref[rows : rows + HUB, :], hub)
         hub = jnp.where(away == 0, own_ref[:HUB, :], hub)
-        table_ref[4 * rows : 4 * rows + HUB, :] = dot(hub, weight_s).astype(BF16)
+        table_ref[4 * rows : 4 * rows + HUB, :] = half_table(hub, weight_s)
         table_ref[4 * rows + HUB :, :] = jnp.zeros_like(table_ref[4 * rows + HUB :, :])
         total_ref[...] = jnp.zeros_like(total_ref)
 
     block = out_ref.shape[0]
-    count = block // LANES
-    spans = [
+    part = min(block, 512)
+    count = part // LANES
+    first = step * (block // LANES)
+    valid = valid_ref[0]
+    near_spans, far_spans = [
         tuple((start + at, 2 * LANES) for at in range(0, rows, 2 * LANES)) for start in (0, 2 * rows)
     ]
     hubs = ((3 * rows, LANES),)
-    picks = jnp.concatenate(
-        [
-            selector(send_ref, step * count, count, spans[0] + spans[1]),
-            selector(recv_ref, step * count, count, spans[0] + spans[1]),
-            selector(send_ref, step * count, count, hubs),
-        ],
-        axis=1,
-    )
-    activated = silu(pre_ref[...] + dot(picks, table_ref[...])).astype(BF16)
-    mixed = dot(activated, wo_ref[0])
-    normed = layer_norm(mixed, gain_ref[layer : layer + 1, :], shift_ref[layer : layer + 1, :])
-    spot = step * block + lax.broadcasted_iota(jnp.int32, (block, 1), 0)
-    updated = jnp.where(spot < valid_ref[0], edges_ref[...].astype(F32) + normed, 0.0).astype(BF16)
-    out_ref[...] = updated
-    total_ref[...] += dot(selector_rows(recv_ref, step * count, count, 3 * rows), updated)
+    halves = []
+    for i in range(block // part):
+        at = first + i * count
+        picks = jnp.concatenate(
+            [
+                selector(send_ref, at, count, near_spans + far_spans),
+                selector(recv_ref, at, count, near_spans + far_spans),
+                selector(send_ref, at, count, hubs),
+            ],
+            axis=1,
+        )
+        halves.append(pre_ref[i * part : (i + 1) * part, :] + dot(picks, table_ref[...]))
+    updates = []
+    for i, half in enumerate(halves):
+        mixed = dot(silu_of_half(half).astype(BF16), wo_ref[0])
+        normed = layer_norm(mixed, gain_ref[layer : layer + 1, :], shift_ref[layer : layer + 1, :])
+        latent = edges_ref[i * part : (i + 1) * part, :].astype(F32)
+        updates.append((latent + normed).astype(BF16))
+        out_ref[i * part : (i + 1) * part, :] = updates[-1]
+    live = selector_rows(recv_ref, first, block // LANES, 3 * rows, valid)
+    total_ref[...] += dot(live, jnp.concatenate(updates, axis=0))
+
+    @pl.when((step + 1) * block > valid)
+    def _():
+        slot = step * block + lax.broadcasted_iota(jnp.int32, (block, 1), 0)
+        out_ref[...] = jnp.where(slot < valid, out_ref[...].astype(F32), 0.0).astype(BF16)
 
     @pl.when(step == pl.num_programs(0) - 1)
     def _():
@@ -234,7 +253,7 @@
     summed = from_prev_ref[...].astype(F32) + kept_ref[...] + from_next_ref[...].astype(F32)
     pre_node = dot(nodes, wh_ref[0, 0]) + dot(summed.astype(BF16), wa_ref[0, 0])
     pre_node = pre_node + bias_ref[layer : layer + 1, :]
-    mixed = dot(silu(pre_node).astype(BF16), wo_ref[0])
+    mixed = dot(silu_of_half(pre_node * 0.5).astype(BF16), wo_ref[0])
     normed = layer_norm(mixed, gain_ref[layer : layer + 1, :], shift_ref[layer : layer + 1, :])
     out_ref[...] = (nodes.astype(F32) + normed).astype(BF16)
 
@@ -280,6 +299,8 @@
     size = lax.axis_size("patch")
     block = min(512, slots)
     steps = slots // block
+    pair = min(1024, slots)
+    by_pair = pl.BlockSpec((pair, width), lambda i: (i, 0))
     send = senders.reshape(slots // LANES, LANES)
     recv = receivers.reshape(slots // LANES, LANES)
     by_block = pl.BlockSpec((block, width), lambda i: (i, 0))
@@ -348,14 +369,14 @@
                 jax.ShapeDtypeStruct((rows, width), F32),
                 jax.ShapeDtypeStruct((rows, width), BF16),
             ),
-            grid=(steps,),
+            grid=(slots // pair,),
             in_specs=[
                 scalars(),
                 scalars(),
                 whole(send.shape),
                 whole(recv.shape),
-                by_block,
-                by_block,
+                by_pair,
+                by_pair,
             ]
             + [whole(nodes.shape)] * (1 + len(near))
             + [
@@ -366,7 +387,7 @@
                 whole(edge_gain.shape),
                 whole(edge_shift.shape),
             ],
-            out_specs=(by_block,) + (whole((rows, width)),) * 3,
+            out_specs=(by_pair,) + (whole((rows, width)),) * 3,
             scratch_shapes=[
                 pltpu.VMEM((2 * rows, width), BF16),
                 pltpu.VMEM((4 * rows + LANES, width), BF16),

time: 77.8 us -> 75.5 us (0.970)
  Pallas kernels: 38.1 us -> 35.1 us
    pallas_call x2, Pallas kernels: 21.1 us -> 18.1 us  [local(): pl.pallas_call(functools.partial(edge_kernel, rows, layer, size), out_sha...]
where the time goes in v6:
time: 75.5 us; the launch traced here: 75.2 us
  Pallas kernels  35.1 us (46%)
  waiting for transfers between devices  19.5 us (26%)
  starting transfers between devices  18.2 us (24%)
  between operations  1.48 us (2%)
  local copies, waits for them, and re-layouts  0.9 us (1%)
    ppermute x10, waiting for transfers between devices, from_behind(): lax.ppermute(block, axis, [((i - distance) % size, i) for i in range(size)])  19.5 us
    ppermute x10, starting transfers between devices, from_behind(): lax.ppermute(block, axis, [((i - distance) % size, i) for i in range(size)])  18.2 us
    pallas_call x2, Pallas kernels, local(): pl.pallas_call(functools.partial(edge_kernel, rows, layer, size), out_sha...  18.1 us
    pallas_call x2, Pallas kernels, start_edges(): pl.pallas_call(functools.partial(first_kernel, late, 0, steps), out_shape...  9.2 us
    pallas_call x2, Pallas kernels, local(): pl.pallas_call(functools.partial(node_kernel, layer), out_shape=jax.Shape...  3.53 us
    pallas_call x1, Pallas kernels, local(): pl.pallas_call(own_kernel, out_shape=jax.ShapeDtypeStruct((slots, width),...  2.47 us
    pallas_call x1, Pallas kernels, local(): pl.pallas_call(functools.partial(linear_kernel, layer + 1), out_shape=jax...  1.79 us
  transfers between devices with their start and end apart: 10, of which 6 were waited for; matrix products, arithmetic and copies ran while one was open for 1% of the time, Pallas kernels for 12%

profile of v6, /device:TPU:0, one launch (start us, length us, event | category | flops | bytes accessed | tf_op | source)
XLA Modules:
  0.0 75.2 jit_solution(4774678288408803036)
XLA Ops:
  0.6 4.3 %early_part.1.refs_6_ = f32[2048,512]{1,0:T(8,128)S(1)} custom-call(s32[16,128]{1,0:T(8,128)} %bitcast.3, s32[16,128]{1,0:T(8,128)} %bitcast.8, bf16[256,512]{1,0:T(8,128)(2,1)} %nodes_ref.1, f32[2,512]{1,0:T(2,128)} %bias_ref.3, bf16[2048,512]{1,0:T(8,128)(2,1)} %refs_4_.5, bf16[2,3,512,512]{3,2,1,0:T(8,128)(2,1)} %refs_11_.3), custom_call_target="tpu_custom_call" | custom-call | flops 2147483648 | bytes 6291456 | tf_op jit(solution)/shard_map/early_part/pallas_call | solution.py:317
  5.0 5.1 %collective-permute-start.1 = (bf16[256,512]{1,0:T(8,128)(2,1)}, bf16[256,512]{1,0:T(8,128)(2,1)S(1)}, u32[]{:S(2)}, u32[]{:S(2)}) collective-permute-start(bf16[256,512]{1,0:T(8,128)(2,1)} %nodes_ref.1), channel_id=1, source_target_pairs={{1,0},{2,1},{3,2},{0,3},{5,4},{6,5},{7,6},{4,7},{9,8},{10,9},{11,1... | collective-permute-start | bytes 786440 | tf_op jit(solution)/shard_map/ppermute | solution.py:24
  10.1 0.8 %slice.6 = bf16[32,512]{1,0:T(8,128)(2,1)S(1)} slice(bf16[256,512]{1,0:T(8,128)(2,1)} %nodes_ref.1), slice={[0:32], [0:512]} | slice | bytes 65536 | tf_op jit(solution)/shard_map/slice | solution.py:344
  11.0 1.0 %collective-permute-start.2 = (bf16[32,512]{1,0:T(8,128)(2,1)S(1)}, bf16[32,512]{1,0:T(8,128)(2,1)S(1)}, u32[]{:S(2)}, u32[]{:S(2)}) collective-permute-start(bf16[32,512]{1,0:T(8,128)(2,1)S(1)} %slice.6), channel_id=1, source_target_pairs={{2,0},{3,1},{0,2},{1,3},{6,4},{7,5},{4,6},{5,7},{10,8},{11,9},{8,1... | collective-permute-start | bytes 98312 | tf_op jit(solution)/shard_map/ppermute | solution.py:24
  12.0 4.9 %late_part.1.refs_5_ = f32[2048,512]{1,0:T(8,128)S(1)} custom-call(s32[16,128]{1,0:T(8,128)} %bitcast.4, s32[16,128]{1,0:T(8,128)} %bitcast.9, bf16[256,512]{1,0:T(8,128)(2,1)} %nodes_ref.1, f32[2,512]{1,0:T(2,128)} %bias_ref.3, bf16[2048,512]{1,0:T(8,128)(2,1)} %refs_4_.5, bf16[2,3,512,512]{3,2,1,0:T(8,128)(2,1)} %refs_11_.3, ...), custom_call_target="tpu_custom_call", output_to_operand_aliasing={{}: (6, {})} | custom-call | flops 2147483648 | bytes 6291456 | tf_op jit(solution)/shard_map/late_part/pallas_call | solution.py:317
  17.6 3.2 %collective-permute-done.2.refs_9_ = bf16[32,512]{1,0:T(8,128)(2,1)S(1)} collective-permute-done((bf16[32,512]{1,0:T(8,128)(2,1)S(1)}, bf16[32,512]{1,0:T(8,128)(2,1)S(1)}, u32[]{:S(2)}, u32[]{:S(2)}) %collective-permute-start.2) | collective-permute-done | bytes 32800 | tf_op jit(solution)/shard_map/ppermute | solution.py:24
  20.8 8.7 %edge_part.2 = (bf16[2048,512]{1,0:T(8,128)(2,1)S(1)}, bf16[256,512]{1,0:T(8,128)(2,1)S(1)}, f32[256,512]{1,0:T(8,128)S(1)}, bf16[256,512]{1,0:T(8,128)(2,1)S(1)}) custom-call(s32[1]{0:T(128)S(6)} %copy.20.refs_0_, s32[2]{0:T(128)S(1)} %bitcast.13, s32[16,128]{1,0:T(8,128)S(1)} %bitcast.5, s32[16,128]{1,0:T(8,128)S(1)} %bitcast.10, ...), custom_call_target="tpu_custom_call" | custom-call | flops 6442450944 | bytes 8388608 | tf_op jit(solution)/shard_map/edge_part/pallas_call | solution.py:364
  29.6 0.5 collective-permute-start.3
  30.1 3.4 %collective-permute-start.4 = (bf16[256,512]{1,0:T(8,128)(2,1)S(1)}, bf16[256,512]{1,0:T(8,128)(2,1)S(1)}, u32[]{:S(2)}, u32[]{:S(2)}) collective-permute-start(bf16[256,512]{1,0:T(8,128)(2,1)S(1)} %get-tuple-element.16), channel_id=1, source_target_pairs={{1,0},{2,1},{3,2},{0,3},{5,4},{6,5},{7,6},{4,7},{9,8},{10,9},{11,1... | collective-permute-start | bytes 786440 | tf_op jit(solution)/shard_map/ppermute | solution.py:24
  33.5 1.8 %linear_part.1.refs_0_.pre_ref = f32[2048,512]{1,0:T(8,128)S(1)} custom-call(bf16[2048,512]{1,0:T(8,128)(2,1)S(1)} %get-tuple-element.17.edges_ref.refs_4_, bf16[2,3,512,512]{3,2,1,0:T(8,128)(2,1)S(1)} %copy-done, f32[2,512]{1,0:T(2,128)S(1)} %copy-done.6), custom_call_target="tpu_custom_call" | custom-call | flops 1073741824 | bytes 6291456 | tf_op jit(solution)/shard_map/linear_part/pallas_call | solution.py:419
  35.3 2.6 %collective-permute-done.3.from_prev_ref = bf16[256,512]{1,0:T(8,128)(2,1)S(1)} collective-permute-done((bf16[256,512]{1,0:T(8,128)(2,1)S(1)}, bf16[256,512]{1,0:T(8,128)(2,1)S(1)}, u32[]{:S(2)}, u32[]{:S(2)}) %collective-permute-start.3) | collective-permute-done | bytes 262176 | tf_op jit(solution)/shard_map/ppermute | solution.py:24
  37.9 2.3 %collective-permute-done.4.from_next_ref = bf16[256,512]{1,0:T(8,128)(2,1)S(1)} collective-permute-done((bf16[256,512]{1,0:T(8,128)(2,1)S(1)}, bf16[256,512]{1,0:T(8,128)(2,1)S(1)}, u32[]{:S(2)}, u32[]{:S(2)}) %collective-permute-start.4) | collective-permute-done | bytes 262176 | tf_op jit(solution)/shard_map/ppermute | solution.py:24
  40.2 1.9 %node_part.2.nodes_ref.refs_6_ = bf16[256,512]{1,0:T(8,128)(2,1)S(1)} custom-call(bf16[256,512]{1,0:T(8,128)(2,1)} %nodes_ref.1, f32[256,512]{1,0:T(8,128)S(1)} %get-tuple-element.14.kept_ref, bf16[256,512]{1,0:T(8,128)(2,1)S(1)} %collective-permute-done.3.from_prev_ref, bf16[256,512]{1,0:T(8,128)(2,1)S(1)} %collective-permute-done.4.from_next_ref, ...), custom_call_target="tpu_custom_call" | custom-call | flops 402653184 | bytes 1572864 | tf_op jit(solution)/shard_map/node_part/pallas_call | solution.py:434
  42.1 2.7 %collective-permute-start.6 = (bf16[256,512]{1,0:T(8,128)(2,1)S(1)}, bf16[256,512]{1,0:T(8,128)(2,1)S(1)}, u32[]{:S(2)}, u32[]{:S(2)}) collective-permute-start(bf16[256,512]{1,0:T(8,128)(2,1)S(1)} %node_part.2.nodes_ref.refs_6_), channel_id=1, source_target_pairs={{1,0},{2,1},{3,2},{0,3},{5,4},{6,5},{7,6},{4,7},{9,8},{10,9},{11,1... | collective-permute-start | bytes 786440 | tf_op jit(solution)/shard_map/ppermute | solution.py:24
  44.8 0.4 collective-permute-start.5
  45.2 1.2 %collective-permute-start.7 = (bf16[32,512]{1,0:T(8,128)(2,1)S(1)}, bf16[32,512]{1,0:T(8,128)(2,1)S(1)}, u32[]{:S(2)}, u32[]{:S(2)}) collective-permute-start(bf16[32,512]{1,0:T(8,128)(2,1)S(1)} %slice.8), channel_id=1, source_target_pairs={{2,0},{3,1},{0,2},{1,3},{6,4},{7,5},{4,6},{5,7},{10,8},{11,9},{8,1... | collective-permute-start | bytes 98312 | tf_op jit(solution)/shard_map/ppermute | solution.py:24
  46.4 2.5 %own_part.1.refs_5_ = f32[2048,512]{1,0:T(8,128)S(1)} custom-call(s32[16,128]{1,0:T(8,128)S(1)} %bitcast.6, s32[16,128]{1,0:T(8,128)S(1)} %bitcast.11, bf16[256,512]{1,0:T(8,128)(2,1)S(1)} %node_part.2.nodes_ref.refs_6_, bf16[2,3,512,512]{3,2,1,0:T(8,128)(2,1)S(1)} %copy-done, bf16[2,3,512,512]{3,2,1,0:T(8,128)(2,1)S(1)} %copy-done, ...), custom_call_target="tpu_custom_call" | custom-call | flops 1073741824 | bytes 8388608 | tf_op jit(solution)/shard_map/own_part/pallas_call | solution.py:352
  48.9 5.6 %collective-permute-done.7.refs_9_ = bf16[32,512]{1,0:T(8,128)(2,1)S(1)} collective-permute-done((bf16[32,512]{1,0:T(8,128)(2,1)S(1)}, bf16[32,512]{1,0:T(8,128)(2,1)S(1)}, u32[]{:S(2)}, u32[]{:S(2)}) %collective-permute-start.7) | collective-permute-done | bytes 32800 | tf_op jit(solution)/shard_map/ppermute | solution.py:24
  54.5 9.3 %edge_part.3 = (bf16[2048,512]{1,0:T(8,128)(2,1)}, bf16[256,512]{1,0:T(8,128)(2,1)S(1)}, f32[256,512]{1,0:T(8,128)S(1)}, bf16[256,512]{1,0:T(8,128)(2,1)S(1)}) custom-call(s32[1]{0:T(128)S(6)} %copy.20.refs_0_, s32[2]{0:T(128)S(1)} %bitcast.14, s32[16,128]{1,0:T(8,128)S(1)} %bitcast.7, s32[16,128]{1,0:T(8,128)S(1)} %bitcast.12, ...), custom_call_target="tpu_custom_call" | custom-call | flops 6442450944 | bytes 8388608 | tf_op jit(solution)/shard_map/edge_part/pallas_call | solution.py:364
  63.8 0.4 collective-permute-start.8
  64.2 3.5 %collective-permute-start.9 = (bf16[256,512]{1,0:T(8,128)(2,1)S(1)}, bf16[256,512]{1,0:T(8,128)(2,1)S(1)}, u32[]{:S(2)}, u32[]{:S(2)}) collective-permute-start(bf16[256,512]{1,0:T(8,128)(2,1)S(1)} %get-tuple-element.20), channel_id=1, source_target_pairs={{1,0},{2,1},{3,2},{0,3},{5,4},{6,5},{7,6},{4,7},{9,8},{10,9},{11,1... | collective-permute-start | bytes 786440 | tf_op jit(solution)/shard_map/ppermute | solution.py:24
  67.7 4.4 %collective-permute-done.8.from_prev_ref = bf16[256,512]{1,0:T(8,128)(2,1)S(1)} collective-permute-done((bf16[256,512]{1,0:T(8,128)(2,1)S(1)}, bf16[256,512]{1,0:T(8,128)(2,1)S(1)}, u32[]{:S(2)}, u32[]{:S(2)}) %collective-permute-start.8) | collective-permute-done | bytes 262176 | tf_op jit(solution)/shard_map/ppermute | solution.py:24
  72.1 1.4 %collective-permute-done.9.from_next_ref = bf16[256,512]{1,0:T(8,128)(2,1)S(1)} collective-permute-done((bf16[256,512]{1,0:T(8,128)(2,1)S(1)}, bf16[256,512]{1,0:T(8,128)(2,1)S(1)}, u32[]{:S(2)}, u32[]{:S(2)}) %collective-permute-start.9) | collective-permute-done | bytes 262176 | tf_op jit(solution)/shard_map/ppermute | solution.py:24
  73.5 1.6 %node_part.3 = bf16[256,512]{1,0:T(8,128)(2,1)} custom-call(bf16[256,512]{1,0:T(8,128)(2,1)S(1)} %node_part.2.nodes_ref.refs_6_, f32[256,512]{1,0:T(8,128)S(1)} %get-tuple-element.18.kept_ref, bf16[256,512]{1,0:T(8,128)(2,1)S(1)} %collective-permute-done.8.from_prev_ref, bf16[256,512]{1,0:T(8,128)(2,1)S(1)} %collective-permute-done.9.from_next_ref, ...), custom_call_target="tpu_custom_call" | custom-call | flops 402653184 | bytes 1572864 | tf_op jit(solution)/shard_map/node_part/pallas_call | solution.py:434
  (34 shorter events, 0.1 us)
Async XLA Ops:
  5.0 15.8 %collective-permute-start.1 = (bf16[256,512]{1,0:T(8,128)(2,1)}, bf16[256,512]{1,0:T(8,128)(2,1)S(1)}, u32[]{:S(2)}, u32[]{:S(2)}) collective-permute-start(bf16[256,512]{1,0:T(8,128)(2,1)} %nodes_ref.1), channel_id=1, source_target_pairs={{1,0},{2,1},{3,2},{0,3},{5,4},{6,5},{7,6},{4,7},{9,8},{10,9},{11,1... | collective-permute-start | bytes 786440 | tf_op jit(solution)/shard_map/ppermute | solution.py:24
  10.1 10.6 %collective-permute-start = (bf16[256,512]{1,0:T(8,128)(2,1)}, bf16[256,512]{1,0:T(8,128)(2,1)S(1)}, u32[]{:S(2)}, u32[]{:S(2)}) collective-permute-start(bf16[256,512]{1,0:T(8,128)(2,1)} %nodes_ref.1), channel_id=1, source_target_pairs={{3,0},{0,1},{1,2},{2,3},{7,4},{4,5},{5,6},{6,7},{11,8},{8,9},{9,10... | collective-permute-start | bytes 786440 | tf_op jit(solution)/shard_map/ppermute | solution.py:24
  10.9 9.8 %copy-start = (bf16[2,3,512,512]{3,2,1,0:T(8,128)(2,1)S(1)}, bf16[2,3,512,512]{3,2,1,0:T(8,128)(2,1)}, u32[]{:S(2)}) copy-start(bf16[2,3,512,512]{3,2,1,0:T(8,128)(2,1)} %refs_11_.3) | copy-start | bytes 9437188
  10.9 9.8 %copy-start.2 = (bf16[2048,512]{1,0:T(8,128)(2,1)S(1)}, bf16[2048,512]{1,0:T(8,128)(2,1)}, u32[]{:S(2)}) copy-start(bf16[2048,512]{1,0:T(8,128)(2,1)} %refs_4_.5) | copy-start | bytes 6291460
  10.9 9.8 %copy-start.4 = (s32[2048]{0:T(1024)S(1)}, s32[2048]{0:T(1024)}, u32[]{:S(2)}) copy-start(s32[2048]{0:T(1024)} %param.18) | copy-start | bytes 24580
  10.9 9.8 %copy-start.5 = (s32[2048]{0:T(1024)S(1)}, s32[2048]{0:T(1024)}, u32[]{:S(2)}) copy-start(s32[2048]{0:T(1024)} %param.19) | copy-start | bytes 24580
  11.0 9.8 %copy-start.10 = (bf16[2,512,512]{2,1,0:T(8,128)(2,1)S(1)}, bf16[2,512,512]{2,1,0:T(8,128)(2,1)}, u32[]{:S(2)}) copy-start(bf16[2,512,512]{2,1,0:T(8,128)(2,1)} %refs_12_.3) | copy-start | bytes 3145732
  11.0 9.8 %copy-start.11 = (f32[2,512]{1,0:T(2,128)S(1)}, f32[2,512]{1,0:T(2,128)}, u32[]{:S(2)}) copy-start(f32[2,512]{1,0:T(2,128)} %refs_13_.3) | copy-start | bytes 12292
  11.0 9.8 %copy-start.12 = (f32[2,512]{1,0:T(2,128)S(1)}, f32[2,512]{1,0:T(2,128)}, u32[]{:S(2)}) copy-start(f32[2,512]{1,0:T(2,128)} %refs_14_.3) | copy-start | bytes 12292
  11.0 9.8 %copy-start.13 = (s32[2,1]{0,1:T(1,128)S(1)}, s32[2,1]{0,1:T(1,128)}, u32[]{:S(2)}) copy-start(s32[2,1]{0,1:T(1,128)} %param.21) | copy-start | bytes 28
  11.0 9.7 %collective-permute-start.2 = (bf16[32,512]{1,0:T(8,128)(2,1)S(1)}, bf16[32,512]{1,0:T(8,128)(2,1)S(1)}, u32[]{:S(2)}, u32[]{:S(2)}) collective-permute-start(bf16[32,512]{1,0:T(8,128)(2,1)S(1)} %slice.6), channel_id=1, source_target_pairs={{2,0},{3,1},{0,2},{1,3},{6,4},{7,5},{4,6},{5,7},{10,8},{11,9},{8,1... | collective-permute-start | bytes 98312 | tf_op jit(solution)/shard_map/ppermute | solution.py:24
  20.8 12.6 %copy-start.6 = (f32[2,512]{1,0:T(2,128)S(1)}, f32[2,512]{1,0:T(2,128)}, u32[]{:S(2)}) copy-start(f32[2,512]{1,0:T(2,128)} %bias_ref.3) | copy-start | bytes 12292
  29.6 8.3 %collective-permute-start.3 = (bf16[256,512]{1,0:T(8,128)(2,1)S(1)}, bf16[256,512]{1,0:T(8,128)(2,1)S(1)}, u32[]{:S(2)}, u32[]{:S(2)}) collective-permute-start(bf16[256,512]{1,0:T(8,128)(2,1)S(1)} %get-tuple-element.15), channel_id=1, source_target_pairs={{3,0},{0,1},{1,2},{2,3},{7,4},{4,5},{5,6},{6,7},{11,8},{8,9},{9,10... | collective-permute-start | bytes 786440 | tf_op jit(solution)/shard_map/ppermute | solution.py:24
  30.1 10.1 %collective-permute-start.4 = (bf16[256,512]{1,0:T(8,128)(2,1)S(1)}, bf16[256,512]{1,0:T(8,128)(2,1)S(1)}, u32[]{:S(2)}, u32[]{:S(2)}) collective-permute-start(bf16[256,512]{1,0:T(8,128)(2,1)S(1)} %get-tuple-element.16), channel_id=1, source_target_pairs={{1,0},{2,1},{3,2},{0,3},{5,4},{6,5},{7,6},{4,7},{9,8},{10,9},{11,1... | collective-permute-start | bytes 786440 | tf_op jit(solution)/shard_map/ppermute | solution.py:24
  33.5 6.7 %copy-start.1 = (bf16[2,2,512,512]{3,2,1,0:T(8,128)(2,1)S(1)}, bf16[2,2,512,512]{3,2,1,0:T(8,128)(2,1)}, u32[]{:S(2)}) copy-start(bf16[2,2,512,512]{3,2,1,0:T(8,128)(2,1)} %wa_ref.3) | copy-start | bytes 6291460
  33.5 6.7 %copy-start.3 = (bf16[2,512,512]{2,1,0:T(8,128)(2,1)S(1)}, bf16[2,512,512]{2,1,0:T(8,128)(2,1)}, u32[]{:S(2)}) copy-start(bf16[2,512,512]{2,1,0:T(8,128)(2,1)} %wo_ref.3) | copy-start | bytes 3145732
  33.5 6.7 %copy-start.7 = (f32[2,512]{1,0:T(2,128)S(1)}, f32[2,512]{1,0:T(2,128)}, u32[]{:S(2)}) copy-start(f32[2,512]{1,0:T(2,128)} %bias_ref.5) | copy-start | bytes 12292
  33.5 6.7 %copy-start.8 = (f32[2,512]{1,0:T(2,128)S(1)}, f32[2,512]{1,0:T(2,128)}, u32[]{:S(2)}) copy-start(f32[2,512]{1,0:T(2,128)} %gain_ref.3) | copy-start | bytes 12292
  33.5 6.7 %copy-start.9 = (f32[2,512]{1,0:T(2,128)S(1)}, f32[2,512]{1,0:T(2,128)}, u32[]{:S(2)}) copy-start(f32[2,512]{1,0:T(2,128)} %shift_ref.3) | copy-start | bytes 12292
  42.1 12.4 %collective-permute-start.6 = (bf16[256,512]{1,0:T(8,128)(2,1)S(1)}, bf16[256,512]{1,0:T(8,128)(2,1)S(1)}, u32[]{:S(2)}, u32[]{:S(2)}) collective-permute-start(bf16[256,512]{1,0:T(8,128)(2,1)S(1)} %node_part.2.nodes_ref.refs_6_), channel_id=1, source_target_pairs={{1,0},{2,1},{3,2},{0,3},{5,4},{6,5},{7,6},{4,7},{9,8},{10,9},{11,1... | collective-permute-start | bytes 786440 | tf_op jit(solution)/shard_map/ppermute | solution.py:24
  44.8 9.7 %collective-permute-start.5 = (bf16[256,512]{1,0:T(8,128)(2,1)S(1)}, bf16[256,512]{1,0:T(8,128)(2,1)S(1)}, u32[]{:S(2)}, u32[]{:S(2)}) collective-permute-start(bf16[256,512]{1,0:T(8,128)(2,1)S(1)} %node_part.2.nodes_ref.refs_6_), channel_id=1, source_target_pairs={{3,0},{0,1},{1,2},{2,3},{7,4},{4,5},{5,6},{6,7},{11,8},{8,9},{9,10... | collective-permute-start | bytes 786440 | tf_op jit(solution)/shard_map/ppermute | solution.py:24
  45.2 9.3 %collective-permute-start.7 = (bf16[32,512]{1,0:T(8,128)(2,1)S(1)}, bf16[32,512]{1,0:T(8,128)(2,1)S(1)}, u32[]{:S(2)}, u32[]{:S(2)}) collective-permute-start(bf16[32,512]{1,0:T(8,128)(2,1)S(1)} %slice.8), channel_id=1, source_target_pairs={{2,0},{3,1},{0,2},{1,3},{6,4},{7,5},{4,6},{5,7},{10,8},{11,9},{8,1... | collective-permute-start | bytes 98312 | tf_op jit(solution)/shard_map/ppermute | solution.py:24
  63.8 8.3 %collective-permute-start.8 = (bf16[256,512]{1,0:T(8,128)(2,1)S(1)}, bf16[256,512]{1,0:T(8,128)(2,1)S(1)}, u32[]{:S(2)}, u32[]{:S(2)}) collective-permute-start(bf16[256,512]{1,0:T(8,128)(2,1)S(1)} %get-tuple-element.19), channel_id=1, source_target_pairs={{3,0},{0,1},{1,2},{2,3},{7,4},{4,5},{5,6},{6,7},{11,8},{8,9},{9,10... | collective-permute-start | bytes 786440 | tf_op jit(solution)/shard_map/ppermute | solution.py:24
  64.2 9.3 %collective-permute-start.9 = (bf16[256,512]{1,0:T(8,128)(2,1)S(1)}, bf16[256,512]{1,0:T(8,128)(2,1)S(1)}, u32[]{:S(2)}, u32[]{:S(2)}) collective-permute-start(bf16[256,512]{1,0:T(8,128)(2,1)S(1)} %get-tuple-element.20), channel_id=1, source_target_pairs={{1,0},{2,1},{3,2},{0,3},{5,4},{6,5},{7,6},{4,7},{9,8},{10,9},{11,1... | collective-permute-start | bytes 786440 | tf_op jit(solution)/shard_map/ppermute | solution.py:24

commit v7 on v6

--- a/solution.py
+++ b/solution.py
@@ -76,6 +76,10 @@
 def linear_kernel(layer, edges_ref, weight_ref, bias_ref, out_ref):
     ahead = dot(edges_ref[...], weight_ref[0, 0]) + bias_ref[layer : layer + 1, :]
     out_ref[...] = ahead * 0.5
+
+
+def store_kernel(held_ref, out_ref):
+    out_ref[...] = held_ref[...]
 
 
 def own_table(nodes, ws_ref, wr_ref, table_ref):
@@ -312,8 +316,9 @@
         given = (held,) if late else ()
         fixed = [
             pltpu.with_memory_space_constraint(value, pltpu.HBM)
-            for value in (send, recv, nodes, edge_bias, edges, edge_in)
+            for value in (send, recv, edge_bias, edges, edge_in)
         ]
+        around = nodes if late else pltpu.with_memory_space_constraint(nodes, pltpu.HBM)
         return pl.pallas_call(
             functools.partial(first_kernel, late, 0, steps),
             out_shape=jax.ShapeDtypeStruct((slots, width), F32),
@@ -335,7 +340,7 @@
             compiler_params=pltpu.CompilerParams(vmem_limit_bytes=GRANT),
             cost_estimate=cost(2 * square, 6 * slots * width),
             name="late_part" if late else "early_part",
-        )(*fixed, *given)
+        )(*fixed[:2], around, *fixed[2:], *given)
 
     early = start_edges(None)
     sent, early = lax.optimization_barrier((nodes, early))
@@ -431,6 +436,18 @@
                 name="linear_part",
             )(edges, edge_in, edge_bias)
             after = (pre,)
+        else:
+            edges = pl.pallas_call(
+                store_kernel,
+                out_shape=jax.ShapeDtypeStruct((slots, width), BF16),
+                grid=(steps,),
+                in_specs=[by_block],
+                out_specs=by_block,
+                compiler_params=pltpu.CompilerParams(vmem_limit_bytes=GRANT),
+                cost_estimate=cost(0, 4 * slots * width),
+                name="store_part",
+            )(edges)
+            after = (pltpu.with_memory_space_constraint(edges, pltpu.HBM),)
         nodes = pl.pallas_call(
             functools.partial(node_kernel, layer),
             out_shape=jax.ShapeDtypeStruct((rows, width), BF16),

time: 75.5 us -> 73.7 us (0.976)
  waiting for transfers between devices: 19.5 us -> 18.4 us
  starting transfers between devices: 18.2 us -> 19.2 us
  local copies, waits for them, and re-layouts: 0.9 us -> 0.09 us
    pallas_call x0 -> x1, Pallas kernels: none -> 1.83 us  [local(): pl.pallas_call(store_kernel, out_shape=jax.ShapeDtypeStruct((slots, width...]
    pallas_call x2, Pallas kernels: 18.1 us -> 16.7 us  [local(): pl.pallas_call(functools.partial(edge_kernel, rows, layer, size), out_sha...]
    ppermute x10, waiting for transfers between devices: 19.5 us -> 18.4 us  [from_behind(): lax.ppermute(block, axis, [((i - distance) % size, i) for i in range(size)])]
    ppermute x10, starting transfers between devices: 18.2 us -> 19.2 us  [from_behind(): lax.ppermute(block, axis, [((i - distance) % size, i) for i in range(size)])]
    pallas_call x2, Pallas kernels: 3.53 us -> 2.57 us  [local(): pl.pallas_call(functools.partial(node_kernel, layer), out_shape=jax.Shape...]
    slice x2, local copies, waits for them, and re-layouts: 0.83 us -> 0.01 us  [local(): top = sent[:HUB]]
  transfers between devices with their start and end apart: 10 -> 10, of which waited for: 6 -> 7; matrix products, arithmetic and copies ran while one was open for 1% -> 0% of each run, Pallas kernels for 12% -> 15%
where the time goes in v7:
time: 73.7 us; the launch traced here: 73.5 us
  Pallas kernels  34.4 us (47%)
  starting transfers between devices  19.2 us (26%)
  waiting for transfers between devices  18.4 us (25%)
  between operations  1.52 us (2%)
    ppermute x10, starting transfers between devices, from_behind(): lax.ppermute(block, axis, [((i - distance) % size, i) for i in range(size)])  19.2 us
    ppermute x10, waiting for transfers between devices, from_behind(): lax.ppermute(block, axis, [((i - distance) % size, i) for i in range(size)])  18.4 us
    pallas_call x2, Pallas kernels, local(): pl.pallas_call(functools.partial(edge_kernel, rows, layer, size), out_sha...  16.7 us
    pallas_call x2, Pallas kernels, start_edges(): pl.pallas_call(functools.partial(first_kernel, late, 0, steps), out_shape...  8.99 us
    pallas_call x2, Pallas kernels, local(): pl.pallas_call(functools.partial(node_kernel, layer), out_shape=jax.Shape...  2.57 us
    pallas_call x1, Pallas kernels, local(): pl.pallas_call(own_kernel, out_shape=jax.ShapeDtypeStruct((slots, width),...  2.47 us
    pallas_call x1, Pallas kernels, local(): pl.pallas_call(store_kernel, out_shape=jax.ShapeDtypeStruct((slots, width...  1.83 us
    pallas_call x1, Pallas kernels, local(): pl.pallas_call(functools.partial(linear_kernel, layer + 1), out_shape=jax...  1.79 us
  transfers between devices with their start and end apart: 10, of which 7 were waited for; matrix products, arithmetic and copies ran while one was open for 0% of the time, Pallas kernels for 15%

profile of v7, /device:TPU:0, one launch (start us, length us, event | category | flops | bytes accessed | tf_op | source)
XLA Modules:
  0.0 73.5 jit_solution(13773810213705739613)
XLA Ops:
  0.6 4.4 %early_part.1.refs_6_ = f32[2048,512]{1,0:T(8,128)S(1)} custom-call(s32[16,128]{1,0:T(8,128)} %bitcast.3, s32[16,128]{1,0:T(8,128)} %bitcast.8, bf16[256,512]{1,0:T(8,128)(2,1)} %nodes_ref.1, f32[2,512]{1,0:T(2,128)} %bias_ref.3, bf16[2048,512]{1,0:T(8,128)(2,1)} %refs_4_.5, bf16[2,3,512,512]{3,2,1,0:T(8,128)(2,1)} %refs_11_.3), custom_call_target="tpu_custom_call" | custom-call | flops 2147483648 | bytes 6291456 | tf_op jit(solution)/shard_map/early_part/pallas_call | solution.py:322
  5.0 5.1 %collective-permute-start.1 = (bf16[256,512]{1,0:T(8,128)(2,1)S(1)}, bf16[256,512]{1,0:T(8,128)(2,1)S(1)}, u32[]{:S(2)}, u32[]{:S(2)}) collective-permute-start(bf16[256,512]{1,0:T(8,128)(2,1)S(1)} %copy-done.4), channel_id=1, source_target_pairs={{1,0},{2,1},{3,2},{0,3},{5,4},{6,5},{7,6},{4,7},{9,8},{10,9},{11,1... | collective-permute-start | bytes 786440 | tf_op jit(solution)/shard_map/ppermute | solution.py:24
  10.3 1.1 %collective-permute-start.2 = (bf16[32,512]{1,0:T(8,128)(2,1)S(1)}, bf16[32,512]{1,0:T(8,128)(2,1)S(1)}, u32[]{:S(2)}, u32[]{:S(2)}) collective-permute-start(bf16[32,512]{1,0:T(8,128)(2,1)S(1)} %slice.6), channel_id=1, source_target_pairs={{2,0},{3,1},{0,2},{1,3},{6,4},{7,5},{4,6},{5,7},{10,8},{11,9},{8,1... | collective-permute-start | bytes 98312 | tf_op jit(solution)/shard_map/ppermute | solution.py:24
  11.3 4.6 %late_part.1.refs_5_ = f32[2048,512]{1,0:T(8,128)S(1)} custom-call(s32[16,128]{1,0:T(8,128)} %bitcast.4, s32[16,128]{1,0:T(8,128)} %bitcast.9, bf16[256,512]{1,0:T(8,128)(2,1)S(1)} %copy-done.4, f32[2,512]{1,0:T(2,128)} %bias_ref.3, bf16[2048,512]{1,0:T(8,128)(2,1)} %refs_4_.5, bf16[2,3,512,512]{3,2,1,0:T(8,128)(2,1)} %refs_11_.3, ...), custom_call_target="tpu_custom_call", output_to_operand_aliasing={{}: (6, {})} | custom-call | flops 2147483648 | bytes 6291456 | tf_op jit(solution)/shard_map/late_part/pallas_call | solution.py:322
  16.6 3.8 %collective-permute-done.2.refs_9_ = bf16[32,512]{1,0:T(8,128)(2,1)S(1)} collective-permute-done((bf16[32,512]{1,0:T(8,128)(2,1)S(1)}, bf16[32,512]{1,0:T(8,128)(2,1)S(1)}, u32[]{:S(2)}, u32[]{:S(2)}) %collective-permute-start.2) | collective-permute-done | bytes 32800 | tf_op jit(solution)/shard_map/ppermute | solution.py:24
  20.4 8.3 %edge_part.2 = (bf16[2048,512]{1,0:T(8,128)(2,1)S(1)}, bf16[256,512]{1,0:T(8,128)(2,1)S(1)}, f32[256,512]{1,0:T(8,128)S(1)}, bf16[256,512]{1,0:T(8,128)(2,1)S(1)}) custom-call(s32[1]{0:T(128)S(6)} %copy.20.refs_0_, s32[2]{0:T(128)S(1)} %bitcast.13, s32[16,128]{1,0:T(8,128)S(1)} %bitcast.5, s32[16,128]{1,0:T(8,128)S(1)} %bitcast.10, ...), custom_call_target="tpu_custom_call" | custom-call | flops 6442450944 | bytes 8388608 | tf_op jit(solution)/shard_map/edge_part/pallas_call | solution.py:369
  29.5 3.2 %collective-permute-start.4 = (bf16[256,512]{1,0:T(8,128)(2,1)S(1)}, bf16[256,512]{1,0:T(8,128)(2,1)S(1)}, u32[]{:S(2)}, u32[]{:S(2)}) collective-permute-start(bf16[256,512]{1,0:T(8,128)(2,1)S(1)} %get-tuple-element.16), channel_id=1, source_target_pairs={{1,0},{2,1},{3,2},{0,3},{5,4},{6,5},{7,6},{4,7},{9,8},{10,9},{11,1... | collective-permute-start | bytes 786440 | tf_op jit(solution)/shard_map/ppermute | solution.py:24
  32.7 1.8 %linear_part.1.refs_0_.pre_ref = f32[2048,512]{1,0:T(8,128)S(1)} custom-call(bf16[2048,512]{1,0:T(8,128)(2,1)S(1)} %get-tuple-element.17.edges_ref.refs_4_, bf16[2,3,512,512]{3,2,1,0:T(8,128)(2,1)S(1)} %copy-done, f32[2,512]{1,0:T(2,128)S(1)} %copy-done.7), custom_call_target="tpu_custom_call" | custom-call | flops 1073741824 | bytes 6291456 | tf_op jit(solution)/shard_map/linear_part/pallas_call | solution.py:424
  34.5 2.6 %collective-permute-done.3.from_prev_ref = bf16[256,512]{1,0:T(8,128)(2,1)S(1)} collective-permute-done((bf16[256,512]{1,0:T(8,128)(2,1)S(1)}, bf16[256,512]{1,0:T(8,128)(2,1)S(1)}, u32[]{:S(2)}, u32[]{:S(2)}) %collective-permute-start.3) | collective-permute-done | bytes 262176 | tf_op jit(solution)/shard_map/ppermute | solution.py:24
  37.1 3.5 %collective-permute-done.4.from_next_ref = bf16[256,512]{1,0:T(8,128)(2,1)S(1)} collective-permute-done((bf16[256,512]{1,0:T(8,128)(2,1)S(1)}, bf16[256,512]{1,0:T(8,128)(2,1)S(1)}, u32[]{:S(2)}, u32[]{:S(2)}) %collective-permute-start.4) | collective-permute-done | bytes 262176 | tf_op jit(solution)/shard_map/ppermute | solution.py:24
  40.6 0.9 %node_part.2.nodes_ref.refs_6_ = bf16[256,512]{1,0:T(8,128)(2,1)S(1)} custom-call(bf16[256,512]{1,0:T(8,128)(2,1)S(1)} %copy-done.4, f32[256,512]{1,0:T(8,128)S(1)} %get-tuple-element.14.kept_ref, bf16[256,512]{1,0:T(8,128)(2,1)S(1)} %collective-permute-done.3.from_prev_ref, bf16[256,512]{1,0:T(8,128)(2,1)S(1)} %collective-permute-done.4.from_next_ref, ...), custom_call_target="tpu_custom_call" | custom-call | flops 402653184 | bytes 1572864 | tf_op jit(solution)/shard_map/node_part/pallas_call | solution.py:451
  41.5 1.0 %collective-permute-start.6 = (bf16[256,512]{1,0:T(8,128)(2,1)S(1)}, bf16[256,512]{1,0:T(8,128)(2,1)S(1)}, u32[]{:S(2)}, u32[]{:S(2)}) collective-permute-start(bf16[256,512]{1,0:T(8,128)(2,1)S(1)} %node_part.2.nodes_ref.refs_6_), channel_id=1, source_target_pairs={{1,0},{2,1},{3,2},{0,3},{5,4},{6,5},{7,6},{4,7},{9,8},{10,9},{11,1... | collective-permute-start | bytes 786440 | tf_op jit(solution)/shard_map/ppermute | solution.py:24
  42.5 1.7 %collective-permute-start.5 = (bf16[256,512]{1,0:T(8,128)(2,1)S(1)}, bf16[256,512]{1,0:T(8,128)(2,1)S(1)}, u32[]{:S(2)}, u32[]{:S(2)}) collective-permute-start(bf16[256,512]{1,0:T(8,128)(2,1)S(1)} %node_part.2.nodes_ref.refs_6_), channel_id=1, source_target_pairs={{3,0},{0,1},{1,2},{2,3},{7,4},{4,5},{5,6},{6,7},{11,8},{8,9},{9,10... | collective-permute-start | bytes 786440 | tf_op jit(solution)/shard_map/ppermute | solution.py:24
  44.2 2.5 %collective-permute-start.7 = (bf16[32,512]{1,0:T(8,128)(2,1)S(1)}, bf16[32,512]{1,0:T(8,128)(2,1)S(1)}, u32[]{:S(2)}, u32[]{:S(2)}) collective-permute-start(bf16[32,512]{1,0:T(8,128)(2,1)S(1)} %slice.8), channel_id=1, source_target_pairs={{2,0},{3,1},{0,2},{1,3},{6,4},{7,5},{4,6},{5,7},{10,8},{11,9},{8,1... | collective-permute-start | bytes 98312 | tf_op jit(solution)/shard_map/ppermute | solution.py:24
  46.8 2.5 %own_part.1.refs_5_ = f32[2048,512]{1,0:T(8,128)S(1)} custom-call(s32[16,128]{1,0:T(8,128)S(1)} %bitcast.6, s32[16,128]{1,0:T(8,128)S(1)} %bitcast.11, bf16[256,512]{1,0:T(8,128)(2,1)S(1)} %node_part.2.nodes_ref.refs_6_, bf16[2,3,512,512]{3,2,1,0:T(8,128)(2,1)S(1)} %copy-done, bf16[2,3,512,512]{3,2,1,0:T(8,128)(2,1)S(1)} %copy-done, ...), custom_call_target="tpu_custom_call" | custom-call | flops 1073741824 | bytes 8388608 | tf_op jit(solution)/shard_map/own_part/pallas_call | solution.py:357
  49.2 0.9 %collective-permute-done.7.refs_9_ = bf16[32,512]{1,0:T(8,128)(2,1)S(1)} collective-permute-done((bf16[32,512]{1,0:T(8,128)(2,1)S(1)}, bf16[32,512]{1,0:T(8,128)(2,1)S(1)}, u32[]{:S(2)}, u32[]{:S(2)}) %collective-permute-start.7) | collective-permute-done | bytes 32800 | tf_op jit(solution)/shard_map/ppermute | solution.py:24
  50.2 3.2 %collective-permute-done.5.refs_7_ = bf16[256,512]{1,0:T(8,128)(2,1)S(1)} collective-permute-done((bf16[256,512]{1,0:T(8,128)(2,1)S(1)}, bf16[256,512]{1,0:T(8,128)(2,1)S(1)}, u32[]{:S(2)}, u32[]{:S(2)}) %collective-permute-start.5) | collective-permute-done | bytes 262176 | tf_op jit(solution)/shard_map/ppermute | solution.py:24
  53.4 8.4 %edge_part.3 = (bf16[2048,512]{1,0:T(8,128)(2,1)S(1)}, bf16[256,512]{1,0:T(8,128)(2,1)S(1)}, f32[256,512]{1,0:T(8,128)S(1)}, bf16[256,512]{1,0:T(8,128)(2,1)S(1)}) custom-call(s32[1]{0:T(128)S(6)} %copy.20.refs_0_, s32[2]{0:T(128)S(1)} %bitcast.14, s32[16,128]{1,0:T(8,128)S(1)} %bitcast.7, s32[16,128]{1,0:T(8,128)S(1)} %bitcast.12, ...), custom_call_target="tpu_custom_call" | custom-call | flops 6442450944 | bytes 8388608 | tf_op jit(solution)/shard_map/edge_part/pallas_call | solution.py:369
  61.7 1.0 %collective-permute-start.8 = (bf16[256,512]{1,0:T(8,128)(2,1)S(1)}, bf16[256,512]{1,0:T(8,128)(2,1)S(1)}, u32[]{:S(2)}, u32[]{:S(2)}) collective-permute-start(bf16[256,512]{1,0:T(8,128)(2,1)S(1)} %get-tuple-element.19), channel_id=1, source_target_pairs={{3,0},{0,1},{1,2},{2,3},{7,4},{4,5},{5,6},{6,7},{11,8},{8,9},{9,10... | collective-permute-start | bytes 786440 | tf_op jit(solution)/shard_map/ppermute | solution.py:24
  62.7 2.9 %collective-permute-start.9 = (bf16[256,512]{1,0:T(8,128)(2,1)S(1)}, bf16[256,512]{1,0:T(8,128)(2,1)S(1)}, u32[]{:S(2)}, u32[]{:S(2)}) collective-permute-start(bf16[256,512]{1,0:T(8,128)(2,1)S(1)} %get-tuple-element.20), channel_id=1, source_target_pairs={{1,0},{2,1},{3,2},{0,3},{5,4},{6,5},{7,6},{4,7},{9,8},{10,9},{11,1... | collective-permute-start | bytes 786440 | tf_op jit(solution)/shard_map/ppermute | solution.py:24
  65.6 1.8 %store_part.1.refs_0_ = bf16[2048,512]{1,0:T(8,128)(2,1)} custom-call(bf16[2048,512]{1,0:T(8,128)(2,1)S(1)} %get-tuple-element.21.held_ref), custom_call_target="tpu_custom_call" | custom-call | bytes 4194304 | tf_op jit(solution)/shard_map/store_part/pallas_call | solution.py:440
  67.4 2.6 %collective-permute-done.8.from_prev_ref = bf16[256,512]{1,0:T(8,128)(2,1)S(1)} collective-permute-done((bf16[256,512]{1,0:T(8,128)(2,1)S(1)}, bf16[256,512]{1,0:T(8,128)(2,1)S(1)}, u32[]{:S(2)}, u32[]{:S(2)}) %collective-permute-start.8) | collective-permute-done | bytes 262176 | tf_op jit(solution)/shard_map/ppermute | solution.py:24
  70.1 1.8 %collective-permute-done.9.from_next_ref = bf16[256,512]{1,0:T(8,128)(2,1)S(1)} collective-permute-done((bf16[256,512]{1,0:T(8,128)(2,1)S(1)}, bf16[256,512]{1,0:T(8,128)(2,1)S(1)}, u32[]{:S(2)}, u32[]{:S(2)}) %collective-permute-start.9) | collective-permute-done | bytes 262176 | tf_op jit(solution)/shard_map/ppermute | solution.py:24
  71.9 1.6 %node_part.3 = bf16[256,512]{1,0:T(8,128)(2,1)} custom-call(bf16[256,512]{1,0:T(8,128)(2,1)S(1)} %node_part.2.nodes_ref.refs_6_, f32[256,512]{1,0:T(8,128)S(1)} %get-tuple-element.18.kept_ref, bf16[256,512]{1,0:T(8,128)(2,1)S(1)} %collective-permute-done.8.from_prev_ref, bf16[256,512]{1,0:T(8,128)(2,1)S(1)} %collective-permute-done.9.from_next_ref, ...), custom_call_target="tpu_custom_call" | custom-call | flops 402653184 | bytes 1572864 | tf_op jit(solution)/shard_map/node_part/pallas_call | solution.py:451
  (37 shorter events, 0.8 us)
Async XLA Ops:
  5.0 15.3 %collective-permute-start.1 = (bf16[256,512]{1,0:T(8,128)(2,1)S(1)}, bf16[256,512]{1,0:T(8,128)(2,1)S(1)}, u32[]{:S(2)}, u32[]{:S(2)}) collective-permute-start(bf16[256,512]{1,0:T(8,128)(2,1)S(1)} %copy-done.4), channel_id=1, source_target_pairs={{1,0},{2,1},{3,2},{0,3},{5,4},{6,5},{7,6},{4,7},{9,8},{10,9},{11,1... | collective-permute-start | bytes 786440 | tf_op jit(solution)/shard_map/ppermute | solution.py:24
  10.2 10.2 %collective-permute-start = (bf16[256,512]{1,0:T(8,128)(2,1)S(1)}, bf16[256,512]{1,0:T(8,128)(2,1)S(1)}, u32[]{:S(2)}, u32[]{:S(2)}) collective-permute-start(bf16[256,512]{1,0:T(8,128)(2,1)S(1)} %copy-done.4), channel_id=1, source_target_pairs={{3,0},{0,1},{1,2},{2,3},{7,4},{4,5},{5,6},{6,7},{11,8},{8,9},{9,10... | collective-permute-start | bytes 786440 | tf_op jit(solution)/shard_map/ppermute | solution.py:24
  10.2 10.2 %copy-start = (bf16[2,3,512,512]{3,2,1,0:T(8,128)(2,1)S(1)}, bf16[2,3,512,512]{3,2,1,0:T(8,128)(2,1)}, u32[]{:S(2)}) copy-start(bf16[2,3,512,512]{3,2,1,0:T(8,128)(2,1)} %refs_11_.3) | copy-start | bytes 9437188
  10.2 10.2 %copy-start.2 = (bf16[2048,512]{1,0:T(8,128)(2,1)S(1)}, bf16[2048,512]{1,0:T(8,128)(2,1)}, u32[]{:S(2)}) copy-start(bf16[2048,512]{1,0:T(8,128)(2,1)} %refs_4_.5) | copy-start | bytes 6291460
  10.2 10.2 %copy-start.5 = (s32[2048]{0:T(1024)S(1)}, s32[2048]{0:T(1024)}, u32[]{:S(2)}) copy-start(s32[2048]{0:T(1024)} %param.18) | copy-start | bytes 24580
  10.2 10.2 %copy-start.6 = (s32[2048]{0:T(1024)S(1)}, s32[2048]{0:T(1024)}, u32[]{:S(2)}) copy-start(s32[2048]{0:T(1024)} %param.19) | copy-start | bytes 24580
  10.2 10.2 %copy-start.11 = (bf16[2,512,512]{2,1,0:T(8,128)(2,1)S(1)}, bf16[2,512,512]{2,1,0:T(8,128)(2,1)}, u32[]{:S(2)}) copy-start(bf16[2,512,512]{2,1,0:T(8,128)(2,1)} %refs_12_.3) | copy-start | bytes 3145732
  10.2 10.2 %copy-start.12 = (f32[2,512]{1,0:T(2,128)S(1)}, f32[2,512]{1,0:T(2,128)}, u32[]{:S(2)}) copy-start(f32[2,512]{1,0:T(2,128)} %refs_13_.3) | copy-start | bytes 12292
  10.2 10.2 %copy-start.13 = (f32[2,512]{1,0:T(2,128)S(1)}, f32[2,512]{1,0:T(2,128)}, u32[]{:S(2)}) copy-start(f32[2,512]{1,0:T(2,128)} %refs_14_.3) | copy-start | bytes 12292
  10.2 10.2 %copy-start.14 = (s32[2,1]{0,1:T(1,128)S(1)}, s32[2,1]{0,1:T(1,128)}, u32[]{:S(2)}) copy-start(s32[2,1]{0,1:T(1,128)} %param.21) | copy-start | bytes 28
  10.3 10.1 %collective-permute-start.2 = (bf16[32,512]{1,0:T(8,128)(2,1)S(1)}, bf16[32,512]{1,0:T(8,128)(2,1)S(1)}, u32[]{:S(2)}, u32[]{:S(2)}) collective-permute-start(bf16[32,512]{1,0:T(8,128)(2,1)S(1)} %slice.6), channel_id=1, source_target_pairs={{2,0},{3,1},{0,2},{1,3},{6,4},{7,5},{4,6},{5,7},{10,8},{11,9},{8,1... | collective-permute-start | bytes 98312 | tf_op jit(solution)/shard_map/ppermute | solution.py:24
  20.4 12.2 %copy-start.7 = (f32[2,512]{1,0:T(2,128)S(1)}, f32[2,512]{1,0:T(2,128)}, u32[]{:S(2)}) copy-start(f32[2,512]{1,0:T(2,128)} %bias_ref.3) | copy-start | bytes 12292
  28.8 8.3 %collective-permute-start.3 = (bf16[256,512]{1,0:T(8,128)(2,1)S(1)}, bf16[256,512]{1,0:T(8,128)(2,1)S(1)}, u32[]{:S(2)}, u32[]{:S(2)}) collective-permute-start(bf16[256,512]{1,0:T(8,128)(2,1)S(1)} %get-tuple-element.15), channel_id=1, source_target_pairs={{3,0},{0,1},{1,2},{2,3},{7,4},{4,5},{5,6},{6,7},{11,8},{8,9},{9,10... | collective-permute-start | bytes 786440 | tf_op jit(solution)/shard_map/ppermute | solution.py:24
  29.5 11.1 %collective-permute-start.4 = (bf16[256,512]{1,0:T(8,128)(2,1)S(1)}, bf16[256,512]{1,0:T(8,128)(2,1)S(1)}, u32[]{:S(2)}, u32[]{:S(2)}) collective-permute-start(bf16[256,512]{1,0:T(8,128)(2,1)S(1)} %get-tuple-element.16), channel_id=1, source_target_pairs={{1,0},{2,1},{3,2},{0,3},{5,4},{6,5},{7,6},{4,7},{9,8},{10,9},{11,1... | collective-permute-start | bytes 786440 | tf_op jit(solution)/shard_map/ppermute | solution.py:24
  32.7 7.9 %copy-start.1 = (bf16[2,2,512,512]{3,2,1,0:T(8,128)(2,1)S(1)}, bf16[2,2,512,512]{3,2,1,0:T(8,128)(2,1)}, u32[]{:S(2)}) copy-start(bf16[2,2,512,512]{3,2,1,0:T(8,128)(2,1)} %wa_ref.3) | copy-start | bytes 6291460
  32.7 7.9 %copy-start.3 = (bf16[2,512,512]{2,1,0:T(8,128)(2,1)S(1)}, bf16[2,512,512]{2,1,0:T(8,128)(2,1)}, u32[]{:S(2)}) copy-start(bf16[2,512,512]{2,1,0:T(8,128)(2,1)} %wo_ref.3) | copy-start | bytes 3145732
  32.7 7.9 %copy-start.8 = (f32[2,512]{1,0:T(2,128)S(1)}, f32[2,512]{1,0:T(2,128)}, u32[]{:S(2)}) copy-start(f32[2,512]{1,0:T(2,128)} %bias_ref.5) | copy-start | bytes 12292
  32.7 7.9 %copy-start.9 = (f32[2,512]{1,0:T(2,128)S(1)}, f32[2,512]{1,0:T(2,128)}, u32[]{:S(2)}) copy-start(f32[2,512]{1,0:T(2,128)} %gain_ref.3) | copy-start | bytes 12292
  32.7 7.9 %copy-start.10 = (f32[2,512]{1,0:T(2,128)S(1)}, f32[2,512]{1,0:T(2,128)}, u32[]{:S(2)}) copy-start(f32[2,512]{1,0:T(2,128)} %shift_ref.3) | copy-start | bytes 12292
  41.5 8.6 %collective-permute-start.6 = (bf16[256,512]{1,0:T(8,128)(2,1)S(1)}, bf16[256,512]{1,0:T(8,128)(2,1)S(1)}, u32[]{:S(2)}, u32[]{:S(2)}) collective-permute-start(bf16[256,512]{1,0:T(8,128)(2,1)S(1)} %node_part.2.nodes_ref.refs_6_), channel_id=1, source_target_pairs={{1,0},{2,1},{3,2},{0,3},{5,4},{6,5},{7,6},{4,7},{9,8},{10,9},{11,1... | collective-permute-start | bytes 786440 | tf_op jit(solution)/shard_map/ppermute | solution.py:24
  42.5 10.8 %collective-permute-start.5 = (bf16[256,512]{1,0:T(8,128)(2,1)S(1)}, bf16[256,512]{1,0:T(8,128)(2,1)S(1)}, u32[]{:S(2)}, u32[]{:S(2)}) collective-permute-start(bf16[256,512]{1,0:T(8,128)(2,1)S(1)} %node_part.2.nodes_ref.refs_6_), channel_id=1, source_target_pairs={{3,0},{0,1},{1,2},{2,3},{7,4},{4,5},{5,6},{6,7},{11,8},{8,9},{9,10... | collective-permute-start | bytes 786440 | tf_op jit(solution)/shard_map/ppermute | solution.py:24
  44.2 5.9 %collective-permute-start.7 = (bf16[32,512]{1,0:T(8,128)(2,1)S(1)}, bf16[32,512]{1,0:T(8,128)(2,1)S(1)}, u32[]{:S(2)}, u32[]{:S(2)}) collective-permute-start(bf16[32,512]{1,0:T(8,128)(2,1)S(1)} %slice.8), channel_id=1, source_target_pairs={{2,0},{3,1},{0,2},{1,3},{6,4},{7,5},{4,6},{5,7},{10,8},{11,9},{8,1... | collective-permute-start | bytes 98312 | tf_op jit(solution)/shard_map/ppermute | solution.py:24
  61.7 8.3 %collective-permute-start.8 = (bf16[256,512]{1,0:T(8,128)(2,1)S(1)}, bf16[256,512]{1,0:T(8,128)(2,1)S(1)}, u32[]{:S(2)}, u32[]{:S(2)}) collective-permute-start(bf16[256,512]{1,0:T(8,128)(2,1)S(1)} %get-tuple-element.19), channel_id=1, source_target_pairs={{3,0},{0,1},{1,2},{2,3},{7,4},{4,5},{5,6},{6,7},{11,8},{8,9},{9,10... | collective-permute-start | bytes 786440 | tf_op jit(solution)/shard_map/ppermute | solution.py:24
  62.7 9.2 %collective-permute-start.9 = (bf16[256,512]{1,0:T(8,128)(2,1)S(1)}, bf16[256,512]{1,0:T(8,128)(2,1)S(1)}, u32[]{:S(2)}, u32[]{:S(2)}) collective-permute-start(bf16[256,512]{1,0:T(8,128)(2,1)S(1)} %get-tuple-element.20), channel_id=1, source_target_pairs={{1,0},{2,1},{3,2},{0,3},{5,4},{6,5},{7,6},{4,7},{9,8},{10,9},{11,1... | collective-permute-start | bytes 786440 | tf_op jit(solution)/shard_map/ppermute | solution.py:24
  (1 other events, 4.4 us)
